TPU v7x, 128 devices: a whole 4x4x4 slice. The times are simulated.
128 devices in a mesh: seq: 16 (over z, x), head: 8 (over y, core).
Axes of the slice: x: 4, y: 4, z: 4, core: 2. Of those that a mesh axis runs over, the one named last changes fastest.
Arguments:
- x_inputs: bfloat16 [131072, 1024], P('seq', 'head'), may hold values from -6 to 6
- x_in_proj: bfloat16 [131072, 128], P('seq'), may hold values from -0.5 to 0.5
- x_out_proj: bfloat16 [131072, 128], P('seq'), may hold values from -6 to 6
- x_log_decay: float32 [16, 131072], P('head', 'seq'), may hold values from -0.6 to 0
- x_step: float32 [16, 131072], P('head', 'seq'), may hold values from 0 to 0.5
- z_source: int32 [131072], P('seq'), may hold values from 0 to 131071, as said below
- z_in_proj: bfloat16 [131072, 128], P('seq'), may hold values from -0.5 to 0.5
- z_out_proj: bfloat16 [131072, 128], P('seq'), may hold values from -6 to 6
- z_log_decay: float32 [16, 131072], P('head', 'seq'), may hold values from -0.6 to 0
- z_step: float32 [16, 131072], P('head', 'seq'), may hold values from 0 to 0.5
- gate_branch: bfloat16 [131072, 1024], P('seq', 'head'), may hold values from -8 to 8
- norm_gain: float32 [1024], P('head'), may hold values from 0.1 to 1.9
- out_weight: bfloat16 [1024, 512], P('head'), may hold values from -0.1875 to 0.1875
Outputs:
- layer_out: bfloat16 [131072, 512], P(('seq', 'head'))
Inputs may be any that keep to these rules, and one draw needn't show every extreme that they name: z_source is a permutation; every block of 8192 consecutive z-order positions takes exactly 512 tokens from each block of 8192 consecutive x-order tokens.
All inputs are finite; a program needn't handle non-finite values.
Results may differ from a plain program's by a relative error of at most 0.034.
Values may be sent and summed in bfloat16 or wider, within the bound.
No kernel may reach another device: no remote copies, remote signals or barrier semaphores. Data moves between devices by JAX's collectives and lax.ppermute only.
A program may use at most 128 MiB of HBM per device.

v0:
```python
import jax
import jax.numpy as jnp
from jax import lax
from jax.sharding import PartitionSpec as P

BLOCK = 512


def shifted(value, axis, steps):
    count = lax.axis_size(axis)
    initial, last = (max(0, -steps), min(count, count - steps))
    return lax.ppermute(value, axis, [(source, source + steps) for source in range(initial, last)])


def local_blocks(inputs, b_mat, c_mat, log_decay, step):
    count = inputs.shape[0]
    blocks = count // BLOCK
    heads = log_decay.shape[0]
    width = inputs.shape[1]
    head_width = width // heads
    state = b_mat.shape[1]
    cum = jnp.cumsum(log_decay.reshape(heads, blocks, BLOCK), axis=2).transpose(1, 0, 2)
    totals = cum[:, :, -1]
    step_blocks = step.reshape(heads, blocks, BLOCK).transpose(1, 0, 2)
    u_blocks = inputs.reshape(blocks, BLOCK, heads, head_width)
    b_blocks = b_mat.reshape(blocks, BLOCK, state)
    c_blocks = c_mat.reshape(blocks, BLOCK, state)
    rows = lax.broadcasted_iota(jnp.int32, (BLOCK, BLOCK), 0)
    cols = lax.broadcasted_iota(jnp.int32, (BLOCK, BLOCK), 1)
    lower = rows >= cols

    def one_block(carry, pieces):
        u_blk, b_blk, c_blk, cum_blk, d_blk, tot_blk = pieces
        scores = jnp.dot(c_blk, b_blk.T, preferred_element_type=jnp.float32)
        diff = jnp.where(lower[None], cum_blk[:, :, None] - cum_blk[:, None, :], -jnp.inf)
        weights = (scores[None] * jnp.exp(diff) * d_blk[:, None, :]).astype(jnp.bfloat16)
        intra = jnp.einsum("hts,shp->thp", weights, u_blk, preferred_element_type=jnp.float32)
        scale = (jnp.exp(tot_blk[:, None] - cum_blk) * d_blk).T
        contrib = (u_blk * scale[:, :, None]).astype(jnp.bfloat16)
        state_add = jnp.einsum("shp,sn->hpn", contrib, b_blk, preferred_element_type=jnp.float32)
        updated = jnp.exp(tot_blk)[:, None, None] * carry + state_add
        return (updated, (intra, carry))

    start = jnp.zeros((heads, head_width, state), jnp.float32)
    final, (intra_all, local_in) = lax.scan(
        one_block, start, (u_blocks, b_blocks, c_blocks, cum, step_blocks, totals)
    )
    return (intra_all, local_in, final, cum, totals, c_blocks)


def incoming_state(device_decay, final):

    def relay(index, pair):
        received = shifted(pair[1].astype(jnp.bfloat16), "seq", 1).astype(jnp.float32)
        return (received, device_decay[:, None, None] * received + final)

    start, _ = lax.fori_loop(0, lax.axis_size("seq") - 1, relay, (jnp.zeros_like(final), final))
    return start


def ssd_scan(inputs, b_mat, c_mat, log_decay, step):
    intra_all, local_in, final, cum, totals, c_blocks = local_blocks(
        inputs, b_mat, c_mat, log_decay, step
    )
    device_decay = jnp.exp(jnp.sum(totals, axis=0))
    start = incoming_state(device_decay, final)
    before = jnp.cumsum(totals, axis=0) - totals
    carried = local_in + jnp.exp(before)[:, :, None, None] * start[None]
    inter = jnp.einsum(
        "bqn,bhpn->bqhp", c_blocks, carried.astype(jnp.bfloat16), preferred_element_type=jnp.float32
    )
    inter = inter * jnp.exp(cum).transpose(0, 2, 1)[:, :, :, None]
    return (intra_all + inter).astype(jnp.bfloat16).reshape(inputs.shape)


def body(
    x_inputs,
    x_in_proj,
    x_out_proj,
    x_log_decay,
    x_step,
    z_source,
    z_in_proj,
    z_out_proj,
    z_log_decay,
    z_step,
    gate_branch,
    norm_gain,
    out_weight,
):
    y_x = ssd_scan(x_inputs, x_in_proj, x_out_proj, x_log_decay, x_step)
    whole = lax.all_gather(y_x, "seq", axis=0, tiled=True)
    u_z = jnp.take(whole, z_source, axis=0)
    y_z = ssd_scan(u_z, z_in_proj, z_out_proj, z_log_decay, z_step)
    gated = y_z.astype(jnp.float32) * jax.nn.silu(gate_branch.astype(jnp.float32))
    squares = lax.psum(jnp.sum(gated * gated, axis=1).astype(jnp.bfloat16), "head").astype(
        jnp.float32
    )
    mean_square = squares / (gated.shape[1] * lax.axis_size("head"))
    normed = (gated * lax.rsqrt(mean_square[:, None] + 1e-05) * norm_gain).astype(jnp.bfloat16)
    return lax.psum_scatter(
        jnp.dot(normed, out_weight, preferred_element_type=jnp.float32).astype(jnp.bfloat16),
        "head",
        scatter_dimension=0,
        tiled=True,
    )


def solution(mesh):
    placed = (
        P("seq", "head"),
        P("seq", None),
        P("seq", None),
        P("head", "seq"),
        P("head", "seq"),
        P("seq"),
        P("seq", None),
        P("seq", None),
        P("head", "seq"),
        P("head", "seq"),
        P("seq", "head"),
        P("head"),
        P("head", None),
    )
    return jax.shard_map(
        body, mesh=mesh, in_specs=placed, out_specs=P(("seq", "head"), None), check_vma=False
    )
```

profile of v0, /device:TPU:1, one launch (start us, length us, event | category | flops | bytes accessed | tf_op | source)
XLA Modules:
  0.0 932.2 jit_solution(13976984456812221220)
XLA Ops:
  14.1 8.2 reshape.159
  22.3 10.6 %copy.53 = bf16[16,512,2,64]{1,3,2,0:T(8,128)(2,1)} copy(bf16[16,512,2,64]{3,2,1,0:T(2,128)(2,1)} %reshape.159) | data formatting | bytes 4194304
  35.5 93.9 %while.56 = (s32[]{:T(128)}, f32[2,64,128]{2,1,0:T(8,128)S(1)}, f32[16,512,2,64]{1,3,2,0:T(8,128)}, f32[16,2,64,128]{3,2,1,0:T(8,128)S(1)}, f32[16,2]{1,0:T(8,12...) while((s32[]{:T(128)}, f32[2,64,128]{2,1,0:T(8,128)S(1)}, ...), condition=%wide.region_3.4_spmd.clone, body=%wide.region_2.3_spmd.clone.sunk | while | flops 154142720 | bytes 3853496 | solution.py:45
  130.2 101.2 %while.54 = (s32[]{:T(128)}, f32[2,64,128]{2,1,0:T(8,128)}, bf16[2,64,128]{2,1,0:T(8,128)(2,1)S(1)}, f32[2]{0:T(128)S(1)}, f32[2,64,128]{2,1,0:T(8,128)S(1)}, /*index=5*/s32[]{:T(128)}) while((s32[]{:T(128)}, f32[2,64,128]{2,1,0:T(8,128)}, bf16[2,64,128]{2,1,0:T(8,128)(2,1)S(1)}, f32[2]{0:T(128)S(1)}, f32[2,64,128]{2,1,0:T(8,128)S(1)}, ...), condition=%wide.region_7.8_spmd, body=%wide.region_6.7_spmd.sunk | while | flops 65538 | bytes 327797 | solution.py:57
  157.4 5.7 collective-permute-start
  164.8 5.7 collective-permute-start
  172.2 5.7 collective-permute-start
  179.6 5.9 collective-permute-start
  194.4 5.7 collective-permute-start
  201.8 5.7 collective-permute-start
  216.6 5.7 collective-permute-start
  235.0 7.3 copy.73
  242.3 7.8 reshape.160
  254.2 221.1 %all-gather.2.cloned.1.call-done = bf16[131072,128]{1,0:T(8,128)(2,1)} async-done(((bf16[8192,128]{1,0:T(8,128)(2,1)}), bf16[131072,128]{1,0:T(8,128)(2,1)}) %all-gather.2.cloned.1.call-update) | async-done | bytes 33554448 | tf_op jit(solution)/shard_map/all_gather | solution.py:92
  475.3 122.0 %gather_fusion = bf16[8192,128]{1,0:T(8,128)(2,1)} fusion(bf16[131072,128]{1,0:T(8,128)(2,1)} %all-gather.2.cloned.1.call-done, s32[8192]{0:T(1024)S(1)} %fusion.69), kind=kCustom, calls=%fused_computation | custom fusion | bytes 4227072 | tf_op jit(solution)/shard_map/jit(_take)/gather | solution.py:93
  609.1 93.9 %while.57 = (s32[]{:T(128)}, f32[2,64,128]{2,1,0:T(8,128)S(1)}, f32[16,512,2,64]{1,3,2,0:T(8,128)}, f32[16,2,64,128]{3,2,1,0:T(8,128)S(1)}, f32[16,2]{1,0:T(8,12...) while((s32[]{:T(128)}, f32[2,64,128]{2,1,0:T(8,128)S(1)}, ...), condition=%wide.region_11.12_spmd.clone, body=%wide.region_10.11_spmd.clone.sunk | while | flops 154142720 | bytes 3853496 | solution.py:45
  703.7 99.9 %while.55 = (s32[]{:T(128)}, f32[2,64,128]{2,1,0:T(8,128)}, bf16[2,64,128]{2,1,0:T(8,128)(2,1)S(1)}, f32[2]{0:T(128)S(1)}, f32[2,64,128]{2,1,0:T(8,128)S(1)}, /*index=5*/s32[]{:T(128)}) while((s32[]{:T(128)}, f32[2,64,128]{2,1,0:T(8,128)}, bf16[2,64,128]{2,1,0:T(8,128)(2,1)S(1)}, f32[2]{0:T(128)S(1)}, f32[2,64,128]{2,1,0:T(8,128)S(1)}, ...), condition=%wide.region_15.16_spmd, body=%wide.region_14.15_spmd.sunk | while | flops 65538 | bytes 327797 | solution.py:57
  737.0 5.7 collective-permute-start.1
  751.8 5.9 collective-permute-start.1
  774.0 5.7 collective-permute-start.1
  788.8 5.7 collective-permute-start.1
  816.5 36.8 %psum.7 = bf16[8192]{0:T(1024)(128)(2,1)S(1)} all-reduce(bf16[8192]{0:T(1024)(128)(2,1)S(1)} %multiply_reduce_fusion), channel_id=1, replica_groups=mesh['seq'=16,'head'=8] {'head'}, use_global_device_ids=true, to_apply=%region_17.18 | all-reduce | flops 8192 | bytes 32768 | tf_op jit(solution)/shard_map/psum | solution.py:96
  853.3 8.6 convolution_convert_fusion
  861.9 63.4 %reduce-scatter.2.cloned.1.call-done = bf16[1024,512]{1,0:T(8,128)(2,1)} async-done(((bf16[8192,512]{1,0:T(8,128)(2,1)}), bf16[1024,512]{1,0:T(8,128)(2,1)}) %reduce-scatter.2.cloned.1.call-update) | async-done | bytes 1048592 | tf_op jit(solution)/shard_map/reduce_scatter | solution.py:101
  (430 shorter events, 367.1 us)
Async XLA Ops:
  6.5 468.8 %all-gather.2.cloned.1.call-start = ((), (), s32[]{:S(2)}) async-start(), calls=%async_computation.1 | async-start | bytes 35651584 | tf_op jit(solution)/shard_map/all_gather | solution.py:92
  130.2 4.9 collective-permute-start
  151.6 5.2 collective-permute-start
  157.4 6.8 collective-permute-start
  164.8 6.8 collective-permute-start
  172.2 6.8 collective-permute-start
  179.6 6.9 collective-permute-start
  187.1 6.6 collective-permute-start
  194.4 6.8 collective-permute-start
  201.8 6.8 collective-permute-start
  209.2 6.8 collective-permute-start
  216.6 6.8 collective-permute-start
  224.0 6.8 collective-permute-start
  250.1 675.3 %reduce-scatter.2.cloned.1.call-start = ((), (), s32[]{:S(2)}) async-start(), calls=%async_computation.2 | async-start | bytes 9437184 | tf_op jit(solution)/shard_map/reduce_scatter | solution.py:101
  729.7 6.8 collective-permute-start.1
  737.0 6.8 collective-permute-start.1
  744.4 6.8 collective-permute-start.1
  751.8 6.9 collective-permute-start.1
  759.4 6.6 collective-permute-start.1
  766.6 6.8 collective-permute-start.1
  774.0 6.8 collective-permute-start.1
  781.4 6.8 collective-permute-start.1
  788.8 6.8 collective-permute-start.1
  796.2 6.8 collective-permute-start.1
  (12 other events, 924.5 us)
Sparse Core Ops, SparseCore 0:
  250.2 225.0 all-gather.1
  862.1 63.2 reduce-scatter.1
where the time goes:
time: 937 us; the launch traced here: 932 us
  waiting for transfers between devices  315 us (34%)
  local copies, waits for them, and re-layouts  186 us (20%)
  matrix products  173 us (18%)
  starting transfers between devices  152 us (16%)
  other arithmetic  53.4 us (6%)
  blocking collectives  36.8 us (4%)
  between operations  13.6 us (1%)
    all_gather x1, waiting for transfers between devices, body(): whole = lax.all_gather(y_x, 'seq', axis=0, tiled=True)  221 us
    ppermute x30, starting transfers between devices, shifted(): lax.ppermute(value, axis, [(source, source + steps) for source in range(i...  152 us
    gather x2, local copies, waits for them, and re-layouts, body(): u_z = jnp.take(whole, z_source, axis=0)  126 us
    dot_general x32, matrix products, one_block(): jnp.einsum('hts,shp->thp', weights, u_blk, preferred_element_type=jnp.flo...  80.4 us
    reduce_scatter x1, waiting for transfers between devices, body(): lax.psum_scatter(jnp.dot(normed, out_weight, preferred_element_type=jnp.f...  63.4 us
    dot_general x32, matrix products, one_block(): scores = jnp.dot(c_blk, b_blk.T, preferred_element_type=jnp.float32)  40.4 us
    psum x1, blocking collectives, body(): lax.psum(jnp.sum(gated * gated, axis=1).astype(jnp.bfloat16), 'head')  36.8 us
    dot_general x32, matrix products, one_block(): jnp.einsum('shp,sn->hpn', contrib, b_blk, preferred_element_type=jnp.floa...  36.7 us
  transfers between devices with their start and end apart: 32, of which 32 were waited for; matrix products, arithmetic and copies ran while one was open for 0% of the time, Pallas kernels for 0%

commit v1 on v0

v1 whole, which is shorter than its diff:
```python
import functools

import jax
import jax.numpy as jnp
from jax import lax
from jax.experimental import pallas as pl
from jax.experimental.pallas import tpu as pltpu
from jax.sharding import PartitionSpec as P

TOK = 8192
LANES = 128
CHUNK = 128
STEP = 1024
STEPS = TOK // STEP
PIECE = 512
GROUPS = 16
TAIL = 144
MSG = 160
F32 = jnp.float32
BF16 = jnp.bfloat16


def mm(a, b):
    return jnp.dot(a, b, preferred_element_type=F32)


def per_channel(rows, at):
    part = rows[:, at * CHUNK : (at + 1) * CHUNK]
    high = part.astype(BF16).astype(F32)
    low = part - high
    both = jnp.concatenate([high, low], axis=1)
    wide = jnp.concatenate(
        [jnp.broadcast_to(both[0:1], (64, 2 * CHUNK)), jnp.broadcast_to(both[1:2], (64, 2 * CHUNK))], axis=0
    )
    return wide.astype(BF16)


def nt(a, b):
    return lax.dot_general(a, b, (((1,), (1,)), ((), ())), preferred_element_type=F32)


def masks():
    row = lax.broadcasted_iota(jnp.int32, (CHUNK, CHUNK), 0)
    col = lax.broadcasted_iota(jnp.int32, (CHUNK, CHUNK), 1)
    lower = row >= col
    tri = jnp.where(lower, 1.0, 0.0).astype(BF16)
    eye = jnp.where(row == col, 1.0, 0.0).astype(BF16)
    return lower, jnp.concatenate([tri, tri], axis=1), jnp.concatenate([eye, eye], axis=1)


def scan_states(g_ref, d_ref, b_ref, read_u, u2_ref, msg_ref, state, total, first, last):
    _, tri, eye = masks()

    @pl.when(first)
    def _():
        state[...] = jnp.zeros_like(state)
        total[...] = jnp.zeros_like(total)

    carry = state[...]
    sums = total[0:1, :]
    for at in range(STEP // CHUNK):
        rows = slice(at * CHUNK, (at + 1) * CHUNK)
        cum = nt(tri, per_channel(g_ref, at))
        step = nt(eye, per_channel(d_ref, at))
        mid = cum[CHUNK // 2 - 1 : CHUNK // 2]
        tot = cum[CHUNK - 1 : CHUNK]
        u2 = (read_u(at) * (jnp.exp(mid - cum) * step)).astype(BF16)
        u2_ref[rows, :] = u2
        carry = jnp.exp(tot) * carry + jnp.exp(tot - mid) * mm(b_ref[rows, :].T, u2)
        sums = sums + tot
    state[...] = carry
    total[0:1, :] = sums

    @pl.when(last)
    def _():
        high = sums.astype(BF16).astype(F32)
        mid = (sums - high).astype(BF16).astype(F32)
        low = sums - high - mid
        pad = jnp.zeros((TAIL - CHUNK - 3, LANES), F32)
        msg_ref[...] = jnp.concatenate([carry, high, mid, low, pad], axis=0).astype(BF16)


def states_x_kernel(g_ref, d_ref, b_ref, u_ref, u2_ref, msg_ref, state, total):
    step = pl.program_id(0)

    def read_u(at):
        return u_ref[at * CHUNK : (at + 1) * CHUNK, :].astype(F32)

    scan_states(g_ref, d_ref, b_ref, read_u, u2_ref, msg_ref, state, total, step == 0, step == STEPS - 1)


def states_z_kernel(place, g_ref, d_ref, b_ref, got_ref, u2_ref, msg_ref, state, total, wide, ordered):
    step = pl.program_id(0)

    @pl.when(step < STEPS)
    def _():
        wide[...] = got_ref[...].astype(F32)

        def put(i, _):
            for k in range(16):
                row = i * 16 + k
                ordered[pl.ds(place[step * STEP + row], 1), :] = wide[pl.ds(row, 1), :]
            return 0

        lax.fori_loop(0, STEP // 16, put, 0)

    @pl.when(step >= STEPS)
    def _():
        base = (step - STEPS) * STEP

        def read_u(at):
            return ordered[pl.ds(pl.multiple_of(base + at * CHUNK, CHUNK), CHUNK), :]

        scan_states(
            g_ref, d_ref, b_ref, read_u, u2_ref, msg_ref, state, total, step == STEPS, step == 2 * STEPS - 1
        )


def start_state(got_ref, state):
    me = lax.axis_index("seq")
    state[...] = jnp.zeros_like(state)
    for k in range(GROUPS - 1):

        @pl.when(k < me)
        def _():
            tail = got_ref[k, CHUNK:TAIL, :].astype(F32)
            decay = jnp.exp(tail[0:1] + tail[1:2] + tail[2:3])
            state[...] = decay * state[...] + got_ref[k, 0:CHUNK, :].astype(F32)


def scan_outputs(g_ref, b_ref, c_ref, u2_ref, state, write):
    lower, tri, _ = masks()
    carry = state[...]
    for at in range(STEP // CHUNK):
        rows = slice(at * CHUNK, (at + 1) * CHUNK)
        cum = nt(tri, per_channel(g_ref, at))
        mid = cum[CHUNK // 2 - 1 : CHUNK // 2]
        tot = cum[CHUNK - 1 : CHUNK]
        b_t = b_ref[rows, :].T
        c_blk = c_ref[rows, :]
        u2 = u2_ref[rows, :]
        scores = jnp.where(lower, mm(c_blk, b_t), 0.0).astype(BF16)
        held = (carry * jnp.exp(mid)).astype(BF16)
        left = jnp.concatenate([scores, c_blk], axis=1)
        right = jnp.concatenate([u2, held], axis=0)
        write(at, jnp.exp(cum - mid) * mm(left, right))
        carry = jnp.exp(tot) * carry + jnp.exp(tot - mid) * mm(b_t, u2)
    state[...] = carry


def outputs_x_kernel(pick, g_ref, b_ref, c_ref, u2_ref, got_ref, out_ref, state, y_all, rows_ref):
    step = pl.program_id(0)

    @pl.when(step == 0)
    def _():
        start_state(got_ref, state)

    @pl.when(step < STEPS)
    def _():
        def write(at, value):
            y_all[pl.ds(pl.multiple_of(step * STEP + at * CHUNK, CHUNK), CHUNK), :] = value

        scan_outputs(g_ref, b_ref, c_ref, u2_ref, state, write)

    @pl.when(step >= STEPS)
    def _():
        base = (step - STEPS) * STEP

        def take(i, _):
            for k in range(16):
                row = i * 16 + k
                rows_ref[pl.ds(row, 1), :] = y_all[pl.ds(pick[base + row], 1), :]
            return 0

        lax.fori_loop(0, STEP // 16, take, 0)
        out_ref[...] = rows_ref[...].astype(BF16)


def outputs_z_kernel(g_ref, b_ref, c_ref, u2_ref, gate_ref, got_ref, out_ref, state):
    @pl.when(pl.program_id(0) == 0)
    def _():
        start_state(got_ref, state)

    def write(at, value):
        rows = slice(at * CHUNK, (at + 1) * CHUNK)
        gate = gate_ref[rows, :].astype(F32)
        silu = gate / (1.0 + jnp.exp(-gate))
        out_ref[rows, :] = (value.astype(BF16).astype(F32) * silu).astype(BF16)

    scan_outputs(g_ref, b_ref, c_ref, u2_ref, state, write)


def final_kernel(x_ref, w_ref, out_ref):
    parts = [x_ref[k].astype(F32) for k in range(8)]
    squares = sum(part * part for part in parts)
    mean = jnp.sum(squares, axis=1, keepdims=True) * (1.0 / 1024.0)
    scale = lax.rsqrt(mean + 1e-05)
    total = None
    for k in range(8):
        pieces = w_ref[k, LANES:TAIL, 0:LANES].astype(F32)
        gain = pieces[0:1] + pieces[1:2] + pieces[2:3]
        term = mm((parts[k] * scale * gain).astype(BF16), w_ref[k, 0:LANES, :])
        total = term if total is None else total + term
    out_ref[...] = total.astype(BF16)


def spec(shape, index):
    return pl.BlockSpec(shape, index)


def params():
    return pltpu.CompilerParams(dimension_semantics=("arbitrary",), vmem_limit_bytes=48 * 1024 * 1024)


def cost(flops, bytes_accessed):
    return pl.CostEstimate(flops=flops, bytes_accessed=bytes_accessed, transcendentals=0)


ROW = (STEP, LANES)
PAIR = (2, STEP)
STATE_SCRATCH = [pltpu.VMEM((CHUNK, LANES), F32)]


def states_x(g, d, b, u):
    return pl.pallas_call(
        states_x_kernel,
        name="states_x",
        grid=(STEPS,),
        in_specs=[
            spec(PAIR, lambda i: (0, i)),
            spec(PAIR, lambda i: (0, i)),
            spec(ROW, lambda i: (i, 0)),
            spec(ROW, lambda i: (i, 0)),
        ],
        out_specs=[spec(ROW, lambda i: (i, 0)), spec((TAIL, LANES), lambda i: (0, 0))],
        out_shape=[jax.ShapeDtypeStruct((TOK, LANES), BF16), jax.ShapeDtypeStruct((TAIL, LANES), BF16)],
        scratch_shapes=STATE_SCRATCH + [pltpu.VMEM((8, LANES), F32)],
        compiler_params=params(),
        cost_estimate=cost(2 * TOK * 128 * 640, 6 << 20),
    )(g, d, b, u)


def states_z(place, g, d, b, got):
    late = lambda i, _: (jnp.maximum(i - STEPS, 0), 0)
    late_pair = lambda i, _: (0, jnp.maximum(i - STEPS, 0))
    return pl.pallas_call(
        states_z_kernel,
        name="states_z",
        grid_spec=pltpu.PrefetchScalarGridSpec(
            num_scalar_prefetch=1,
            grid=(2 * STEPS,),
            in_specs=[
                spec(PAIR, late_pair),
                spec(PAIR, late_pair),
                spec(ROW, late),
                spec(ROW, lambda i, _: (jnp.minimum(i, STEPS - 1), 0)),
            ],
            out_specs=[spec(ROW, late), spec((TAIL, LANES), lambda i, _: (0, 0))],
            scratch_shapes=STATE_SCRATCH
            + [pltpu.VMEM((8, LANES), F32), pltpu.VMEM(ROW, F32), pltpu.VMEM((TOK, LANES), F32)],
        ),
        out_shape=[jax.ShapeDtypeStruct((TOK, LANES), BF16), jax.ShapeDtypeStruct((TAIL, LANES), BF16)],
        compiler_params=params(),
        cost_estimate=cost(2 * TOK * 128 * 640, 6 << 20),
    )(place, g, d, b, got)


def outputs_x(pick, g, b, c, u2, got):
    early = lambda i, _: (jnp.minimum(i, STEPS - 1), 0)
    return pl.pallas_call(
        outputs_x_kernel,
        name="outputs_x",
        grid_spec=pltpu.PrefetchScalarGridSpec(
            num_scalar_prefetch=1,
            grid=(2 * STEPS,),
            in_specs=[
                spec(PAIR, lambda i, _: (0, jnp.minimum(i, STEPS - 1))),
                spec(ROW, early),
                spec(ROW, early),
                spec(ROW, early),
                spec((GROUPS, MSG, LANES), lambda i, _: (0, 0, 0)),
            ],
            out_specs=spec(ROW, lambda i, _: (jnp.maximum(i - STEPS, 0), 0)),
            scratch_shapes=STATE_SCRATCH + [pltpu.VMEM((TOK, LANES), F32), pltpu.VMEM(ROW, F32)],
        ),
        out_shape=jax.ShapeDtypeStruct((TOK, LANES), BF16),
        compiler_params=params(),
        cost_estimate=cost(2 * TOK * 128 * 896, 8 << 20),
    )(pick, g, b, c, u2, got)


def outputs_z(g, b, c, u2, gate, got):
    return pl.pallas_call(
        outputs_z_kernel,
        name="outputs_z",
        grid=(STEPS,),
        in_specs=[
            spec(PAIR, lambda i: (0, i)),
            spec(ROW, lambda i: (i, 0)),
            spec(ROW, lambda i: (i, 0)),
            spec(ROW, lambda i: (i, 0)),
            spec(ROW, lambda i: (i, 0)),
            spec((GROUPS, TAIL, LANES), lambda i: (0, 0, 0)),
        ],
        out_specs=spec(ROW, lambda i: (i, 0)),
        out_shape=jax.ShapeDtypeStruct((TOK, LANES), BF16),
        scratch_shapes=STATE_SCRATCH,
        compiler_params=params(),
        cost_estimate=cost(2 * TOK * 128 * 896, 10 << 20),
    )(g, b, c, u2, gate, got)


def final(x, w):
    rows = 256
    return pl.pallas_call(
        final_kernel,
        name="final",
        grid=(1024 // rows,),
        in_specs=[
            spec((8, rows, LANES), lambda i: (0, i, 0)),
            spec((8, TAIL, 512), lambda i: (0, 0, 0)),
        ],
        out_specs=spec((rows, 512), lambda i: (i, 0)),
        out_shape=jax.ShapeDtypeStruct((1024, 512), BF16),
        compiler_params=params(),
        cost_estimate=cost(2 * 1024 * 1024 * 512, 5 << 20),
    )(x, w)


def three_pieces(value):
    high = lax.reduce_precision(value, 8, 7)
    mid = lax.reduce_precision(value - high, 8, 7)
    return high, mid, value - high - mid


def body(
    x_inputs,
    x_in_proj,
    x_out_proj,
    x_log_decay,
    x_step,
    z_source,
    z_in_proj,
    z_out_proj,
    z_log_decay,
    z_step,
    gate_branch,
    norm_gain,
    out_weight,
):
    order = jnp.sort(z_source * TOK + lax.iota(jnp.int32, TOK))
    place = order & (TOK - 1)
    source = (order >> 13) & (TOK - 1)
    lists = jnp.concatenate(
        [(source >> 6).reshape(GROUPS, 4, LANES), (source & 63).reshape(GROUPS, 4, LANES)], axis=1
    ).astype(BF16)

    gain = jnp.pad(jnp.stack(three_pieces(norm_gain)), ((0, TAIL - LANES - 3), (0, 512 - LANES))).astype(BF16)
    weights = lax.all_gather(jnp.concatenate([out_weight, gain], axis=0), "head", axis=0, tiled=False)

    u2_x, tail_x = states_x(x_log_decay, x_step, x_in_proj, x_inputs)
    message = jnp.concatenate(
        [
            jnp.broadcast_to(tail_x[None], (GROUPS, TAIL, LANES)),
            lists,
            jnp.zeros((GROUPS, MSG - TAIL - 8, LANES), BF16),
        ],
        axis=1,
    )
    got_x = lax.all_to_all(message, "seq", 0, 0)
    wanted = got_x[:, TAIL : TAIL + 8].astype(jnp.int32)
    pick = (wanted[:, 0:4] * 64 + wanted[:, 4:8]).reshape(TOK)
    sent = outputs_x(pick, x_log_decay, x_in_proj, x_out_proj, u2_x, got_x)
    received = lax.all_to_all(sent.reshape(GROUPS, PIECE, LANES), "seq", 0, 0).reshape(TOK, LANES)
    u2_z, tail_z = states_z(place, z_log_decay, z_step, z_in_proj, received)
    got_z = lax.all_to_all(jnp.broadcast_to(tail_z[None], (GROUPS, TAIL, LANES)), "seq", 0, 0)
    gated = outputs_z(z_log_decay, z_in_proj, z_out_proj, u2_z, gate_branch, got_z)
    whole = lax.all_to_all(gated.reshape(8, 1024, LANES), "head", 0, 0)
    return final(whole, weights)


def solution(mesh):
    placed = (
        P("seq", "head"),
        P("seq", None),
        P("seq", None),
        P("head", "seq"),
        P("head", "seq"),
        P("seq"),
        P("seq", None),
        P("seq", None),
        P("head", "seq"),
        P("head", "seq"),
        P("seq", "head"),
        P("head"),
        P("head", None),
    )
    return jax.shard_map(
        body, mesh=mesh, in_specs=placed, out_specs=P(("seq", "head"), None), check_vma=False
    )
```

time: 937 us -> 218 us (0.23)
  waiting for transfers between devices: 315 us -> 35 us
  local copies, waits for them, and re-layouts: 186 us -> 8.28 us
  matrix products: 173 us -> 0 us
  starting transfers between devices: 152 us -> 12.1 us
  Pallas kernels: 0 us -> 89.1 us
  other arithmetic: 53.4 us -> 8.47 us
  blocking collectives: 36.8 us -> 50.7 us
    all_gather x1, waiting for transfers between devices: 221 us -> 0.01 us  [body(): lax.all_gather(jnp.concatenate([out_weight, gain], axis=0), 'head', axis=...]
    dot_general x99 -> x0, matrix products: 173 us -> none  [the longest x32 80.4 us: one_block(): jnp.einsum('hts,shp->thp', weights, u_blk, preferred_element_type=jnp.flo...]
    ppermute x30 -> x0, starting transfers between devices: 152 us -> none  [shifted(): lax.ppermute(value, axis, [(source, source + steps) for source in range(i...]
    gather x2 -> x0, local copies, waits for them, and re-layouts: 126 us -> none  [body(): u_z = jnp.take(whole, z_source, axis=0)]
    pallas_call x0 -> x5, Pallas kernels: none -> 89.1 us  [the longest x1 27.6 us: outputs_x(): pl.pallas_call(outputs_x_kernel, name='outputs_x', grid_spec=pltpu.Prefet...]
    reduce_scatter x1 -> x0, waiting for transfers between devices: 63.4 us -> none  [body(): lax.psum_scatter(jnp.dot(normed, out_weight, preferred_element_type=jnp.f...]
    all_to_all x0 -> x2, blocking collectives: none -> 50.7 us  [the longest x1 30.7 us: body(): lax.all_to_all(sent.reshape(GROUPS, PIECE, LANES), 'seq', 0, 0)]
    psum x1 -> x0, blocking collectives: 36.8 us -> none  [body(): lax.psum(jnp.sum(gated * gated, axis=1).astype(jnp.bfloat16), 'head')]
  transfers between devices with their start and end apart: 32 -> 3, of which waited for: 32 -> 2; matrix products, arithmetic and copies ran while one was open for 0% -> 0% of each run, Pallas kernels for 0% -> 7%
where the time goes in v1:
time: 218 us; the launch traced here: 217 us
  Pallas kernels  89.1 us (41%)
  blocking collectives  50.7 us (23%)
  waiting for transfers between devices  35 us (16%)
  between operations  13.6 us (6%)
  starting transfers between devices  12.1 us (6%)
  other arithmetic  8.47 us (4%)
  local copies, waits for them, and re-layouts  8.28 us (4%)
    all_to_all x1, blocking collectives, body(): lax.all_to_all(sent.reshape(GROUPS, PIECE, LANES), 'seq', 0, 0)  30.7 us
    pallas_call x1, Pallas kernels, outputs_x(): pl.pallas_call(outputs_x_kernel, name='outputs_x', grid_spec=pltpu.Prefet...  27.6 us
    pallas_call x1, Pallas kernels, states_z(): pl.pallas_call(states_z_kernel, name='states_z', grid_spec=pltpu.Prefetch...  27.3 us
    all_to_all x1, waiting for transfers between devices, body(): whole = lax.all_to_all(gated.reshape(8, 1024, LANES), 'head', 0, 0)  26.3 us
    all_to_all x1, blocking collectives, body(): got_x = lax.all_to_all(message, 'seq', 0, 0)  20 us
    pallas_call x1, Pallas kernels, outputs_z(): pl.pallas_call(outputs_z_kernel, name='outputs_z', grid=(STEPS,), in_spec...  15.4 us
    pallas_call x1, Pallas kernels, states_x(): pl.pallas_call(states_x_kernel, name='states_x', grid=(STEPS,), in_specs=...  14.6 us
    all_to_all x1, waiting for transfers between devices, body(): lax.all_to_all(jnp.broadcast_to(tail_z[None], (GROUPS, TAIL, LANES)), 'se...  8.63 us
  transfers between devices with their start and end apart: 3, of which 2 were waited for; matrix products, arithmetic and copies ran while one was open for 0% of the time, Pallas kernels for 7%

profile of v1, /device:TPU:1, one launch (start us, length us, event | category | flops | bytes accessed | tf_op | source)
XLA Modules:
  0.0 217.2 jit_solution(11929299458991474871)
XLA Ops:
  6.5 0.8 iota_add_fusion
  7.3 6.8 %sort.15 = (s32[8192]{0:T(1024)S(1)}, s32[8192]{0:T(1024)}) sort(s32[8192]{0:T(1024)S(1)} %iota_add_fusion, s32[8192]{0:T(1024)S(1)} %iota.7), dimensions={0}, to_apply=%region_0.0 | sort | flops 106496 | bytes 131072 | tf_op jit(solution)/shard_map/jit(sort)/sort | solution.py:351
  14.1 0.1 pad.14.clone
  14.2 1.6 copy-done.1
  15.8 0.8 copy-done.6
  16.6 0.8 copy-done.8
  17.5 14.6 %states_x.1 = (bf16[8192,128]{1,0:T(8,128)(2,1)S(1)}, bf16[144,128]{1,0:T(8,128)(2,1)S(1)}) custom-call(f32[2,8192]{1,0:T(2,128)S(1)} %copy-done.6, f32[2,8192]{1,0:T(2,128)S(1)} %copy-done.8, bf16[8192,128]{1,0:T(8,128)(2,1)S(1)} %copy-done.1, bf16[8192,128]{1,0:T(8,128)(2,1)} %u_ref.1), custom_call_target="tpu_custom_call" | custom-call | flops 1342177280 | bytes 6291456 | tf_op jit(solution)/shard_map/states_x/pallas_call | solution.py:225
  32.1 0.1 broadcast_in_dim.6
  32.2 0.2 maximum_maximum_fusion
  32.4 20.0 %all_to_all.20.got_ref = bf16[16,160,128]{2,1,0:T(8,128)(2,1)S(1)} all-to-all(bf16[16,160,128]{2,1,0:T(8,128)(2,1)S(1)} %maximum_maximum_fusion), channel_id=1, replica_groups=mesh['seq'=16,'head'=8] {'seq'}, dimensions={0} | all-to-all | bytes 1310720 | tf_op jit(solution)/shard_map/all_to_all | solution.py:370
  52.5 27.6 %outputs_x.1 = bf16[8192,128]{1,0:T(8,128)(2,1)S(1)} custom-call(s32[8192]{0:T(1024)S(1)} %bitcast.16, f32[2,8192]{1,0:T(2,128)S(1)} %copy-done.6, bf16[8192,128]{1,0:T(8,128)(2,1)S(1)} %copy-done.1, bf16[8192,128]{1,0:T(8,128)(2,1)} %c_ref.2, bf16[8192,128]{1,0:T(8,128)(2,1)} %copy-done.4, bf16[16,160,128]{2,1,0:T(8,128)(2,1)S(1)} %all_to_all.20.got_ref), custom_call_target="tpu_custom_call" | custom-call | flops 1879048192 | bytes 8388608 | tf_op jit(solution)/shard_map/outputs_x/pallas_call | solution.py:270
  80.1 30.7 %all_to_all.21 = bf16[16,512,128]{2,1,0:T(8,128)(2,1)} all-to-all(bf16[16,512,128]{2,1,0:T(8,128)(2,1)S(1)} %bitcast.14), channel_id=1, replica_groups=mesh['seq'=16,'head'=8] {'seq'}, dimensions={0} | all-to-all | bytes 4194304 | tf_op jit(solution)/shard_map/all_to_all | solution.py:374
  110.9 27.3 %states_z.1 = (bf16[8192,128]{1,0:T(8,128)(2,1)S(1)}, bf16[144,128]{1,0:T(8,128)(2,1)S(1)}) custom-call(s32[8192]{0:T(1024)S(1)} %get-tuple-element.18.place, f32[2,8192]{1,0:T(2,128)S(1)} %copy-done.7, f32[2,8192]{1,0:T(2,128)S(1)} %copy-done.9, bf16[8192,128]{1,0:T(8,128)(2,1)S(1)} %copy-done.2, bf16[8192,128]{1,0:T(8,128)(2,1)} %bitcast.17), custom_call_target="tpu_custom_call" | custom-call | flops 1342177280 | bytes 6291456 | tf_op jit(solution)/shard_map/states_z/pallas_call | solution.py:246
  138.2 1.3 copy-done.3
  139.5 0.9 broadcast_in_dim.8
  140.4 3.6 %all-to-all-start.2 = ((bf16[16,144,128]{2,1,0:T(8,128)(2,1)}), bf16[16,144,128]{2,1,0:T(8,128)(2,1)S(1)}, u32[]{:S(2)}, u32[]{:S(2)}) async-start(bf16[16,144,128]{2,1,0:T(8,128)(2,1)} %broadcast_in_dim.8), calls=%async_computation.2 | async-start | bytes 1179648 | tf_op jit(solution)/shard_map/all_to_all | solution.py:376
  144.1 0.7 pad_maximum_fusion
  144.8 8.6 %all-to-all-done.2.got_ref = bf16[16,144,128]{2,1,0:T(8,128)(2,1)S(1)} async-done(((bf16[16,144,128]{2,1,0:T(8,128)(2,1)}), bf16[16,144,128]{2,1,0:T(8,128)(2,1)S(1)}, u32[]{:S(2)}, u32[]{:S(2)}) %all-to-all-start.2) | async-done | bytes 589856 | tf_op jit(solution)/shard_map/all_to_all | solution.py:376
  153.4 15.4 %outputs_z.1 = bf16[8192,128]{1,0:T(8,128)(2,1)S(1)} custom-call(f32[2,8192]{1,0:T(2,128)S(1)} %copy-done.7, bf16[8192,128]{1,0:T(8,128)(2,1)S(1)} %copy-done.2, bf16[8192,128]{1,0:T(8,128)(2,1)} %c_ref.3, bf16[8192,128]{1,0:T(8,128)(2,1)} %copy-done.3, bf16[8192,128]{1,0:T(8,128)(2,1)} %gate_ref.1, bf16[16,144,128]{2,1,0:T(8,128)(2,1)S(1)} %all-to-all-done.2.got_ref), custom_call_target="tpu_custom_call" | custom-call | flops 1879048192 | bytes 10485760 | tf_op jit(solution)/shard_map/outputs_z/pallas_call | solution.py:293
  168.8 1.3 copy-done
  170.2 8.4 %all-to-all-start.3 = ((bf16[8,1024,128]{2,1,0:T(8,128)(2,1)}), bf16[8,1024,128]{2,1,0:T(8,128)(2,1)S(1)}, u32[]{:S(2)}, u32[]{:S(2)}) async-start(bf16[8,1024,128]{2,1,0:T(8,128)(2,1)} %bitcast.13), calls=%async_computation.3 | async-start | bytes 4194304 | tf_op jit(solution)/shard_map/all_to_all | solution.py:378
  178.6 26.3 %all-to-all-done.3.x_ref = bf16[8,1024,128]{2,1,0:T(8,128)(2,1)S(1)} async-done(((bf16[8,1024,128]{2,1,0:T(8,128)(2,1)}), bf16[8,1024,128]{2,1,0:T(8,128)(2,1)S(1)}, u32[]{:S(2)}, u32[]{:S(2)}) %all-to-all-start.3) | async-done | bytes 2097184 | tf_op jit(solution)/shard_map/all_to_all | solution.py:378
  204.9 1.3 copy-done.5
  206.2 4.1 %final.1 = bf16[1024,512]{1,0:T(8,128)(2,1)} custom-call(bf16[8,1024,128]{2,1,0:T(8,128)(2,1)S(1)} %all-to-all-done.3.x_ref, bf16[8,144,512]{2,1,0:T(8,128)(2,1)S(1)} %bitcast.15), custom_call_target="tpu_custom_call" | custom-call | flops 1073741824 | bytes 5242880 | tf_op jit(solution)/shard_map/final/pallas_call | solution.py:315
  (28 shorter events, 0.2 us)
Async XLA Ops:
  14.2 1.6 copy-start.1
  15.8 0.8 copy-start.6
  16.6 0.8 copy-start.8
  32.1 20.4 %copy-start.4 = (bf16[8192,128]{1,0:T(8,128)(2,1)}, bf16[8192,128]{1,0:T(8,128)(2,1)S(1)}, u32[]{:S(2)}) copy-start(bf16[8192,128]{1,0:T(8,128)(2,1)S(1)} %get-tuple-element.13.u2_ref) | copy-start | bytes 6291460
  80.1 30.7 %copy-start.2 = (bf16[8192,128]{1,0:T(8,128)(2,1)S(1)}, bf16[8192,128]{1,0:T(8,128)(2,1)}, u32[]{:S(2)}) copy-start(bf16[8192,128]{1,0:T(8,128)(2,1)} %b_ref.7) | copy-start | bytes 6291460
  80.1 30.7 %copy-start.7 = (f32[2,8192]{1,0:T(2,128)S(1)}, f32[2,8192]{1,0:T(2,128)}, u32[]{:S(2)}) copy-start(f32[2,8192]{1,0:T(2,128)} %g_ref.7) | copy-start | bytes 196612
  80.1 30.7 %copy-start.9 = (f32[2,8192]{1,0:T(2,128)S(1)}, f32[2,8192]{1,0:T(2,128)}, u32[]{:S(2)}) copy-start(f32[2,8192]{1,0:T(2,128)} %d_ref.3) | copy-start | bytes 196612
  110.8 33.2 %copy-start.11 = (f32[128]{0:T(128)S(1)}, f32[128]{0:T(128)}, u32[]{:S(2)}) copy-start(f32[128]{0:T(128)} %param.24) | copy-start | bytes 1540
  110.8 33.2 %copy-start.10 = (bf16[128,512]{1,0:T(8,128)(2,1)S(1)}, bf16[128,512]{1,0:T(8,128)(2,1)}, u32[]{:S(2)}) copy-start(bf16[128,512]{1,0:T(8,128)(2,1)} %param.25) | copy-start | bytes 393220
  138.2 1.3 copy-start.3
  140.4 13.0 %all-to-all-start.2 = ((bf16[16,144,128]{2,1,0:T(8,128)(2,1)}), bf16[16,144,128]{2,1,0:T(8,128)(2,1)S(1)}, u32[]{:S(2)}, u32[]{:S(2)}) async-start(bf16[16,144,128]{2,1,0:T(8,128)(2,1)} %broadcast_in_dim.8), calls=%async_computation.2 | async-start | bytes 1179648 | tf_op jit(solution)/shard_map/all_to_all | solution.py:376
  144.0 34.6 %all-gather.3.cloned.1.call-start = ((), (), s32[]{:S(2)}) async-start(), calls=%async_computation.4 | async-start | bytes 1327104 | tf_op jit(solution)/shard_map/all_gather | solution.py:359
  168.8 1.3 copy-start
  170.2 34.8 %all-to-all-start.3 = ((bf16[8,1024,128]{2,1,0:T(8,128)(2,1)}), bf16[8,1024,128]{2,1,0:T(8,128)(2,1)S(1)}, u32[]{:S(2)}, u32[]{:S(2)}) async-start(bf16[8,1024,128]{2,1,0:T(8,128)(2,1)} %bitcast.13), calls=%async_computation.3 | async-start | bytes 4194304 | tf_op jit(solution)/shard_map/all_to_all | solution.py:378
  204.9 1.3 copy-start.5
Sparse Core Ops, SparseCore 0:
  146.5 28.0 all-gather.2

commit v2 on v0

v2 whole, which is shorter than its diff:
```python
import functools

import jax
import jax.numpy as jnp
from jax import lax
from jax.experimental import pallas as pl
from jax.experimental.pallas import tpu as pltpu
from jax.sharding import PartitionSpec as P

TOK = 8192
LANES = 128
CHUNK = 128
STEP = 1024
PER = STEP // CHUNK
STEPS = TOK // STEP
PIECE = 512
GROUPS = 16
TAIL = 136
MSG = 144
UNROLL = 32
F32 = jnp.float32
BF16 = jnp.bfloat16


def mm(a, b):
    return jnp.dot(a, b, preferred_element_type=F32)


def nt(a, b):
    return lax.dot_general(a, b, (((1,), (1,)), ((), ())), preferred_element_type=F32)


def tn(a, b):
    return lax.dot_general(a, b, (((0,), (0,)), ((), ())), preferred_element_type=F32)


def iotas():
    shape = (CHUNK, CHUNK)
    return lax.broadcasted_iota(jnp.int32, shape, 0), lax.broadcasted_iota(jnp.int32, shape, 1)


def ones(condition):
    return jnp.where(condition, 1.0, 0.0).astype(BF16)


def pieces(value, axis):
    high = value.astype(BF16)
    rest = value - high.astype(F32)
    mid = rest.astype(BF16)
    low = (rest - mid.astype(F32)).astype(BF16)
    return jnp.concatenate([high, mid, low], axis=axis)


def thrice(mask, axis):
    return jnp.concatenate([mask, mask, mask], axis=axis)


def wide(column):
    return jnp.broadcast_to(column, (CHUNK, LANES))


def by_head(first, second):
    return jnp.where(lax.broadcasted_iota(jnp.int32, (1, LANES), 1) < 64, first, second)


def row_pair(slab, at):
    return by_head(slab[2 * at : 2 * at + 1], slab[2 * at + 1 : 2 * at + 2])


def spread_mask():
    row = lax.broadcasted_iota(jnp.int32, (48, STEP), 0) & 15
    col = lax.broadcasted_iota(jnp.int32, (48, STEP), 1)
    return ones(row == 2 * (col >> 7) + ((col >> 6) & 1))


def spread(slab, mask):
    return tn(pieces(slab, 0), mask)


def slab_at(step):
    return pl.ds(pl.multiple_of(16 * step, 16), 16)


def end_weights(g, d):
    row, col = iotas()
    inner = mm(pieces(g, 1), thrice(ones(row > col), 0))
    total = wide(inner[:, 0:1] + g[:, 0:1])
    later = mm(thrice(ones((col > row) & ((col & 1) == (row & 1))), 1), pieces(total, 0))
    whole = later[0:2] + total[0:2]
    return jnp.exp(inner + later) * d, by_head(whole[0:1], whole[1:2])


def scan_factors(g, d):
    row, col = iotas()
    cum = mm(pieces(g, 1), thrice(ones(row <= col), 0))
    mid = wide(cum[:, CHUNK // 2 - 1 : CHUNK // 2])
    total = wide(cum[:, CHUNK - 1 : CHUNK])
    before = mm(thrice(ones((col < row) & ((col & 1) == (row & 1))), 1), pieces(total, 0))
    return (
        jnp.exp(mid - cum) * d,
        jnp.exp(cum - mid),
        jnp.exp(mid),
        jnp.exp(total),
        jnp.exp(total - mid),
        jnp.exp(mid + before),
    )


def write_tail(msg_ref, state, total):
    high = total.astype(BF16).astype(F32)
    mid = (total - high).astype(BF16).astype(F32)
    low = total - high - mid
    pad = jnp.zeros((TAIL - CHUNK - 3, LANES), F32)
    msg_ref[...] = jnp.concatenate([state, high, mid, low, pad], axis=0).astype(BF16)


def chunk_rows(at):
    return slice(at * CHUNK, (at + 1) * CHUNK)


def states_x_kernel(g_ref, d_ref, b_ref, u_ref, msg_ref, weights, mask, state, total):
    step = pl.program_id(0)

    @pl.when(step == 0)
    def _():
        weights[...], total[0:1, :] = end_weights(g_ref[...], d_ref[...])
        mask[...] = spread_mask()
        state[...] = jnp.zeros_like(state)

    scale = spread(weights[slab_at(step), :], mask[...])
    parts = [
        (u_ref[chunk_rows(at), :].astype(F32) * scale[:, chunk_rows(at)]).astype(BF16) for at in range(PER)
    ]
    state[...] += tn(b_ref[...], jnp.concatenate(parts, axis=0))

    @pl.when(step == STEPS - 1)
    def _():
        write_tail(msg_ref, state[...], total[0:1, :])


def local_scan(u2s, scores, b_ts, cs, slabs, r_slab, mask, state, y_ref):
    into, end, add = slabs
    carry = state[...]
    sums = [mm(b_ts[at], u2s[at]) for at in range(PER)]
    helds = []
    for at in range(PER):
        helds.append((carry * row_pair(into, at)).astype(BF16))
        carry = row_pair(end, at) * carry + row_pair(add, at) * sums[at]
    state[...] = carry
    back = spread(r_slab, mask)
    for at in range(PER):
        left = jnp.concatenate([scores[at], cs[at]], axis=1)
        right = jnp.concatenate([u2s[at], helds[at]], axis=0)
        y_ref[chunk_rows(at), :] = back[:, chunk_rows(at)] * mm(left, right)


def local_x_kernel(g_ref, d_ref, b_ref, c_ref, u_ref, y_ref, r_ref, e_ref, a_all, ends, mask, state):
    step = pl.program_id(0)

    @pl.when(step == 0)
    def _():
        a_all[...], r_ref[...], ends[0], ends[1], ends[2], e_ref[...] = scan_factors(g_ref[...], d_ref[...])
        mask[...] = spread_mask()
        state[...] = jnp.zeros_like(state)

    row, col = iotas()
    lower = row >= col
    here = slab_at(step)
    scale = spread(a_all[here, :], mask[...])
    u2s = [(u_ref[chunk_rows(at), :].astype(F32) * scale[:, chunk_rows(at)]).astype(BF16) for at in range(PER)]
    b_ts = [b_ref[chunk_rows(at), :].T for at in range(PER)]
    cs = [c_ref[chunk_rows(at), :] for at in range(PER)]
    scores = [jnp.where(lower, mm(cs[at], b_ts[at]), 0.0).astype(BF16) for at in range(PER)]
    slabs = (ends[0, here, :], ends[1, here, :], ends[2, here, :])
    local_scan(u2s, scores, b_ts, cs, slabs, r_ref[here, :], mask[...], state, y_ref)


def start_state(got_ref, state):
    me = lax.axis_index("seq")
    state[...] = jnp.zeros_like(state)
    for k in range(GROUPS - 1):

        @pl.when(k < me)
        def _():
            tail = got_ref[k, CHUNK:TAIL, :].astype(F32)
            decay = jnp.exp(tail[0:1] + tail[1:2] + tail[2:3])
            state[...] = decay * state[...] + got_ref[k, 0:CHUNK, :].astype(F32)


def add_start(y_ref, c_ref, r_slab, e_slab, mask, state, write):
    back = spread(r_slab, mask)
    start = state[...]
    for at in range(PER):
        held = (start * row_pair(e_slab, at)).astype(BF16)
        write(at, y_ref[chunk_rows(at), :] + back[:, chunk_rows(at)] * mm(c_ref[chunk_rows(at), :], held))


def invert_lists(got_ref, slots):
    high = lax.broadcasted_iota(jnp.int32, (64, LANES), 0).astype(F32)
    low = lax.broadcasted_iota(jnp.int32, (LANES, LANES), 0).astype(F32)
    lane = lax.broadcasted_iota(jnp.int32, (64, LANES), 1).astype(F32)
    total = jnp.zeros((LANES, LANES), F32)
    for k in range(GROUPS):
        lists = got_ref[k, TAIL:MSG, :].astype(F32)
        lefts, rights = [], []
        for q in range(4):
            hit = high == lists[q : q + 1]
            lefts.append(
                jnp.concatenate([jnp.where(hit, float(4 * k + q), 0.0), jnp.where(hit, lane, 0.0)], axis=0).astype(BF16)
            )
            rights.append(ones(low == lists[4 + q : 5 + q]))
        total = total + nt(jnp.concatenate(lefts, axis=1), jnp.concatenate(rights, axis=1))
    slots[...] = (total[0:64] * 128.0 + total[64:128]).astype(jnp.int32)


def send_x_kernel(
    y_ref, c_ref, r_ref, e_ref, got_ref, out_ref, state, mask, rows, ordered, slots, table, sem
):
    step = pl.program_id(0)

    @pl.when(step == 0)
    def _():
        invert_lists(got_ref, slots)
        copy = pltpu.make_async_copy(slots, table, sem)
        copy.start()
        start_state(got_ref, state)
        mask[...] = spread_mask()
        copy.wait()

    @pl.when(step < STEPS)
    def _():
        here = slab_at(step)

        def write(at, value):
            rows[chunk_rows(at), :] = value

        add_start(y_ref, c_ref, r_ref[here, :], e_ref[here, :], mask[...], state, write)

        def put(i, _):
            line = step * PER + i // 4
            base = (i % 4) * UNROLL
            for k in range(UNROLL):
                ordered[pl.ds(table[line, base + k], 1), :] = rows[pl.ds(i * UNROLL + k, 1), :]
            return 0

        lax.fori_loop(0, STEP // UNROLL, put, 0)

    @pl.when(step >= STEPS)
    def _():
        base = pl.multiple_of((step - STEPS) * STEP, STEP)
        out_ref[...] = ordered[pl.ds(base, STEP), :].astype(BF16)


def before_z_kernel(
    g_ref, d_ref, b_ref, c_ref, s_ref, b_t_ref, w_ref, t_ref, a_ref, r_ref, e_ref, ends_ref
):
    @pl.when(pl.program_id(0) == 0)
    def _():
        w_ref[...], total = end_weights(g_ref[...], d_ref[...])
        t_ref[...] = jnp.broadcast_to(total, (8, LANES))
        a_ref[...], r_ref[...], ends_ref[0], ends_ref[1], ends_ref[2], e_ref[...] = scan_factors(
            g_ref[...], d_ref[...]
        )

    row, col = iotas()
    lower = row >= col
    for at in range(PER):
        b_t = b_ref[chunk_rows(at), :].T
        b_t_ref[:, chunk_rows(at)] = b_t
        s_ref[chunk_rows(at), :] = jnp.where(lower, mm(c_ref[chunk_rows(at), :], b_t), 0.0).astype(BF16)


def states_z_kernel(place, w_ref, t_ref, a_ref, b_t_ref, got_ref, u2_ref, msg_ref, mask, state, rows, ordered):
    step = pl.program_id(0)

    @pl.when(step == 0)
    def _():
        mask[...] = spread_mask()
        state[...] = jnp.zeros_like(state)

    @pl.when(step < STEPS)
    def _():
        rows[...] = got_ref[...].astype(F32)

        def put(i, _):
            base = step * STEP + i * UNROLL
            for k in range(UNROLL):
                ordered[pl.ds(place[base + k], 1), :] = rows[pl.ds(i * UNROLL + k, 1), :]
            return 0

        lax.fori_loop(0, STEP // UNROLL, put, 0)

    @pl.when(step >= STEPS)
    def _():
        base = (step - STEPS) * STEP
        here = slab_at(step - STEPS)
        weight = spread(w_ref[here, :], mask[...])
        scale = spread(a_ref[here, :], mask[...])
        parts = []
        for at in range(PER):
            u = ordered[pl.ds(pl.multiple_of(base + at * CHUNK, CHUNK), CHUNK), :]
            u2_ref[chunk_rows(at), :] = (u * scale[:, chunk_rows(at)]).astype(BF16)
            parts.append((u * weight[:, chunk_rows(at)]).astype(BF16))
        state[...] += mm(b_t_ref[...], jnp.concatenate(parts, axis=0))

    @pl.when(step == 2 * STEPS - 1)
    def _():
        write_tail(msg_ref, state[...], t_ref[0:1, :])


def local_z_kernel(u2_ref, s_ref, b_t_ref, c_ref, r_ref, ends_ref, y_ref, mask, state):
    step = pl.program_id(0)

    @pl.when(step == 0)
    def _():
        mask[...] = spread_mask()
        state[...] = jnp.zeros_like(state)

    here = slab_at(step)
    u2s = [u2_ref[chunk_rows(at), :] for at in range(PER)]
    scores = [s_ref[chunk_rows(at), :] for at in range(PER)]
    b_ts = [b_t_ref[:, chunk_rows(at)] for at in range(PER)]
    cs = [c_ref[chunk_rows(at), :] for at in range(PER)]
    slabs = (ends_ref[0, here, :], ends_ref[1, here, :], ends_ref[2, here, :])
    local_scan(u2s, scores, b_ts, cs, slabs, r_ref[here, :], mask[...], state, y_ref)


def gate_z_kernel(y_ref, c_ref, gate_ref, r_ref, e_ref, got_ref, out_ref, state, mask):
    step = pl.program_id(0)

    @pl.when(step == 0)
    def _():
        start_state(got_ref, state)
        mask[...] = spread_mask()

    def write(at, value):
        gate = gate_ref[chunk_rows(at), :].astype(F32)
        silu = gate / (1.0 + jnp.exp(-gate))
        out_ref[chunk_rows(at), :] = (value.astype(BF16).astype(F32) * silu).astype(BF16)

    here = slab_at(step)
    add_start(y_ref, c_ref, r_ref[here, :], e_ref[here, :], mask[...], state, write)


def final_kernel(x_ref, w_ref, out_ref):
    parts = [x_ref[k].astype(F32) for k in range(8)]
    squares = sum(part * part for part in parts)
    mean = jnp.sum(squares, axis=1, keepdims=True) * (1.0 / 1024.0)
    scale = lax.rsqrt(mean + 1e-05)
    total = None
    for k in range(8):
        parts3 = w_ref[k, LANES:TAIL, 0:LANES].astype(F32)
        gain = parts3[0:1] + parts3[1:2] + parts3[2:3]
        term = mm((parts[k] * scale * gain).astype(BF16), w_ref[k, 0:LANES, :])
        total = term if total is None else total + term
    out_ref[...] = total.astype(BF16)


ROW = (STEP, LANES)
FLAT = (CHUNK, LANES)
GOT_X = (GROUPS, MSG, LANES)
GOT_Z = (GROUPS, TAIL, LANES)
ENDS = (3, CHUNK, LANES)
MASK = pltpu.VMEM((48, STEP), BF16)
STATE = pltpu.VMEM(FLAT, F32)


def block(shape, index):
    return pl.BlockSpec(shape, index)


def fixed(shape):
    return pl.BlockSpec(shape, lambda *_: (0,) * len(shape))


def each(i, *_):
    return (i, 0)


def early(i, *_):
    return (jnp.minimum(i, STEPS - 1), 0)


def late(i, *_):
    return (jnp.maximum(i - STEPS, 0), 0)


def struct(shape, dtype):
    return jax.ShapeDtypeStruct(shape, dtype)


def call(kernel, name, steps, ins, outs, shapes, scratch, mib, prefetch=0, limit=56):
    return pl.pallas_call(
        kernel,
        name=name,
        grid_spec=pltpu.PrefetchScalarGridSpec(
            num_scalar_prefetch=prefetch, grid=(steps,), in_specs=ins, out_specs=outs, scratch_shapes=scratch
        ),
        out_shape=shapes,
        compiler_params=pltpu.CompilerParams(
            dimension_semantics=("arbitrary",), vmem_limit_bytes=limit * 1024 * 1024
        ),
        cost_estimate=pl.CostEstimate(flops=mib << 28, bytes_accessed=mib << 20, transcendentals=0),
    )


def states_x(g, d, b, u):
    return call(
        states_x_kernel, "states_x", STEPS,
        [fixed(FLAT), fixed(FLAT), block(ROW, each), block(ROW, each)],
        fixed((TAIL, LANES)), struct((TAIL, LANES), BF16),
        [STATE, MASK, STATE, pltpu.VMEM((8, LANES), F32)], 4,
    )(g, d, b, u)


def local_x(g, d, b, c, u):
    return call(
        local_x_kernel, "local_x", STEPS,
        [fixed(FLAT), fixed(FLAT), block(ROW, each), block(ROW, each), block(ROW, each)],
        [block(ROW, each), fixed(FLAT), fixed(FLAT)],
        [struct((TOK, LANES), F32), struct(FLAT, F32), struct(FLAT, F32)],
        [STATE, pltpu.VMEM(ENDS, F32), MASK, STATE], 10,
    )(g, d, b, c, u)


def send_x(y, c, r, e, got):
    return call(
        send_x_kernel, "send_x", 2 * STEPS,
        [block(ROW, early), block(ROW, early), fixed(FLAT), fixed(FLAT), fixed(GOT_X)],
        block(ROW, late), struct((TOK, LANES), BF16),
        [
            STATE, MASK, pltpu.VMEM(ROW, F32), pltpu.VMEM((TOK, LANES), F32),
            pltpu.VMEM((64, LANES), jnp.int32), pltpu.SMEM((64, LANES), jnp.int32), pltpu.SemaphoreType.DMA,
        ], 10,
    )(y, c, r, e, got)


def before_z(g, d, b, c):
    return call(
        before_z_kernel, "before_z", STEPS,
        [fixed(FLAT), fixed(FLAT), block(ROW, each), block(ROW, each)],
        [
            block(ROW, each), block((CHUNK, STEP), lambda i: (0, i)), fixed(FLAT), fixed((8, LANES)),
            fixed(FLAT), fixed(FLAT), fixed(FLAT), fixed(ENDS),
        ],
        [
            struct((TOK, LANES), BF16), struct((CHUNK, TOK), BF16), struct(FLAT, F32), struct((8, LANES), F32),
            struct(FLAT, F32), struct(FLAT, F32), struct(FLAT, F32), struct(ENDS, F32),
        ],
        [], 8,
    )(g, d, b, c)


def states_z(place, w, t, a, b_t, got):
    return call(
        states_z_kernel, "states_z", 2 * STEPS,
        [
            fixed(FLAT), fixed((8, LANES)), fixed(FLAT),
            block((CHUNK, STEP), lambda i, _: (0, jnp.maximum(i - STEPS, 0))), block(ROW, early),
        ],
        [block(ROW, late), fixed((TAIL, LANES))],
        [struct((TOK, LANES), BF16), struct((TAIL, LANES), BF16)],
        [MASK, STATE, pltpu.VMEM(ROW, F32), pltpu.VMEM((TOK, LANES), F32)], 8, prefetch=1,
    )(place, w, t, a, b_t, got)


def local_z(u2, s, b_t, c, r, ends):
    return call(
        local_z_kernel, "local_z", STEPS,
        [
            block(ROW, each), block(ROW, each), block((CHUNK, STEP), lambda i: (0, i)), block(ROW, each),
            fixed(FLAT), fixed(ENDS),
        ],
        block(ROW, each), struct((TOK, LANES), F32), [MASK, STATE], 10,
    )(u2, s, b_t, c, r, ends)


def gate_z(y, c, gate, r, e, got):
    return call(
        gate_z_kernel, "gate_z", STEPS,
        [block(ROW, each), block(ROW, each), block(ROW, each), fixed(FLAT), fixed(FLAT), fixed(GOT_Z)],
        block(ROW, each), struct((TOK, LANES), BF16), [STATE, MASK], 10,
    )(y, c, gate, r, e, got)


def final(x, w):
    rows = 256
    return call(
        final_kernel, "final", 1024 // rows,
        [block((8, rows, LANES), lambda i: (0, i, 0)), fixed((8, TAIL, 512))],
        block((rows, 512), each), struct((1024, 512), BF16), [], 5,
    )(x, w)


def three_pieces(value):
    high = lax.reduce_precision(value, 8, 7)
    mid = lax.reduce_precision(value - high, 8, 7)
    return high, mid, value - high - mid


def flat(value):
    return value.reshape(2, TOK // CHUNK, CHUNK).transpose(1, 0, 2).reshape(CHUNK, LANES)


def body(
    x_inputs,
    x_in_proj,
    x_out_proj,
    x_log_decay,
    x_step,
    z_source,
    z_in_proj,
    z_out_proj,
    z_log_decay,
    z_step,
    gate_branch,
    norm_gain,
    out_weight,
):
    order = jnp.sort(z_source * TOK + lax.iota(jnp.int32, TOK))
    place = order & (TOK - 1)
    source = (order >> 13) & (TOK - 1)
    lists = jnp.concatenate(
        [(source >> 7).reshape(GROUPS, 4, LANES), (source & 127).reshape(GROUPS, 4, LANES)], axis=1
    ).astype(BF16)

    gain = jnp.pad(jnp.stack(three_pieces(norm_gain)), ((0, TAIL - LANES - 3), (0, 512 - LANES))).astype(BF16)
    weights = lax.all_gather(jnp.concatenate([out_weight, gain], axis=0), "head", axis=0, tiled=False)

    g_x, d_x = flat(x_log_decay), flat(x_step)
    tail_x = states_x(g_x, d_x, x_in_proj, x_inputs)
    message = jnp.concatenate([jnp.broadcast_to(tail_x[None], GOT_Z), lists], axis=1)
    message, g_x, d_x = lax.optimization_barrier((message, g_x, d_x))
    got_x = lax.all_to_all(message, "seq", 0, 0)
    y_x, r_x, e_x = local_x(g_x, d_x, x_in_proj, x_out_proj, x_inputs)
    sent = send_x(y_x, x_out_proj, r_x, e_x, got_x)
    sent, g_z, d_z = lax.optimization_barrier((sent, z_log_decay, z_step))
    received = lax.all_to_all(sent.reshape(GROUPS, PIECE, LANES), "seq", 0, 0).reshape(TOK, LANES)
    s_z, b_t, w_z, t_z, a_z, r_z, e_z, ends_z = before_z(flat(g_z), flat(d_z), z_in_proj, z_out_proj)
    u2_z, tail_z = states_z(place, w_z, t_z, a_z, b_t, received)
    got_z = lax.all_to_all(jnp.broadcast_to(tail_z[None], GOT_Z), "seq", 0, 0)
    y_z = local_z(u2_z, s_z, b_t, z_out_proj, r_z, ends_z)
    gated = gate_z(y_z, z_out_proj, gate_branch, r_z, e_z, got_z)
    whole = lax.all_to_all(gated.reshape(8, 1024, LANES), "head", 0, 0)
    return final(whole, weights)


def solution(mesh):
    placed = (
        P("seq", "head"),
        P("seq", None),
        P("seq", None),
        P("head", "seq"),
        P("head", "seq"),
        P("seq"),
        P("seq", None),
        P("seq", None),
        P("head", "seq"),
        P("head", "seq"),
        P("seq", "head"),
        P("head"),
        P("head", None),
    )
    return jax.shard_map(
        body, mesh=mesh, in_specs=placed, out_specs=P(("seq", "head"), None), check_vma=False
    )
```

time: 937 us -> 202 us (0.22)
  waiting for transfers between devices: 315 us -> 49.5 us
  local copies, waits for them, and re-layouts: 186 us -> 6.78 us
  matrix products: 173 us -> 0 us
  starting transfers between devices: 152 us -> 25.8 us
  Pallas kernels: 0 us -> 95.3 us
  other arithmetic: 53.4 us -> 9.69 us
  blocking collectives: 36.8 us -> 0 us
    all_gather x1, waiting for transfers between devices: 221 us -> 1.84 us  [body(): lax.all_gather(jnp.concatenate([out_weight, gain], axis=0), 'head', axis=...]
    dot_general x99 -> x0, matrix products: 173 us -> none  [the longest x32 80.4 us: one_block(): jnp.einsum('hts,shp->thp', weights, u_blk, preferred_element_type=jnp.flo...]
    ppermute x30 -> x0, starting transfers between devices: 152 us -> none  [shifted(): lax.ppermute(value, axis, [(source, source + steps) for source in range(i...]
    gather x2 -> x0, local copies, waits for them, and re-layouts: 126 us -> none  [body(): u_z = jnp.take(whole, z_source, axis=0)]
    pallas_call x0 -> x8, Pallas kernels: none -> 95.3 us  [the longest x1 29.1 us: send_x(): call(send_x_kernel, 'send_x', 2 * STEPS, [block(ROW, early), block(ROW, e...]
    reduce_scatter x1 -> x0, waiting for transfers between devices: 63.4 us -> none  [body(): lax.psum_scatter(jnp.dot(normed, out_weight, preferred_element_type=jnp.f...]
    all_to_all x0 -> x4, waiting for transfers between devices: none -> 47.7 us  [the longest x1 24.5 us: body(): whole = lax.all_to_all(gated.reshape(8, 1024, LANES), 'head', 0, 0)]
    psum x1 -> x0, blocking collectives: 36.8 us -> none  [body(): lax.psum(jnp.sum(gated * gated, axis=1).astype(jnp.bfloat16), 'head')]
  transfers between devices with their start and end apart: 32 -> 5, of which waited for: 32 -> 5; matrix products, arithmetic and copies ran while one was open for 0% -> 0% of each run, Pallas kernels for 0% -> 18%
where the time goes in v2:
time: 202 us; the launch traced here: 201 us
  Pallas kernels  95.3 us (47%)
  waiting for transfers between devices  49.5 us (25%)
  starting transfers between devices  25.8 us (13%)
  between operations  13.5 us (7%)
  other arithmetic  9.69 us (5%)
  local copies, waits for them, and re-layouts  6.78 us (3%)
    pallas_call x1, Pallas kernels, send_x(): call(send_x_kernel, 'send_x', 2 * STEPS, [block(ROW, early), block(ROW, e...  29.1 us
    all_to_all x1, waiting for transfers between devices, body(): whole = lax.all_to_all(gated.reshape(8, 1024, LANES), 'head', 0, 0)  24.5 us
    all_to_all x1, waiting for transfers between devices, body(): lax.all_to_all(sent.reshape(GROUPS, PIECE, LANES), 'seq', 0, 0)  20.9 us
    pallas_call x1, Pallas kernels, states_z(): call(states_z_kernel, 'states_z', 2 * STEPS, [fixed(FLAT), fixed((8, LANE...  17.5 us
    pallas_call x1, Pallas kernels, local_x(): call(local_x_kernel, 'local_x', STEPS, [fixed(FLAT), fixed(FLAT), block(R...  9.82 us
    pallas_call x1, Pallas kernels, local_z(): call(local_z_kernel, 'local_z', STEPS, [block(ROW, each), block(ROW, each...  9.03 us
    pallas_call x1, Pallas kernels, gate_z(): call(gate_z_kernel, 'gate_z', STEPS, [block(ROW, each), block(ROW, each),...  8.75 us
    all_to_all x1, starting transfers between devices, body(): got_x = lax.all_to_all(message, 'seq', 0, 0)  8.43 us
  transfers between devices with their start and end apart: 5, of which 5 were waited for; matrix products, arithmetic and copies ran while one was open for 0% of the time, Pallas kernels for 18%

profile of v2, /device:TPU:1, one launch (start us, length us, event | category | flops | bytes accessed | tf_op | source)
XLA Modules:
  0.0 200.5 jit_solution(15756687110401272753)
XLA Ops:
  7.3 6.8 %sort.15 = (s32[8192]{0:T(1024)S(1)}, s32[8192]{0:T(1024)}) sort(s32[8192]{0:T(1024)S(1)} %iota_add_fusion, s32[8192]{0:T(1024)S(1)} %iota.7), dimensions={0}, to_apply=%region_0.0 | sort | flops 106496 | bytes 131072 | tf_op jit(solution)/shard_map/jit(sort)/sort | solution.py:520
  14.7 7.5 %states_x.1 = bf16[136,128]{1,0:T(8,128)(2,1)} custom-call(f32[128,128]{1,0:T(8,128)} %bitcast.35, f32[128,128]{1,0:T(8,128)} %bitcast.37, bf16[8192,128]{1,0:T(8,128)(2,1)} %b_ref.4, bf16[8192,128]{1,0:T(8,128)(2,1)} %u_ref.3), custom_call_target="tpu_custom_call" | custom-call | flops 1073741824 | bytes 4194304 | tf_op jit(solution)/shard_map/states_x/pallas_call | solution.py:408
  22.2 0.8 broadcast_in_dim.4
  23.0 0.9 pad_maximum_fusion
  23.9 8.4 %all-to-all-start = ((bf16[16,144,128]{2,1,0:T(8,128)(2,1)}), bf16[16,144,128]{2,1,0:T(8,128)(2,1)S(1)}, u32[]{:S(2)}, u32[]{:S(2)}) async-start(bf16[16,144,128]{2,1,0:T(8,128)(2,1)} %pad_maximum_fusion), calls=%async_computation | async-start | bytes 1179648 | tf_op jit(solution)/shard_map/all_to_all | solution.py:534
  32.3 9.8 %local_x.1 = (f32[8192,128]{1,0:T(8,128)}, f32[128,128]{1,0:T(8,128)}, f32[128,128]{1,0:T(8,128)}) custom-call(f32[128,128]{1,0:T(8,128)} %bitcast.36, f32[128,128]{1,0:T(8,128)} %bitcast.38, bf16[8192,128]{1,0:T(8,128)(2,1)} %b_ref.4, bf16[8192,128]{1,0:T(8,128)(2,1)} %c_ref.6, bf16[8192,128]{1,0:T(8,128)(2,1)} %u_ref.3), custom_call_target="tpu_custom_call" | custom-call | flops 2684354560 | bytes 10485760 | tf_op jit(solution)/shard_map/local_x/pallas_call | solution.py:417
  42.1 1.3 all-to-all-done.got_ref
  43.4 0.8 copy-done.3
  44.2 29.1 %send_x.1 = bf16[8192,128]{1,0:T(8,128)(2,1)} custom-call(f32[8192,128]{1,0:T(8,128)} %get-tuple-element.29.y_ref, bf16[8192,128]{1,0:T(8,128)(2,1)} %c_ref.6, f32[128,128]{1,0:T(8,128)} %get-tuple-element.30.r_ref, f32[128,128]{1,0:T(8,128)} %get-tuple-element.31.e_ref, bf16[16,144,128]{2,1,0:T(8,128)(2,1)} %copy-done.3), custom_call_target="tpu_custom_call" | custom-call | flops 2684354560 | bytes 10485760 | tf_op jit(solution)/shard_map/send_x/pallas_call | solution.py:427
  73.3 5.4 %all-to-all-start.1 = ((bf16[16,512,128]{2,1,0:T(8,128)(2,1)}), bf16[16,512,128]{2,1,0:T(8,128)(2,1)S(1)}, u32[]{:S(2)}, u32[]{:S(2)}) async-start(bf16[16,512,128]{2,1,0:T(8,128)(2,1)} %bitcast.34), calls=%async_computation.1 | async-start | bytes 4194304 | tf_op jit(solution)/shard_map/all_to_all | solution.py:538
  78.7 7.8 %before_z.1 = (bf16[8192,128]{1,0:T(8,128)(2,1)}, bf16[128,8192]{1,0:T(8,128)(2,1)}, f32[128,128]{1,0:T(8,128)}, f32[8,128]{1,0:T(8,128)}, f32[128,128]{1,0:T(8,...) custom-call(f32[128,128]{1,0:T(8,128)} %bitcast.42, f32[128,128]{1,0:T(8,128)} %bitcast.43, ...), custom_call_target="tpu_custom_call" | custom-call | flops 2147483648 | bytes 8388608 | tf_op jit(solution)/shard_map/before_z/pallas_call | solution.py:439
  86.5 20.9 %all-to-all-done.1 = bf16[16,512,128]{2,1,0:T(8,128)(2,1)S(1)} async-done(((bf16[16,512,128]{2,1,0:T(8,128)(2,1)}), bf16[16,512,128]{2,1,0:T(8,128)(2,1)S(1)}, u32[]{:S(2)}, u32[]{:S(2)}) %all-to-all-start.1) | async-done | bytes 2097184 | tf_op jit(solution)/shard_map/all_to_all | solution.py:538
  107.4 1.3 copy-done.1
  108.8 17.5 %states_z.1 = (bf16[8192,128]{1,0:T(8,128)(2,1)}, bf16[136,128]{1,0:T(8,128)(2,1)}) custom-call(s32[8192]{0:T(1024)} %get-tuple-element.48.place, f32[128,128]{1,0:T(8,128)} %get-tuple-element.35.w_ref, f32[8,128]{1,0:T(8,128)} %get-tuple-element.36.t_ref, f32[128,128]{1,0:T(8,128)} %get-tuple-element.37.a_ref, bf16[128,8192]{1,0:T(8,128)(2,1)} %get-tuple-element.38.b_t_ref, ...), custom_call_target="tpu_custom_call" | custom-call | flops 2147483648 | bytes 8388608 | tf_op jit(solution)/shard_map/states_z/pallas_call | solution.py:455
  126.3 1.6 broadcast_in_dim.5
  128.0 5.4 %all-to-all-start.2 = ((bf16[16,136,128]{2,1,0:T(8,128)(2,1)}), bf16[16,136,128]{2,1,0:T(8,128)(2,1)S(1)}, u32[]{:S(2)}, u32[]{:S(2)}) async-start(bf16[16,136,128]{2,1,0:T(8,128)(2,1)} %broadcast_in_dim.5), calls=%async_computation.2 | async-start | bytes 1114112 | tf_op jit(solution)/shard_map/all_to_all | solution.py:541
  134.2 9.0 %local_z.1.y_ref = f32[8192,128]{1,0:T(8,128)} custom-call(bf16[8192,128]{1,0:T(8,128)(2,1)} %get-tuple-element.40.u2_ref, bf16[8192,128]{1,0:T(8,128)(2,1)} %get-tuple-element.41.s_ref, bf16[128,8192]{1,0:T(8,128)(2,1)} %get-tuple-element.38.b_t_ref, bf16[8192,128]{1,0:T(8,128)(2,1)} %c_ref.9, f32[128,128]{1,0:T(8,128)} %get-tuple-element.42.r_ref, ...), custom_call_target="tpu_custom_call" | custom-call | flops 2684354560 | bytes 10485760 | tf_op jit(solution)/shard_map/local_z/pallas_call | solution.py:468
  143.2 1.0 all-to-all-done.2.got_ref
  145.0 8.8 %gate_z.1 = bf16[8192,128]{1,0:T(8,128)(2,1)} custom-call(f32[8192,128]{1,0:T(8,128)} %local_z.1.y_ref, bf16[8192,128]{1,0:T(8,128)(2,1)} %c_ref.9, bf16[8192,128]{1,0:T(8,128)(2,1)} %gate_ref.1, f32[128,128]{1,0:T(8,128)} %get-tuple-element.42.r_ref, f32[128,128]{1,0:T(8,128)} %get-tuple-element.44.e_ref, bf16[16,136,128]{2,1,0:T(8,128)(2,1)} %copy-done), custom_call_target="tpu_custom_call" | custom-call | flops 2684354560 | bytes 10485760 | tf_op jit(solution)/shard_map/gate_z/pallas_call | solution.py:479
  153.8 6.5 %all-to-all-start.3 = ((bf16[8,1024,128]{2,1,0:T(8,128)(2,1)}), bf16[8,1024,128]{2,1,0:T(8,128)(2,1)S(1)}, u32[]{:S(2)}, u32[]{:S(2)}) async-start(bf16[8,1024,128]{2,1,0:T(8,128)(2,1)} %bitcast.32), calls=%async_computation.3 | async-start | bytes 4194304 | tf_op jit(solution)/shard_map/all_to_all | solution.py:544
  160.3 1.8 all-gather.3.cloned.1.call-done
  162.1 24.5 %all-to-all-done.3.x_ref = bf16[8,1024,128]{2,1,0:T(8,128)(2,1)S(1)} async-done(((bf16[8,1024,128]{2,1,0:T(8,128)(2,1)}), bf16[8,1024,128]{2,1,0:T(8,128)(2,1)S(1)}, u32[]{:S(2)}, u32[]{:S(2)}) %all-to-all-start.3) | async-done | bytes 2097184 | tf_op jit(solution)/shard_map/all_to_all | solution.py:544
  186.6 1.3 copy-done.2
  187.9 5.8 %final.1 = bf16[1024,512]{1,0:T(8,128)(2,1)} custom-call(bf16[8,1024,128]{2,1,0:T(8,128)(2,1)} %copy-done.2, bf16[8,136,512]{2,1,0:T(8,128)(2,1)} %bitcast.41), custom_call_target="tpu_custom_call" | custom-call | flops 1342177280 | bytes 5242880 | tf_op jit(solution)/shard_map/final/pallas_call | solution.py:488
  (17 shorter events, 2.9 us)
Async XLA Ops:
  23.9 19.5 %all-to-all-start = ((bf16[16,144,128]{2,1,0:T(8,128)(2,1)}), bf16[16,144,128]{2,1,0:T(8,128)(2,1)S(1)}, u32[]{:S(2)}, u32[]{:S(2)}) async-start(bf16[16,144,128]{2,1,0:T(8,128)(2,1)} %pad_maximum_fusion), calls=%async_computation | async-start | bytes 1179648 | tf_op jit(solution)/shard_map/all_to_all | solution.py:534
  43.4 0.8 copy-start.3
  73.3 34.2 %all-to-all-start.1 = ((bf16[16,512,128]{2,1,0:T(8,128)(2,1)}), bf16[16,512,128]{2,1,0:T(8,128)(2,1)S(1)}, u32[]{:S(2)}, u32[]{:S(2)}) async-start(bf16[16,512,128]{2,1,0:T(8,128)(2,1)} %bitcast.34), calls=%async_computation.1 | async-start | bytes 4194304 | tf_op jit(solution)/shard_map/all_to_all | solution.py:538
  107.4 1.3 copy-start.1
  108.8 24.7 %copy-start.5 = (f32[128]{0:T(128)S(1)}, f32[128]{0:T(128)}, u32[]{:S(2)}) copy-start(f32[128]{0:T(128)} %param.24) | copy-start | bytes 1540
  108.8 24.7 %copy-start.4 = (bf16[128,512]{1,0:T(8,128)(2,1)S(1)}, bf16[128,512]{1,0:T(8,128)(2,1)}, u32[]{:S(2)}) copy-start(bf16[128,512]{1,0:T(8,128)(2,1)} %param.25) | copy-start | bytes 393220
  128.0 16.3 %all-to-all-start.2 = ((bf16[16,136,128]{2,1,0:T(8,128)(2,1)}), bf16[16,136,128]{2,1,0:T(8,128)(2,1)S(1)}, u32[]{:S(2)}, u32[]{:S(2)}) async-start(bf16[16,136,128]{2,1,0:T(8,128)(2,1)} %broadcast_in_dim.5), calls=%async_computation.2 | async-start | bytes 1114112 | tf_op jit(solution)/shard_map/all_to_all | solution.py:541
  133.4 28.7 %all-gather.3.cloned.1.call-start = ((), (), s32[]{:S(2)}) async-start(), calls=%async_computation.4 | async-start | bytes 1253376 | tf_op jit(solution)/shard_map/all_gather | solution.py:528
  144.2 0.8 copy-start
  153.8 32.8 %all-to-all-start.3 = ((bf16[8,1024,128]{2,1,0:T(8,128)(2,1)}), bf16[8,1024,128]{2,1,0:T(8,128)(2,1)S(1)}, u32[]{:S(2)}, u32[]{:S(2)}) async-start(bf16[8,1024,128]{2,1,0:T(8,128)(2,1)} %bitcast.32), calls=%async_computation.3 | async-start | bytes 4194304 | tf_op jit(solution)/shard_map/all_to_all | solution.py:544
  186.6 1.3 copy-start.2
Sparse Core Ops, SparseCore 0:
  135.9 26.1 all-gather.2

commit v3 on v2

--- a/solution.py
+++ b/solution.py
@@ -10,14 +10,14 @@
 TOK = 8192
 LANES = 128
 CHUNK = 128
-STEP = 1024
+STEP = 4096
 PER = STEP // CHUNK
 STEPS = TOK // STEP
 PIECE = 512
 GROUPS = 16
-TAIL = 136
-MSG = 144
-UNROLL = 32
+TAIL = 144
+MSG = 160
+WROWS = 136
 F32 = jnp.float32
 BF16 = jnp.bfloat16
 
@@ -68,8 +68,8 @@
 
 
 def spread_mask():
-    row = lax.broadcasted_iota(jnp.int32, (48, STEP), 0) & 15
-    col = lax.broadcasted_iota(jnp.int32, (48, STEP), 1)
+    row = lax.broadcasted_iota(jnp.int32, (6 * PER, STEP), 0) & (2 * PER - 1)
+    col = lax.broadcasted_iota(jnp.int32, (6 * PER, STEP), 1)
     return ones(row == 2 * (col >> 7) + ((col >> 6) & 1))
 
 
@@ -78,7 +78,7 @@
 
 
 def slab_at(step):
-    return pl.ds(pl.multiple_of(16 * step, 16), 16)
+    return pl.ds(pl.multiple_of(2 * PER * step, 2 * PER), 2 * PER)
 
 
 def end_weights(g, d):
@@ -111,18 +111,58 @@
     mid = (total - high).astype(BF16).astype(F32)
     low = total - high - mid
     pad = jnp.zeros((TAIL - CHUNK - 3, LANES), F32)
-    msg_ref[...] = jnp.concatenate([state, high, mid, low, pad], axis=0).astype(BF16)
+    tail = jnp.concatenate([state, high, mid, low, pad], axis=0).astype(BF16)
+    for k in range(GROUPS):
+        msg_ref[k, 0:TAIL, :] = tail
+
+
+def match_rows(index, count):
+    return lax.broadcasted_iota(jnp.int32, (count, LANES), 0) == index
+
+
+def route(z_ref, msg_ref, place_ref):
+    z = z_ref[...]
+    group, token = z >> 13, z & (TOK - 1)
+    row, col = iotas()
+    hits = [group == k for k in range(GROUPS)]
+    inside = mm(jnp.concatenate([ones(hit) for hit in hits], axis=0), ones(row <= col))
+    counts = [inside[64 * k : 64 * k + 64] for k in range(GROUPS)]
+    sums = jnp.concatenate([jnp.broadcast_to(count[:, 127:128], (64, LANES)) for count in counts], axis=1)
+    above = mm(ones(row > col)[0:64, 0:64], sums.astype(BF16))
+    slot = jnp.zeros((64, LANES), F32)
+    for k in range(GROUPS):
+        rank = counts[k] + above[:, k * LANES : (k + 1) * LANES] + float(k * PIECE - 1)
+        slot = jnp.where(hits[k], rank, slot)
+    slot = slot.astype(jnp.int32)
+    slot_high, slot_low = slot >> 7, slot & 127
+    token_high, token_low = (token >> 7).astype(F32), (token & 127).astype(F32)
+    lane = lax.broadcasted_iota(jnp.int32, (1, LANES), 1).astype(F32)
+    total = jnp.zeros((256, LANES), F32)
+    for base in range(0, 64, 4):
+        lefts, rights = [], []
+        for q in range(base, base + 4):
+            hit = match_rows(slot_high[q : q + 1], 64)
+            values = (token_high[q : q + 1], token_low[q : q + 1], float(q), lane)
+            lefts.append(jnp.concatenate([jnp.where(hit, value, 0.0) for value in values], axis=0).astype(BF16))
+            rights.append(ones(match_rows(slot_low[q : q + 1], LANES)))
+        total = total + nt(jnp.concatenate(lefts, axis=1), jnp.concatenate(rights, axis=1))
+    place_ref[...] = (total[128:192] * 128.0 + total[192:256]).astype(jnp.int32)
+    for k in range(GROUPS):
+        rows = slice(4 * k, 4 * k + 4)
+        wanted = jnp.concatenate([total[rows], total[64 + 4 * k : 68 + 4 * k], jnp.zeros((8, LANES), F32)], axis=0)
+        msg_ref[k, TAIL:MSG, :] = wanted.astype(BF16)
 
 
 def chunk_rows(at):
     return slice(at * CHUNK, (at + 1) * CHUNK)
 
 
-def states_x_kernel(g_ref, d_ref, b_ref, u_ref, msg_ref, weights, mask, state, total):
+def states_x_kernel(z_ref, g_ref, d_ref, b_ref, u_ref, msg_ref, place_ref, weights, mask, state, total):
     step = pl.program_id(0)
 
     @pl.when(step == 0)
     def _():
+        route(z_ref, msg_ref, place_ref)
         weights[...], total[0:1, :] = end_weights(g_ref[...], d_ref[...])
         mask[...] = spread_mask()
         state[...] = jnp.zeros_like(state)
@@ -213,6 +253,17 @@
     slots[...] = (total[0:64] * 128.0 + total[64:128]).astype(jnp.int32)
 
 
+def scatter(rows, table, line, ordered):
+    def put(i, _):
+        for q in range(LANES // 8):
+            value = rows[pl.ds(pl.multiple_of(i * LANES + q * 8, 8), 8), :]
+            for k in range(8):
+                ordered[pl.ds(table[line + i, q * 8 + k], 1), :] = value[k : k + 1, :]
+        return 0
+
+    lax.fori_loop(0, PER, put, 0)
+
+
 def send_x_kernel(
     y_ref, c_ref, r_ref, e_ref, got_ref, out_ref, state, mask, rows, ordered, slots, table, sem
 ):
@@ -236,14 +287,7 @@
 
         add_start(y_ref, c_ref, r_ref[here, :], e_ref[here, :], mask[...], state, write)
 
-        def put(i, _):
-            line = step * PER + i // 4
-            base = (i % 4) * UNROLL
-            for k in range(UNROLL):
-                ordered[pl.ds(table[line, base + k], 1), :] = rows[pl.ds(i * UNROLL + k, 1), :]
-            return 0
-
-        lax.fori_loop(0, STEP // UNROLL, put, 0)
+        scatter(rows, table, step * PER, ordered)
 
     @pl.when(step >= STEPS)
     def _():
@@ -282,13 +326,7 @@
     def _():
         rows[...] = got_ref[...].astype(F32)
 
-        def put(i, _):
-            base = step * STEP + i * UNROLL
-            for k in range(UNROLL):
-                ordered[pl.ds(place[base + k], 1), :] = rows[pl.ds(i * UNROLL + k, 1), :]
-            return 0
-
-        lax.fori_loop(0, STEP // UNROLL, put, 0)
+        scatter(rows, place, step * PER, ordered)
 
     @pl.when(step >= STEPS)
     def _():
@@ -335,7 +373,7 @@
 
     def write(at, value):
         gate = gate_ref[chunk_rows(at), :].astype(F32)
-        silu = gate / (1.0 + jnp.exp(-gate))
+        silu = gate * (0.5 * jnp.tanh(0.5 * gate) + 0.5)
         out_ref[chunk_rows(at), :] = (value.astype(BF16).astype(F32) * silu).astype(BF16)
 
     here = slab_at(step)
@@ -349,7 +387,7 @@
     scale = lax.rsqrt(mean + 1e-05)
     total = None
     for k in range(8):
-        parts3 = w_ref[k, LANES:TAIL, 0:LANES].astype(F32)
+        parts3 = w_ref[k, LANES:WROWS, 0:LANES].astype(F32)
         gain = parts3[0:1] + parts3[1:2] + parts3[2:3]
         term = mm((parts[k] * scale * gain).astype(BF16), w_ref[k, 0:LANES, :])
         total = term if total is None else total + term
@@ -361,7 +399,7 @@
 GOT_X = (GROUPS, MSG, LANES)
 GOT_Z = (GROUPS, TAIL, LANES)
 ENDS = (3, CHUNK, LANES)
-MASK = pltpu.VMEM((48, STEP), BF16)
+MASK = pltpu.VMEM((6 * PER, STEP), BF16)
 STATE = pltpu.VMEM(FLAT, F32)
 
 
@@ -404,13 +442,13 @@
     )
 
 
-def states_x(g, d, b, u):
+def states_x(z, g, d, b, u):
     return call(
         states_x_kernel, "states_x", STEPS,
-        [fixed(FLAT), fixed(FLAT), block(ROW, each), block(ROW, each)],
-        fixed((TAIL, LANES)), struct((TAIL, LANES), BF16),
+        [fixed((64, LANES)), fixed(FLAT), fixed(FLAT), block(ROW, each), block(ROW, each)],
+        [fixed(GOT_X), fixed((64, LANES))], [struct(GOT_X, BF16), struct((64, LANES), jnp.int32)],
         [STATE, MASK, STATE, pltpu.VMEM((8, LANES), F32)], 4,
-    )(g, d, b, u)
+    )(z, g, d, b, u)
 
 
 def local_x(g, d, b, c, u):
@@ -458,8 +496,8 @@
             fixed(FLAT), fixed((8, LANES)), fixed(FLAT),
             block((CHUNK, STEP), lambda i, _: (0, jnp.maximum(i - STEPS, 0))), block(ROW, early),
         ],
-        [block(ROW, late), fixed((TAIL, LANES))],
-        [struct((TOK, LANES), BF16), struct((TAIL, LANES), BF16)],
+        [block(ROW, late), fixed(GOT_Z)],
+        [struct((TOK, LANES), BF16), struct(GOT_Z, BF16)],
         [MASK, STATE, pltpu.VMEM(ROW, F32), pltpu.VMEM((TOK, LANES), F32)], 8, prefetch=1,
     )(place, w, t, a, b_t, got)
 
@@ -487,8 +525,8 @@
     rows = 256
     return call(
         final_kernel, "final", 1024 // rows,
-        [block((8, rows, LANES), lambda i: (0, i, 0)), fixed((8, TAIL, 512))],
-        block((rows, 512), each), struct((1024, 512), BF16), [], 5,
+        [block((8, rows, LANES), lambda i: (0, i, 0)), fixed((8, WROWS, 512))],
+        block((rows, 512), each), struct((1024, 512), BF16), [], 5, limit=20,
     )(x, w)
 
 
@@ -517,28 +555,21 @@
     norm_gain,
     out_weight,
 ):
-    order = jnp.sort(z_source * TOK + lax.iota(jnp.int32, TOK))
-    place = order & (TOK - 1)
-    source = (order >> 13) & (TOK - 1)
-    lists = jnp.concatenate(
-        [(source >> 7).reshape(GROUPS, 4, LANES), (source & 127).reshape(GROUPS, 4, LANES)], axis=1
-    ).astype(BF16)
-
-    gain = jnp.pad(jnp.stack(three_pieces(norm_gain)), ((0, TAIL - LANES - 3), (0, 512 - LANES))).astype(BF16)
-    weights = lax.all_gather(jnp.concatenate([out_weight, gain], axis=0), "head", axis=0, tiled=False)
-
     g_x, d_x = flat(x_log_decay), flat(x_step)
-    tail_x = states_x(g_x, d_x, x_in_proj, x_inputs)
-    message = jnp.concatenate([jnp.broadcast_to(tail_x[None], GOT_Z), lists], axis=1)
+    message, place = states_x(z_source.reshape(64, LANES), g_x, d_x, x_in_proj, x_inputs)
     message, g_x, d_x = lax.optimization_barrier((message, g_x, d_x))
     got_x = lax.all_to_all(message, "seq", 0, 0)
     y_x, r_x, e_x = local_x(g_x, d_x, x_in_proj, x_out_proj, x_inputs)
     sent = send_x(y_x, x_out_proj, r_x, e_x, got_x)
-    sent, g_z, d_z = lax.optimization_barrier((sent, z_log_decay, z_step))
+    sent, g_z, d_z, norm_gain, out_weight = lax.optimization_barrier(
+        (sent, z_log_decay, z_step, norm_gain, out_weight)
+    )
+    gain = jnp.pad(jnp.stack(three_pieces(norm_gain)), ((0, WROWS - LANES - 3), (0, 512 - LANES))).astype(BF16)
+    weights = lax.all_gather(jnp.concatenate([out_weight, gain], axis=0), "head", axis=0, tiled=False)
     received = lax.all_to_all(sent.reshape(GROUPS, PIECE, LANES), "seq", 0, 0).reshape(TOK, LANES)
     s_z, b_t, w_z, t_z, a_z, r_z, e_z, ends_z = before_z(flat(g_z), flat(d_z), z_in_proj, z_out_proj)
-    u2_z, tail_z = states_z(place, w_z, t_z, a_z, b_t, received)
-    got_z = lax.all_to_all(jnp.broadcast_to(tail_z[None], GOT_Z), "seq", 0, 0)
+    u2_z, tails_z = states_z(place, w_z, t_z, a_z, b_t, received)
+    got_z = lax.all_to_all(tails_z, "seq", 0, 0)
     y_z = local_z(u2_z, s_z, b_t, z_out_proj, r_z, ends_z)
     gated = gate_z(y_z, z_out_proj, gate_branch, r_z, e_z, got_z)
     whole = lax.all_to_all(gated.reshape(8, 1024, LANES), "head", 0, 0)

time: 202 us -> 165 us (0.82)
  Pallas kernels: 95.3 us -> 64.4 us
  other arithmetic: 9.69 us -> 0.68 us
  waiting for transfers between devices: 49.5 us -> 55.8 us
  local copies, waits for them, and re-layouts: 6.78 us -> 4.24 us
    pallas_call x1, Pallas kernels: 29.1 us -> 13.8 us  [send_x(): call(send_x_kernel, 'send_x', 2 * STEPS, [block(ROW, early), block(ROW, e...]
    sort x1 -> x0, other arithmetic: 6.77 us -> none  [body(): order = jnp.sort(z_source * TOK + lax.iota(jnp.int32, TOK))]
    pallas_call x1, Pallas kernels: 17.5 us -> 13.7 us  [states_z(): call(states_z_kernel, 'states_z', 2 * STEPS, [fixed(FLAT), fixed((8, LANE...]
    pallas_call x1, Pallas kernels: 7.85 us -> 4.79 us  [before_z(): call(before_z_kernel, 'before_z', STEPS, [fixed(FLAT), fixed(FLAT), block...]
    broadcast_in_dim x2 -> x0, local copies, waits for them, and re-layouts: 2.47 us -> none  [the longest x1 1.64 us: body(): got_z = lax.all_to_all(jnp.broadcast_to(tail_z[None], GOT_Z), 'seq', 0, 0)]
    all_to_all x1, waiting for transfers between devices: 1.26 us -> 3.67 us  [body(): got_x = lax.all_to_all(message, 'seq', 0, 0)]
    pallas_call x1, Pallas kernels: 9.03 us -> 6.83 us  [local_z(): call(local_z_kernel, 'local_z', STEPS, [block(ROW, each), block(ROW, each...]
    all_to_all x1, waiting for transfers between devices: 1 us -> 3.05 us  [body(): got_z = lax.all_to_all(tails_z, 'seq', 0, 0)]
  transfers between devices with their start and end apart: 5 -> 5, of which waited for: 5 -> 5; matrix products, arithmetic and copies ran while one was open for 0% -> 0% of each run, Pallas kernels for 18% -> 16%
where the time goes in v3:
time: 165 us; the launch traced here: 164 us
  Pallas kernels  64.4 us (39%)
  waiting for transfers between devices  55.8 us (34%)
  starting transfers between devices  25.8 us (16%)
  between operations  13.5 us (8%)
  local copies, waits for them, and re-layouts  4.24 us (3%)
    all_to_all x1, waiting for transfers between devices, body(): lax.all_to_all(sent.reshape(GROUPS, PIECE, LANES), 'seq', 0, 0)  22.8 us
    all_to_all x1, waiting for transfers between devices, body(): whole = lax.all_to_all(gated.reshape(8, 1024, LANES), 'head', 0, 0)  22.7 us
    pallas_call x1, Pallas kernels, send_x(): call(send_x_kernel, 'send_x', 2 * STEPS, [block(ROW, early), block(ROW, e...  13.8 us
    pallas_call x1, Pallas kernels, states_z(): call(states_z_kernel, 'states_z', 2 * STEPS, [fixed(FLAT), fixed((8, LANE...  13.7 us
    all_to_all x1, starting transfers between devices, body(): got_x = lax.all_to_all(message, 'seq', 0, 0)  8.42 us
    pallas_call x1, Pallas kernels, local_x(): call(local_x_kernel, 'local_x', STEPS, [fixed(FLAT), fixed(FLAT), block(R...  8.08 us
    all_to_all x1, starting transfers between devices, body(): whole = lax.all_to_all(gated.reshape(8, 1024, LANES), 'head', 0, 0)  7 us
    pallas_call x1, Pallas kernels, local_z(): call(local_z_kernel, 'local_z', STEPS, [block(ROW, each), block(ROW, each...  6.83 us
  transfers between devices with their start and end apart: 5, of which 5 were waited for; matrix products, arithmetic and copies ran while one was open for 0% of the time, Pallas kernels for 16%

profile of v3, /device:TPU:1, one launch (start us, length us, event | category | flops | bytes accessed | tf_op | source)
XLA Modules:
  0.0 164.4 jit_solution(18420374780861311538)
XLA Ops:
  6.5 6.3 %states_x.1 = (bf16[16,160,128]{2,1,0:T(8,128)(2,1)}, s32[64,128]{1,0:T(8,128)}) custom-call(s32[64,128]{1,0:T(8,128)} %bitcast.39, f32[128,128]{1,0:T(8,128)} %bitcast.35, f32[128,128]{1,0:T(8,128)} %bitcast.37, bf16[8192,128]{1,0:T(8,128)(2,1)} %b_ref.4, bf16[8192,128]{1,0:T(8,128)(2,1)} %u_ref.3), custom_call_target="tpu_custom_call" | custom-call | flops 1073741824 | bytes 4194304 | tf_op jit(solution)/shard_map/states_x/pallas_call | solution.py:446
  12.8 8.4 %all-to-all-start = ((bf16[16,160,128]{2,1,0:T(8,128)(2,1)}), bf16[16,160,128]{2,1,0:T(8,128)(2,1)S(1)}, u32[]{:S(2)}, u32[]{:S(2)}) async-start(bf16[16,160,128]{2,1,0:T(8,128)(2,1)} %get-tuple-element.35), calls=%async_computation | async-start | bytes 1310720 | tf_op jit(solution)/shard_map/all_to_all | solution.py:561
  21.2 8.1 %local_x.1 = (f32[8192,128]{1,0:T(8,128)}, f32[128,128]{1,0:T(8,128)}, f32[128,128]{1,0:T(8,128)}) custom-call(f32[128,128]{1,0:T(8,128)} %bitcast.36, f32[128,128]{1,0:T(8,128)} %bitcast.38, bf16[8192,128]{1,0:T(8,128)(2,1)} %b_ref.4, bf16[8192,128]{1,0:T(8,128)(2,1)} %c_ref.6, bf16[8192,128]{1,0:T(8,128)(2,1)} %u_ref.3), custom_call_target="tpu_custom_call" | custom-call | flops 2684354560 | bytes 10485760 | tf_op jit(solution)/shard_map/local_x/pallas_call | solution.py:455
  29.3 3.7 %all-to-all-done.got_ref = bf16[16,160,128]{2,1,0:T(8,128)(2,1)S(1)} async-done(((bf16[16,160,128]{2,1,0:T(8,128)(2,1)}), bf16[16,160,128]{2,1,0:T(8,128)(2,1)S(1)}, u32[]{:S(2)}, u32[]{:S(2)}) %all-to-all-start) | async-done | bytes 655392 | tf_op jit(solution)/shard_map/all_to_all | solution.py:561
  33.0 0.8 copy-done.3
  33.8 13.8 %send_x.1 = bf16[8192,128]{1,0:T(8,128)(2,1)} custom-call(f32[8192,128]{1,0:T(8,128)} %get-tuple-element.32.y_ref, bf16[8192,128]{1,0:T(8,128)(2,1)} %c_ref.6, f32[128,128]{1,0:T(8,128)} %get-tuple-element.33.r_ref, f32[128,128]{1,0:T(8,128)} %get-tuple-element.34.e_ref, bf16[16,160,128]{2,1,0:T(8,128)(2,1)} %copy-done.3), custom_call_target="tpu_custom_call" | custom-call | flops 2684354560 | bytes 10485760 | tf_op jit(solution)/shard_map/send_x/pallas_call | solution.py:465
  47.6 3.9 %all-to-all-start.1 = ((bf16[16,512,128]{2,1,0:T(8,128)(2,1)}), bf16[16,512,128]{2,1,0:T(8,128)(2,1)S(1)}, u32[]{:S(2)}, u32[]{:S(2)}) async-start(bf16[16,512,128]{2,1,0:T(8,128)(2,1)} %bitcast.34), calls=%async_computation.1 | async-start | bytes 4194304 | tf_op jit(solution)/shard_map/all_to_all | solution.py:569
  51.6 4.8 %before_z.1 = (bf16[8192,128]{1,0:T(8,128)(2,1)}, bf16[128,8192]{1,0:T(8,128)(2,1)}, f32[128,128]{1,0:T(8,128)}, f32[8,128]{1,0:T(8,128)}, f32[128,128]{1,0:T(8,...) custom-call(f32[128,128]{1,0:T(8,128)} %bitcast.40, f32[128,128]{1,0:T(8,128)} %bitcast.41, ...), custom_call_target="tpu_custom_call" | custom-call | flops 2147483648 | bytes 8388608 | tf_op jit(solution)/shard_map/before_z/pallas_call | solution.py:477
  56.4 22.8 %all-to-all-done.1 = bf16[16,512,128]{2,1,0:T(8,128)(2,1)S(1)} async-done(((bf16[16,512,128]{2,1,0:T(8,128)(2,1)}), bf16[16,512,128]{2,1,0:T(8,128)(2,1)S(1)}, u32[]{:S(2)}, u32[]{:S(2)}) %all-to-all-start.1) | async-done | bytes 2097184 | tf_op jit(solution)/shard_map/all_to_all | solution.py:569
  79.1 1.3 copy-done.2
  80.5 13.7 %states_z.1 = (bf16[8192,128]{1,0:T(8,128)(2,1)}, bf16[16,144,128]{2,1,0:T(8,128)(2,1)}) custom-call(s32[64,128]{1,0:T(8,128)} %get-tuple-element.28.place, f32[128,128]{1,0:T(8,128)} %get-tuple-element.38.w_ref, f32[8,128]{1,0:T(8,128)} %get-tuple-element.39.t_ref, f32[128,128]{1,0:T(8,128)} %get-tuple-element.40.a_ref, ...), custom_call_target="tpu_custom_call" | custom-call | flops 2147483648 | bytes 8388608 | tf_op jit(solution)/shard_map/states_z/pallas_call | solution.py:493
  94.2 6.2 %all-to-all-start.2 = ((bf16[16,144,128]{2,1,0:T(8,128)(2,1)}), bf16[16,144,128]{2,1,0:T(8,128)(2,1)S(1)}, u32[]{:S(2)}, u32[]{:S(2)}) async-start(bf16[16,144,128]{2,1,0:T(8,128)(2,1)} %get-tuple-element.48), calls=%async_computation.2 | async-start | bytes 1179648 | tf_op jit(solution)/shard_map/all_to_all | solution.py:572
  100.4 0.2 all-gather.3.cloned.1.call-start
  100.7 0.7 pad_maximum_fusion
  101.3 0.0 all-gather.3.cloned.1.call-update
  101.4 6.8 %local_z.1.y_ref = f32[8192,128]{1,0:T(8,128)} custom-call(bf16[8192,128]{1,0:T(8,128)(2,1)} %get-tuple-element.43.u2_ref, bf16[8192,128]{1,0:T(8,128)(2,1)} %get-tuple-element.44.s_ref, bf16[128,8192]{1,0:T(8,128)(2,1)} %get-tuple-element.41.b_t_ref, bf16[8192,128]{1,0:T(8,128)(2,1)} %c_ref.9, f32[128,128]{1,0:T(8,128)} %get-tuple-element.45.r_ref, ...), custom_call_target="tpu_custom_call" | custom-call | flops 2684354560 | bytes 10485760 | tf_op jit(solution)/shard_map/local_z/pallas_call | solution.py:506
  108.2 3.1 %all-to-all-done.2.got_ref = bf16[16,144,128]{2,1,0:T(8,128)(2,1)S(1)} async-done(((bf16[16,144,128]{2,1,0:T(8,128)(2,1)}), bf16[16,144,128]{2,1,0:T(8,128)(2,1)S(1)}, u32[]{:S(2)}, u32[]{:S(2)}) %all-to-all-start.2) | async-done | bytes 589856 | tf_op jit(solution)/shard_map/all_to_all | solution.py:572
  111.3 0.8 copy-done.1
  112.1 6.8 %gate_z.1 = bf16[8192,128]{1,0:T(8,128)(2,1)} custom-call(f32[8192,128]{1,0:T(8,128)} %local_z.1.y_ref, bf16[8192,128]{1,0:T(8,128)(2,1)} %c_ref.9, bf16[8192,128]{1,0:T(8,128)(2,1)} %gate_ref.1, f32[128,128]{1,0:T(8,128)} %get-tuple-element.45.r_ref, f32[128,128]{1,0:T(8,128)} %get-tuple-element.47.e_ref, bf16[16,144,128]{2,1,0:T(8,128)(2,1)} %copy-done.1), custom_call_target="tpu_custom_call" | custom-call | flops 2684354560 | bytes 10485760 | tf_op jit(solution)/shard_map/gate_z/pallas_call | solution.py:517
  118.8 7.0 %all-to-all-start.3 = ((bf16[8,1024,128]{2,1,0:T(8,128)(2,1)}), bf16[8,1024,128]{2,1,0:T(8,128)(2,1)S(1)}, u32[]{:S(2)}, u32[]{:S(2)}) async-start(bf16[8,1024,128]{2,1,0:T(8,128)(2,1)} %bitcast.32), calls=%async_computation.3 | async-start | bytes 4194304 | tf_op jit(solution)/shard_map/all_to_all | solution.py:575
  125.8 3.6 %all-gather.3.cloned.1.call-done = bf16[1088,512]{1,0:T(8,128)(2,1)} async-done(((bf16[136,512]{1,0:T(8,128)(2,1)}), bf16[1088,512]{1,0:T(8,128)(2,1)}) %all-gather.3.cloned.1.call-update) | async-done | bytes 1114128 | tf_op jit(solution)/shard_map/all_gather | solution.py:568
  129.5 22.7 %all-to-all-done.3.x_ref = bf16[8,1024,128]{2,1,0:T(8,128)(2,1)S(1)} async-done(((bf16[8,1024,128]{2,1,0:T(8,128)(2,1)}), bf16[8,1024,128]{2,1,0:T(8,128)(2,1)S(1)}, u32[]{:S(2)}, u32[]{:S(2)}) %all-to-all-start.3) | async-done | bytes 2097184 | tf_op jit(solution)/shard_map/all_to_all | solution.py:575
  152.2 1.2 copy-done
  153.4 4.2 %final.1 = bf16[1024,512]{1,0:T(8,128)(2,1)} custom-call(bf16[8,1024,128]{2,1,0:T(8,128)(2,1)S(1)} %all-to-all-done.3.x_ref, bf16[8,136,512]{2,1,0:T(8,128)(2,1)S(1)} %bitcast.31), custom_call_target="tpu_custom_call" | custom-call | flops 1342177280 | bytes 5242880 | tf_op jit(solution)/shard_map/final/pallas_call | solution.py:526
  (10 shorter events, 0.0 us)
Async XLA Ops:
  12.8 20.2 %all-to-all-start = ((bf16[16,160,128]{2,1,0:T(8,128)(2,1)}), bf16[16,160,128]{2,1,0:T(8,128)(2,1)S(1)}, u32[]{:S(2)}, u32[]{:S(2)}) async-start(bf16[16,160,128]{2,1,0:T(8,128)(2,1)} %get-tuple-element.35), calls=%async_computation | async-start | bytes 1310720 | tf_op jit(solution)/shard_map/all_to_all | solution.py:561
  33.0 0.8 copy-start.3
  47.6 31.5 %all-to-all-start.1 = ((bf16[16,512,128]{2,1,0:T(8,128)(2,1)}), bf16[16,512,128]{2,1,0:T(8,128)(2,1)S(1)}, u32[]{:S(2)}, u32[]{:S(2)}) async-start(bf16[16,512,128]{2,1,0:T(8,128)(2,1)} %bitcast.34), calls=%async_computation.1 | async-start | bytes 4194304 | tf_op jit(solution)/shard_map/all_to_all | solution.py:569
  79.1 1.3 copy-start.2
  80.4 20.2 %copy-start.5 = (f32[128]{0:T(128)S(1)}, f32[128]{0:T(128)}, u32[]{:S(2)}) copy-start(f32[128]{0:T(128)} %param.24) | copy-start | bytes 1540
  80.5 20.2 %copy-start.4 = (bf16[128,512]{1,0:T(8,128)(2,1)S(1)}, bf16[128,512]{1,0:T(8,128)(2,1)}, u32[]{:S(2)}) copy-start(bf16[128,512]{1,0:T(8,128)(2,1)} %param.25) | copy-start | bytes 393220
  94.2 17.1 %all-to-all-start.2 = ((bf16[16,144,128]{2,1,0:T(8,128)(2,1)}), bf16[16,144,128]{2,1,0:T(8,128)(2,1)S(1)}, u32[]{:S(2)}, u32[]{:S(2)}) async-start(bf16[16,144,128]{2,1,0:T(8,128)(2,1)} %get-tuple-element.48), calls=%async_computation.2 | async-start | bytes 1179648 | tf_op jit(solution)/shard_map/all_to_all | solution.py:572
  100.4 29.1 %all-gather.3.cloned.1.call-start = ((), (), s32[]{:S(2)}) async-start(), calls=%async_computation.4 | async-start | bytes 1253376 | tf_op jit(solution)/shard_map/all_gather | solution.py:568
  111.3 0.8 copy-start.1
  118.8 33.3 %all-to-all-start.3 = ((bf16[8,1024,128]{2,1,0:T(8,128)(2,1)}), bf16[8,1024,128]{2,1,0:T(8,128)(2,1)S(1)}, u32[]{:S(2)}, u32[]{:S(2)}) async-start(bf16[8,1024,128]{2,1,0:T(8,128)(2,1)} %bitcast.32), calls=%async_computation.3 | async-start | bytes 4194304 | tf_op jit(solution)/shard_map/all_to_all | solution.py:575
  152.2 1.2 copy-start
Sparse Core Ops, SparseCore 0:
  102.9 26.4 all-gather.2

commit v4 on v3

--- a/solution.py
+++ b/solution.py
@@ -1,4 +1,4 @@
-import functools
+import math
 
 import jax
 import jax.numpy as jnp
@@ -95,7 +95,9 @@
     cum = mm(pieces(g, 1), thrice(ones(row <= col), 0))
     mid = wide(cum[:, CHUNK // 2 - 1 : CHUNK // 2])
     total = wide(cum[:, CHUNK - 1 : CHUNK])
-    before = mm(thrice(ones((col < row) & ((col & 1) == (row & 1))), 1), pieces(total, 0))
+    same = (col & 1) == (row & 1)
+    before = mm(thrice(ones((col < row) & same), 1), pieces(total, 0))
+    after = mm(thrice(ones((col > row) & same), 1), pieces(total, 0))
     return (
         jnp.exp(mid - cum) * d,
         jnp.exp(cum - mid),
@@ -103,6 +105,7 @@
         jnp.exp(total),
         jnp.exp(total - mid),
         jnp.exp(mid + before),
+        jnp.exp(total - mid + after),
     )
 
 
@@ -178,7 +181,7 @@
         write_tail(msg_ref, state[...], total[0:1, :])
 
 
-def local_scan(u2s, scores, b_ts, cs, slabs, r_slab, mask, state, y_ref):
+def local_scan(u2s, scores, b_ts, cs, slabs, state, finish):
     into, end, add = slabs
     carry = state[...]
     sums = [mm(b_ts[at], u2s[at]) for at in range(PER)]
@@ -187,19 +190,18 @@
         helds.append((carry * row_pair(into, at)).astype(BF16))
         carry = row_pair(end, at) * carry + row_pair(add, at) * sums[at]
     state[...] = carry
-    back = spread(r_slab, mask)
     for at in range(PER):
         left = jnp.concatenate([scores[at], cs[at]], axis=1)
         right = jnp.concatenate([u2s[at], helds[at]], axis=0)
-        y_ref[chunk_rows(at), :] = back[:, chunk_rows(at)] * mm(left, right)
-
-
-def local_x_kernel(g_ref, d_ref, b_ref, c_ref, u_ref, y_ref, r_ref, e_ref, a_all, ends, mask, state):
+        finish(at, mm(left, right))
+
+
+def local_x_kernel(g_ref, d_ref, b_ref, c_ref, u_ref, y_ref, back_ref, e_ref, a_all, r_all, ends, mask, state):
     step = pl.program_id(0)
 
     @pl.when(step == 0)
     def _():
-        a_all[...], r_ref[...], ends[0], ends[1], ends[2], e_ref[...] = scan_factors(g_ref[...], d_ref[...])
+        a_all[...], r_all[...], ends[0], ends[1], ends[2], e_ref[...], _ = scan_factors(g_ref[...], d_ref[...])
         mask[...] = spread_mask()
         state[...] = jnp.zeros_like(state)
 
@@ -212,7 +214,14 @@
     cs = [c_ref[chunk_rows(at), :] for at in range(PER)]
     scores = [jnp.where(lower, mm(cs[at], b_ts[at]), 0.0).astype(BF16) for at in range(PER)]
     slabs = (ends[0, here, :], ends[1, here, :], ends[2, here, :])
-    local_scan(u2s, scores, b_ts, cs, slabs, r_ref[here, :], mask[...], state, y_ref)
+
+    back = spread(r_all[here, :], mask[...])
+
+    def finish(at, value):
+        y_ref[chunk_rows(at), :] = back[:, chunk_rows(at)] * value
+        back_ref[chunk_rows(at), :] = back[:, chunk_rows(at)]
+
+    local_scan(u2s, scores, b_ts, cs, slabs, state, finish)
 
 
 def start_state(got_ref, state):
@@ -227,12 +236,13 @@
             state[...] = decay * state[...] + got_ref[k, 0:CHUNK, :].astype(F32)
 
 
-def add_start(y_ref, c_ref, r_slab, e_slab, mask, state, write):
-    back = spread(r_slab, mask)
+def add_start(y_ref, c_ref, back_ref, e_slab, state, out_ref):
     start = state[...]
     for at in range(PER):
+        rows = chunk_rows(at)
         held = (start * row_pair(e_slab, at)).astype(BF16)
-        write(at, y_ref[chunk_rows(at), :] + back[:, chunk_rows(at)] * mm(c_ref[chunk_rows(at), :], held))
+        value = y_ref[rows, :] + back_ref[rows, :] * mm(c_ref[rows, :], held)
+        out_ref[rows, :] = value.astype(out_ref.dtype)
 
 
 def invert_lists(got_ref, slots):
@@ -265,7 +275,7 @@
 
 
 def send_x_kernel(
-    y_ref, c_ref, r_ref, e_ref, got_ref, out_ref, state, mask, rows, ordered, slots, table, sem
+    y_ref, c_ref, back_ref, e_ref, got_ref, out_ref, state, rows, ordered, slots, table, sem
 ):
     step = pl.program_id(0)
 
@@ -275,18 +285,11 @@
         copy = pltpu.make_async_copy(slots, table, sem)
         copy.start()
         start_state(got_ref, state)
-        mask[...] = spread_mask()
         copy.wait()
 
     @pl.when(step < STEPS)
     def _():
-        here = slab_at(step)
-
-        def write(at, value):
-            rows[chunk_rows(at), :] = value
-
-        add_start(y_ref, c_ref, r_ref[here, :], e_ref[here, :], mask[...], state, write)
-
+        add_start(y_ref, c_ref, back_ref, e_ref[slab_at(step), :], state, rows)
         scatter(rows, table, step * PER, ordered)
 
     @pl.when(step >= STEPS)
@@ -296,62 +299,74 @@
 
 
 def before_z_kernel(
-    g_ref, d_ref, b_ref, c_ref, s_ref, b_t_ref, w_ref, t_ref, a_ref, r_ref, e_ref, ends_ref
+    g_ref, d_ref, b_ref, c_ref, gate_ref,
+    s_ref, b_t_ref, scale_ref, back_ref, t_ref, f_ref, e_ref, ends_ref, a_all, r_all, mask,
 ):
-    @pl.when(pl.program_id(0) == 0)
-    def _():
-        w_ref[...], total = end_weights(g_ref[...], d_ref[...])
+    step = pl.program_id(0)
+
+    @pl.when(step == 0)
+    def _():
+        _, total = end_weights(g_ref[...], d_ref[...])
         t_ref[...] = jnp.broadcast_to(total, (8, LANES))
-        a_ref[...], r_ref[...], ends_ref[0], ends_ref[1], ends_ref[2], e_ref[...] = scan_factors(
+        a_all[...], r_all[...], ends_ref[0], ends_ref[1], ends_ref[2], e_ref[...], f_ref[...] = scan_factors(
             g_ref[...], d_ref[...]
         )
+        mask[...] = spread_mask()
 
     row, col = iotas()
     lower = row >= col
+    here = slab_at(step)
+    scale = spread(a_all[here, :], mask[...])
+    back = spread(r_all[here, :], mask[...])
     for at in range(PER):
-        b_t = b_ref[chunk_rows(at), :].T
-        b_t_ref[:, chunk_rows(at)] = b_t
-        s_ref[chunk_rows(at), :] = jnp.where(lower, mm(c_ref[chunk_rows(at), :], b_t), 0.0).astype(BF16)
-
-
-def states_z_kernel(place, w_ref, t_ref, a_ref, b_t_ref, got_ref, u2_ref, msg_ref, mask, state, rows, ordered):
+        rows = chunk_rows(at)
+        b_t = b_ref[rows, :].T
+        b_t_ref[:, rows] = b_t
+        s_ref[rows, :] = jnp.where(lower, mm(c_ref[rows, :], b_t), 0.0).astype(BF16)
+        scale_ref[rows, :] = scale[:, rows]
+        gate = gate_ref[rows, :].astype(F32)
+        silu = gate * (0.5 * jnp.tanh(0.5 * gate) + 0.5)
+        back_ref[rows, :] = silu * back[:, rows]
+
+
+def states_z_kernel(place, t_ref, f_ref, scale_ref, b_t_ref, got_ref, u2_ref, msg_ref, state, rows, ordered):
     step = pl.program_id(0)
 
     @pl.when(step == 0)
     def _():
-        mask[...] = spread_mask()
         state[...] = jnp.zeros_like(state)
 
     @pl.when(step < STEPS)
     def _():
         rows[...] = got_ref[...].astype(F32)
-
         scatter(rows, place, step * PER, ordered)
 
     @pl.when(step >= STEPS)
     def _():
         base = (step - STEPS) * STEP
-        here = slab_at(step - STEPS)
-        weight = spread(w_ref[here, :], mask[...])
-        scale = spread(a_ref[here, :], mask[...])
-        parts = []
+        factor = f_ref[slab_at(step - STEPS), :]
+        u2s = []
         for at in range(PER):
+            here = chunk_rows(at)
             u = ordered[pl.ds(pl.multiple_of(base + at * CHUNK, CHUNK), CHUNK), :]
-            u2_ref[chunk_rows(at), :] = (u * scale[:, chunk_rows(at)]).astype(BF16)
-            parts.append((u * weight[:, chunk_rows(at)]).astype(BF16))
-        state[...] += mm(b_t_ref[...], jnp.concatenate(parts, axis=0))
+            u2 = (u * scale_ref[here, :]).astype(BF16)
+            u2_ref[here, :] = u2
+            u2s.append(u2)
+        total = state[...]
+        for at in range(PER):
+            total = total + row_pair(factor, at) * mm(b_t_ref[:, chunk_rows(at)], u2s[at])
+        state[...] = total
 
     @pl.when(step == 2 * STEPS - 1)
     def _():
         write_tail(msg_ref, state[...], t_ref[0:1, :])
 
 
-def local_z_kernel(u2_ref, s_ref, b_t_ref, c_ref, r_ref, ends_ref, y_ref, mask, state):
+def local_z_kernel(u2_ref, s_ref, b_t_ref, c_ref, back_ref, ends_ref, y_ref, state):
     step = pl.program_id(0)
 
     @pl.when(step == 0)
     def _():
-        mask[...] = spread_mask()
         state[...] = jnp.zeros_like(state)
 
     here = slab_at(step)
@@ -360,24 +375,21 @@
     b_ts = [b_t_ref[:, chunk_rows(at)] for at in range(PER)]
     cs = [c_ref[chunk_rows(at), :] for at in range(PER)]
     slabs = (ends_ref[0, here, :], ends_ref[1, here, :], ends_ref[2, here, :])
-    local_scan(u2s, scores, b_ts, cs, slabs, r_ref[here, :], mask[...], state, y_ref)
-
-
-def gate_z_kernel(y_ref, c_ref, gate_ref, r_ref, e_ref, got_ref, out_ref, state, mask):
+
+    def finish(at, value):
+        y_ref[chunk_rows(at), :] = back_ref[chunk_rows(at), :] * value
+
+    local_scan(u2s, scores, b_ts, cs, slabs, state, finish)
+
+
+def gate_z_kernel(y_ref, c_ref, back_ref, e_ref, got_ref, out_ref, state):
     step = pl.program_id(0)
 
     @pl.when(step == 0)
     def _():
         start_state(got_ref, state)
-        mask[...] = spread_mask()
-
-    def write(at, value):
-        gate = gate_ref[chunk_rows(at), :].astype(F32)
-        silu = gate * (0.5 * jnp.tanh(0.5 * gate) + 0.5)
-        out_ref[chunk_rows(at), :] = (value.astype(BF16).astype(F32) * silu).astype(BF16)
-
-    here = slab_at(step)
-    add_start(y_ref, c_ref, r_ref[here, :], e_ref[here, :], mask[...], state, write)
+
+    add_start(y_ref, c_ref, back_ref, e_ref[slab_at(step), :], state, out_ref)
 
 
 def final_kernel(x_ref, w_ref, out_ref):
@@ -427,8 +439,12 @@
     return jax.ShapeDtypeStruct(shape, dtype)
 
 
-def call(kernel, name, steps, ins, outs, shapes, scratch, mib, prefetch=0, limit=56):
-    return pl.pallas_call(
+def call(kernel, name, steps, ins, outs, shapes, scratch, mib, prefetch=0, limit=36, loose=-1):
+    large = 1 << 13
+    shapes = jax.tree.map(
+        lambda shape: pltpu.HBM(shape.shape, shape.dtype) if math.prod(shape.shape) >= large else shape, shapes
+    )
+    made = pl.pallas_call(
         kernel,
         name=name,
         grid_spec=pltpu.PrefetchScalarGridSpec(
@@ -441,6 +457,18 @@
         cost_estimate=pl.CostEstimate(flops=mib << 28, bytes_accessed=mib << 20, transcendentals=0),
     )
 
+    def run(*values):
+        return made(
+            *[
+                pltpu.with_memory_space_constraint(value, pltpu.HBM)
+                if at != loose and value.size >= large
+                else value
+                for at, value in enumerate(values)
+            ]
+        )
+
+    return run
+
 
 def states_x(z, g, d, b, u):
     return call(
@@ -455,70 +483,71 @@
     return call(
         local_x_kernel, "local_x", STEPS,
         [fixed(FLAT), fixed(FLAT), block(ROW, each), block(ROW, each), block(ROW, each)],
-        [block(ROW, each), fixed(FLAT), fixed(FLAT)],
-        [struct((TOK, LANES), F32), struct(FLAT, F32), struct(FLAT, F32)],
-        [STATE, pltpu.VMEM(ENDS, F32), MASK, STATE], 10,
+        [block(ROW, each), block(ROW, each), fixed(FLAT)],
+        [struct((TOK, LANES), F32), struct((TOK, LANES), F32), struct(FLAT, F32)],
+        [STATE, STATE, pltpu.VMEM(ENDS, F32), MASK, STATE], 12,
     )(g, d, b, c, u)
 
 
-def send_x(y, c, r, e, got):
+def send_x(y, c, back, e, got):
     return call(
         send_x_kernel, "send_x", 2 * STEPS,
-        [block(ROW, early), block(ROW, early), fixed(FLAT), fixed(FLAT), fixed(GOT_X)],
+        [block(ROW, early), block(ROW, early), block(ROW, early), fixed(FLAT), fixed(GOT_X)],
         block(ROW, late), struct((TOK, LANES), BF16),
         [
-            STATE, MASK, pltpu.VMEM(ROW, F32), pltpu.VMEM((TOK, LANES), F32),
+            STATE, pltpu.VMEM(ROW, F32), pltpu.VMEM((TOK, LANES), F32),
             pltpu.VMEM((64, LANES), jnp.int32), pltpu.SMEM((64, LANES), jnp.int32), pltpu.SemaphoreType.DMA,
-        ], 10,
-    )(y, c, r, e, got)
-
-
-def before_z(g, d, b, c):
+        ], 12, loose=4,
+    )(y, c, back, e, got)
+
+
+def before_z(g, d, b, c, gate):
     return call(
         before_z_kernel, "before_z", STEPS,
-        [fixed(FLAT), fixed(FLAT), block(ROW, each), block(ROW, each)],
+        [fixed(FLAT), fixed(FLAT), block(ROW, each), block(ROW, each), block(ROW, each)],
         [
-            block(ROW, each), block((CHUNK, STEP), lambda i: (0, i)), fixed(FLAT), fixed((8, LANES)),
-            fixed(FLAT), fixed(FLAT), fixed(FLAT), fixed(ENDS),
+            block(ROW, each), block((CHUNK, STEP), lambda i: (0, i)), block(ROW, each), block(ROW, each),
+            fixed((8, LANES)), fixed(FLAT), fixed(FLAT), fixed(ENDS),
         ],
         [
-            struct((TOK, LANES), BF16), struct((CHUNK, TOK), BF16), struct(FLAT, F32), struct((8, LANES), F32),
-            struct(FLAT, F32), struct(FLAT, F32), struct(FLAT, F32), struct(ENDS, F32),
+            struct((TOK, LANES), BF16), struct((CHUNK, TOK), BF16), struct((TOK, LANES), F32),
+            struct((TOK, LANES), F32), struct((8, LANES), F32), struct(FLAT, F32), struct(FLAT, F32),
+            struct(ENDS, F32),
         ],
-        [], 8,
-    )(g, d, b, c)
-
-
-def states_z(place, w, t, a, b_t, got):
+        [STATE, STATE, MASK], 18,
+    )(g, d, b, c, gate)
+
+
+def states_z(place, t, f, scale, b_t, got):
     return call(
         states_z_kernel, "states_z", 2 * STEPS,
         [
-            fixed(FLAT), fixed((8, LANES)), fixed(FLAT),
+            fixed((8, LANES)), fixed(FLAT), block(ROW, late),
             block((CHUNK, STEP), lambda i, _: (0, jnp.maximum(i - STEPS, 0))), block(ROW, early),
         ],
         [block(ROW, late), fixed(GOT_Z)],
         [struct((TOK, LANES), BF16), struct(GOT_Z, BF16)],
-        [MASK, STATE, pltpu.VMEM(ROW, F32), pltpu.VMEM((TOK, LANES), F32)], 8, prefetch=1,
-    )(place, w, t, a, b_t, got)
-
-
-def local_z(u2, s, b_t, c, r, ends):
+        [STATE, pltpu.VMEM(ROW, F32), pltpu.VMEM((TOK, LANES), F32)], 10, prefetch=1, loose=5,
+    )(place, t, f, scale, b_t, got)
+
+
+def local_z(u2, s, b_t, c, back, ends):
     return call(
         local_z_kernel, "local_z", STEPS,
         [
             block(ROW, each), block(ROW, each), block((CHUNK, STEP), lambda i: (0, i)), block(ROW, each),
-            fixed(FLAT), fixed(ENDS),
+            block(ROW, each), fixed(ENDS),
         ],
-        block(ROW, each), struct((TOK, LANES), F32), [MASK, STATE], 10,
-    )(u2, s, b_t, c, r, ends)
-
-
-def gate_z(y, c, gate, r, e, got):
+        block(ROW, each), struct((TOK, LANES), F32), [STATE], 14,
+    )(u2, s, b_t, c, back, ends)
+
+
+def gate_z(y, c, back, e, got):
     return call(
         gate_z_kernel, "gate_z", STEPS,
-        [block(ROW, each), block(ROW, each), block(ROW, each), fixed(FLAT), fixed(FLAT), fixed(GOT_Z)],
-        block(ROW, each), struct((TOK, LANES), BF16), [STATE, MASK], 10,
-    )(y, c, gate, r, e, got)
+        [block(ROW, each), block(ROW, each), block(ROW, each), fixed(FLAT), fixed(GOT_Z)],
+        block(ROW, each), struct((TOK, LANES), BF16), [STATE], 12, loose=4,
+    )(y, c, back, e, got)
 
 
 def final(x, w):
@@ -526,7 +555,7 @@
     return call(
         final_kernel, "final", 1024 // rows,
         [block((8, rows, LANES), lambda i: (0, i, 0)), fixed((8, WROWS, 512))],
-        block((rows, 512), each), struct((1024, 512), BF16), [], 5, limit=20,
+        block((rows, 512), each), struct((1024, 512), BF16), [], 5, limit=20, loose=0,
     )(x, w)
 
 
@@ -559,19 +588,22 @@
     message, place = states_x(z_source.reshape(64, LANES), g_x, d_x, x_in_proj, x_inputs)
     message, g_x, d_x = lax.optimization_barrier((message, g_x, d_x))
     got_x = lax.all_to_all(message, "seq", 0, 0)
-    y_x, r_x, e_x = local_x(g_x, d_x, x_in_proj, x_out_proj, x_inputs)
-    sent = send_x(y_x, x_out_proj, r_x, e_x, got_x)
+    y_x, back_x, e_x = local_x(g_x, d_x, x_in_proj, x_out_proj, x_inputs)
+    sent = send_x(y_x, x_out_proj, back_x, e_x, got_x)
     sent, g_z, d_z, norm_gain, out_weight = lax.optimization_barrier(
         (sent, z_log_decay, z_step, norm_gain, out_weight)
     )
     gain = jnp.pad(jnp.stack(three_pieces(norm_gain)), ((0, WROWS - LANES - 3), (0, 512 - LANES))).astype(BF16)
     weights = lax.all_gather(jnp.concatenate([out_weight, gain], axis=0), "head", axis=0, tiled=False)
     received = lax.all_to_all(sent.reshape(GROUPS, PIECE, LANES), "seq", 0, 0).reshape(TOK, LANES)
-    s_z, b_t, w_z, t_z, a_z, r_z, e_z, ends_z = before_z(flat(g_z), flat(d_z), z_in_proj, z_out_proj)
-    u2_z, tails_z = states_z(place, w_z, t_z, a_z, b_t, received)
+    s_z, b_t, scale_z, back_z, t_z, f_z, e_z, ends_z = before_z(
+        flat(g_z), flat(d_z), z_in_proj, z_out_proj, gate_branch
+    )
+    received, weights = lax.optimization_barrier((received, weights))
+    u2_z, tails_z = states_z(place, t_z, f_z, scale_z, b_t, received)
     got_z = lax.all_to_all(tails_z, "seq", 0, 0)
-    y_z = local_z(u2_z, s_z, b_t, z_out_proj, r_z, ends_z)
-    gated = gate_z(y_z, z_out_proj, gate_branch, r_z, e_z, got_z)
+    y_z = local_z(u2_z, s_z, b_t, z_out_proj, back_z, ends_z)
+    gated = gate_z(y_z, z_out_proj, back_z, e_z, got_z)
     whole = lax.all_to_all(gated.reshape(8, 1024, LANES), "head", 0, 0)
     return final(whole, weights)
 

time: 165 us -> 163 us (0.988)
  blocking collectives: 0 us -> 31.6 us
  waiting for transfers between devices: 55.8 us -> 27.7 us
  starting transfers between devices: 25.8 us -> 19.2 us
  Pallas kernels: 64.4 us -> 69.2 us
  local copies, waits for them, and re-layouts: 4.24 us -> 0.01 us
    all_to_all x0 -> x1, blocking collectives: none -> 31.6 us  [body(): whole = lax.all_to_all(gated.reshape(8, 1024, LANES), 'head', 0, 0)]
    all_to_all x1, waiting for transfers between devices: 22.8 us -> 0.01 us  [body(): lax.all_to_all(sent.reshape(GROUPS, PIECE, LANES), 'seq', 0, 0)]
    all_to_all x1 -> x0, waiting for transfers between devices: 22.7 us -> none  [body(): whole = lax.all_to_all(gated.reshape(8, 1024, LANES), 'head', 0, 0)]
    all_gather x1, waiting for transfers between devices: 3.63 us -> 19.7 us  [body(): lax.all_gather(jnp.concatenate([out_weight, gain], axis=0), 'head', axis=...]
    all_to_all x1 -> x0, starting transfers between devices: 7 us -> none  [body(): whole = lax.all_to_all(gated.reshape(8, 1024, LANES), 'head', 0, 0)]
    pallas_call x8, Pallas kernels: 64.4 us -> 69.2 us  [run(): made(*[pltpu.with_memory_space_constraint(value, pltpu.HBM) if at != loos...]
    unnamed x12 -> x4, local copies, waits for them, and re-layouts: 4.24 us -> 0.01 us
  transfers between devices with their start and end apart: 5 -> 4, of which waited for: 5 -> 3; matrix products, arithmetic and copies ran while one was open for 0% -> 0% of each run, Pallas kernels for 16% -> 15%
where the time goes in v4:
time: 163 us; the launch traced here: 162 us
  Pallas kernels  69.2 us (42%)
  blocking collectives  31.6 us (19%)
  waiting for transfers between devices  27.7 us (17%)
  starting transfers between devices  19.2 us (12%)
  between operations  13.5 us (8%)
    pallas_call x8, Pallas kernels, run(): made(*[pltpu.with_memory_space_constraint(value, pltpu.HBM) if at != loos...  69.2 us
    all_to_all x1, blocking collectives, body(): whole = lax.all_to_all(gated.reshape(8, 1024, LANES), 'head', 0, 0)  31.6 us
    all_gather x1, waiting for transfers between devices, body(): lax.all_gather(jnp.concatenate([out_weight, gain], axis=0), 'head', axis=...  19.7 us
    all_to_all x1, starting transfers between devices, body(): got_x = lax.all_to_all(message, 'seq', 0, 0)  8.42 us
    all_to_all x1, starting transfers between devices, body(): got_z = lax.all_to_all(tails_z, 'seq', 0, 0)  6.67 us
    all_to_all x1, waiting for transfers between devices, body(): got_z = lax.all_to_all(tails_z, 'seq', 0, 0)  4.36 us
    all_to_all x1, starting transfers between devices, body(): lax.all_to_all(sent.reshape(GROUPS, PIECE, LANES), 'seq', 0, 0)  4.09 us
    all_to_all x1, waiting for transfers between devices, body(): got_x = lax.all_to_all(message, 'seq', 0, 0)  3.64 us
  transfers between devices with their start and end apart: 4, of which 3 were waited for; matrix products, arithmetic and copies ran while one was open for 0% of the time, Pallas kernels for 15%

profile of v4, /device:TPU:1, one launch (start us, length us, event | category | flops | bytes accessed | tf_op | source)
XLA Modules:
  0.0 162.0 jit_solution(430369942314833119)
XLA Ops:
  6.5 6.3 %states_x.1 = (bf16[16,160,128]{2,1,0:T(8,128)(2,1)}, s32[64,128]{1,0:T(8,128)}) custom-call(s32[64,128]{1,0:T(8,128)} %bitcast.38, f32[128,128]{1,0:T(8,128)} %bitcast.34, f32[128,128]{1,0:T(8,128)} %bitcast.36, bf16[8192,128]{1,0:T(8,128)(2,1)} %b_ref.4, bf16[8192,128]{1,0:T(8,128)(2,1)} %u_ref.3), custom_call_target="tpu_custom_call" | custom-call | flops 1073741824 | bytes 4194304 | tf_op jit(solution)/shard_map/states_x/pallas_call | solution.py:461
  12.8 8.4 %all-to-all-start = ((bf16[16,160,128]{2,1,0:T(8,128)(2,1)}), bf16[16,160,128]{2,1,0:T(8,128)(2,1)S(1)}, u32[]{:S(2)}, u32[]{:S(2)}) async-start(bf16[16,160,128]{2,1,0:T(8,128)(2,1)} %get-tuple-element.37), calls=%async_computation | async-start | bytes 1310720 | tf_op jit(solution)/shard_map/all_to_all | solution.py:590
  21.2 8.1 %local_x.1 = (f32[8192,128]{1,0:T(8,128)}, f32[8192,128]{1,0:T(8,128)}, f32[128,128]{1,0:T(8,128)}) custom-call(f32[128,128]{1,0:T(8,128)} %bitcast.35, f32[128,128]{1,0:T(8,128)} %bitcast.37, bf16[8192,128]{1,0:T(8,128)(2,1)} %b_ref.4, bf16[8192,128]{1,0:T(8,128)(2,1)} %c_ref.6, bf16[8192,128]{1,0:T(8,128)(2,1)} %u_ref.3), custom_call_target="tpu_custom_call" | custom-call | flops 3221225472 | bytes 12582912 | tf_op jit(solution)/shard_map/local_x/pallas_call | solution.py:461
  29.3 3.6 %all-to-all-done.got_ref = bf16[16,160,128]{2,1,0:T(8,128)(2,1)S(1)} async-done(((bf16[16,160,128]{2,1,0:T(8,128)(2,1)}), bf16[16,160,128]{2,1,0:T(8,128)(2,1)S(1)}, u32[]{:S(2)}, u32[]{:S(2)}) %all-to-all-start) | async-done | bytes 655392 | tf_op jit(solution)/shard_map/all_to_all | solution.py:590
  33.0 0.0 copy-start.1
  33.0 13.8 %send_x.1 = bf16[8192,128]{1,0:T(8,128)(2,1)} custom-call(f32[8192,128]{1,0:T(8,128)} %get-tuple-element.34.y_ref, bf16[8192,128]{1,0:T(8,128)(2,1)} %c_ref.6, f32[8192,128]{1,0:T(8,128)} %get-tuple-element.35.back_ref, f32[128,128]{1,0:T(8,128)} %get-tuple-element.36.e_ref, bf16[16,160,128]{2,1,0:T(8,128)(2,1)S(1)} %all-to-all-done.got_ref), custom_call_target="tpu_custom_call" | custom-call | flops 3221225472 | bytes 12582912 | tf_op jit(solution)/shard_map/send_x/pallas_call | solution.py:461
  46.8 0.0 copy-done.1
  46.8 0.0 copy-start
  46.8 4.1 %all-to-all-start.1 = ((bf16[16,512,128]{2,1,0:T(8,128)(2,1)}), bf16[16,512,128]{2,1,0:T(8,128)(2,1)S(1)}, u32[]{:S(2)}, u32[]{:S(2)}) async-start(bf16[16,512,128]{2,1,0:T(8,128)(2,1)} %bitcast.32), calls=%async_computation.1 | async-start | bytes 4194304 | tf_op jit(solution)/shard_map/all_to_all | solution.py:598
  50.9 0.0 all-gather.3.cloned.1.call-start
  51.0 0.0 copy-done
  51.0 0.7 pad_maximum_fusion
  51.6 0.0 all-gather.3.cloned.1.call-update
  51.7 8.9 %before_z.1 = (bf16[8192,128]{1,0:T(8,128)(2,1)}, bf16[128,8192]{1,0:T(8,128)(2,1)}, f32[8192,128]{1,0:T(8,128)}, f32[8192,128]{1,0:T(8,128)}, f32[8,128]{1,0:T(...) custom-call(f32[128,128]{1,0:T(8,128)} %bitcast.40, f32[128,128]{1,0:T(8,128)} %bitcast.41, ...), custom_call_target="tpu_custom_call" | custom-call | flops 4831838208 | bytes 18874368 | tf_op jit(solution)/shard_map/before_z/pallas_call | solution.py:461
  60.6 19.7 %all-gather.3.cloned.1.call-done = bf16[1088,512]{1,0:T(8,128)(2,1)} async-done(((bf16[136,512]{1,0:T(8,128)(2,1)}), bf16[1088,512]{1,0:T(8,128)(2,1)}) %all-gather.3.cloned.1.call-update) | async-done | bytes 1114128 | tf_op jit(solution)/shard_map/all_gather | solution.py:597
  80.3 0.0 all-to-all-done.1
  80.3 14.1 %states_z.1 = (bf16[8192,128]{1,0:T(8,128)(2,1)}, bf16[16,144,128]{2,1,0:T(8,128)(2,1)}) custom-call(s32[64,128]{1,0:T(8,128)} %get-tuple-element.30.place, f32[8,128]{1,0:T(8,128)S(1)} %get-tuple-element.40.t_ref, f32[128,128]{1,0:T(8,128)} %get-tuple-element.41.f_ref, f32[8192,128]{1,0:T(8,128)} %get-tuple-element.42.scale_ref, ...), custom_call_target="tpu_custom_call" | custom-call | flops 2684354560 | bytes 10485760 | tf_op jit(solution)/shard_map/states_z/pallas_call | solution.py:461
  94.4 6.7 %all-to-all-start.2 = ((bf16[16,144,128]{2,1,0:T(8,128)(2,1)}), bf16[16,144,128]{2,1,0:T(8,128)(2,1)S(1)}, u32[]{:S(2)}, u32[]{:S(2)}) async-start(bf16[16,144,128]{2,1,0:T(8,128)(2,1)} %get-tuple-element.53), calls=%async_computation.2 | async-start | bytes 1179648 | tf_op jit(solution)/shard_map/all_to_all | solution.py:604
  101.1 7.2 %local_z.1.y_ref = f32[8192,128]{1,0:T(8,128)} custom-call(bf16[8192,128]{1,0:T(8,128)(2,1)} %get-tuple-element.48.u2_ref, bf16[8192,128]{1,0:T(8,128)(2,1)} %get-tuple-element.49.s_ref, bf16[128,8192]{1,0:T(8,128)(2,1)} %get-tuple-element.43.b_t_ref, bf16[8192,128]{1,0:T(8,128)(2,1)} %c_ref.9, f32[8192,128]{1,0:T(8,128)} %get-tuple-element.50.back_ref, ...), custom_call_target="tpu_custom_call" | custom-call | flops 3758096384 | bytes 14680064 | tf_op jit(solution)/shard_map/local_z/pallas_call | solution.py:461
  108.3 4.4 %all-to-all-done.2.got_ref = bf16[16,144,128]{2,1,0:T(8,128)(2,1)S(1)} async-done(((bf16[16,144,128]{2,1,0:T(8,128)(2,1)}), bf16[16,144,128]{2,1,0:T(8,128)(2,1)S(1)}, u32[]{:S(2)}, u32[]{:S(2)}) %all-to-all-start.2) | async-done | bytes 589856 | tf_op jit(solution)/shard_map/all_to_all | solution.py:604
  112.6 5.5 %gate_z.1 = bf16[8192,128]{1,0:T(8,128)(2,1)} custom-call(f32[8192,128]{1,0:T(8,128)} %local_z.1.y_ref, bf16[8192,128]{1,0:T(8,128)(2,1)} %c_ref.9, f32[8192,128]{1,0:T(8,128)} %get-tuple-element.50.back_ref, f32[128,128]{1,0:T(8,128)} %get-tuple-element.52.e_ref, bf16[16,144,128]{2,1,0:T(8,128)(2,1)S(1)} %all-to-all-done.2.got_ref), custom_call_target="tpu_custom_call" | custom-call | flops 3221225472 | bytes 12582912 | tf_op jit(solution)/shard_map/gate_z/pallas_call | solution.py:461
  118.2 31.6 %all_to_all.20.x_ref = bf16[8,1024,128]{2,1,0:T(8,128)(2,1)S(1)} all-to-all(bf16[8,1024,128]{2,1,0:T(8,128)(2,1)} %bitcast.33), channel_id=1, replica_groups=mesh['seq'=16,'head'=8] {'head'}, dimensions={0} | all-to-all | bytes 4194304 | tf_op jit(solution)/shard_map/all_to_all | solution.py:607
  149.8 5.4 %final.1 = bf16[1024,512]{1,0:T(8,128)(2,1)} custom-call(bf16[8,1024,128]{2,1,0:T(8,128)(2,1)S(1)} %all_to_all.20.x_ref, bf16[8,136,512]{2,1,0:T(8,128)(2,1)} %bitcast.39), custom_call_target="tpu_custom_call" | custom-call | flops 1342177280 | bytes 5242880 | tf_op jit(solution)/shard_map/final/pallas_call | solution.py:461
  (2 shorter events, 0.0 us)
Async XLA Ops:
  12.8 20.2 %all-to-all-start = ((bf16[16,160,128]{2,1,0:T(8,128)(2,1)}), bf16[16,160,128]{2,1,0:T(8,128)(2,1)S(1)}, u32[]{:S(2)}, u32[]{:S(2)}) async-start(bf16[16,160,128]{2,1,0:T(8,128)(2,1)} %get-tuple-element.37), calls=%async_computation | async-start | bytes 1310720 | tf_op jit(solution)/shard_map/all_to_all | solution.py:590
  33.0 13.8 %copy-start.1 = (f32[128]{0:T(128)S(1)}, f32[128]{0:T(128)}, u32[]{:S(2)}) copy-start(f32[128]{0:T(128)} %param.24) | copy-start | bytes 1540
  46.8 4.2 %copy-start = (bf16[128,512]{1,0:T(8,128)(2,1)S(1)}, bf16[128,512]{1,0:T(8,128)(2,1)}, u32[]{:S(2)}) copy-start(bf16[128,512]{1,0:T(8,128)(2,1)} %param.25) | copy-start | bytes 393220
  46.8 33.5 %all-to-all-start.1 = ((bf16[16,512,128]{2,1,0:T(8,128)(2,1)}), bf16[16,512,128]{2,1,0:T(8,128)(2,1)S(1)}, u32[]{:S(2)}, u32[]{:S(2)}) async-start(bf16[16,512,128]{2,1,0:T(8,128)(2,1)} %bitcast.32), calls=%async_computation.1 | async-start | bytes 4194304 | tf_op jit(solution)/shard_map/all_to_all | solution.py:598
  50.9 29.4 %all-gather.3.cloned.1.call-start = ((), (), s32[]{:S(2)}) async-start(), calls=%async_computation.4 | async-start | bytes 1253376 | tf_op jit(solution)/shard_map/all_gather | solution.py:597
  94.4 18.2 %all-to-all-start.2 = ((bf16[16,144,128]{2,1,0:T(8,128)(2,1)}), bf16[16,144,128]{2,1,0:T(8,128)(2,1)S(1)}, u32[]{:S(2)}, u32[]{:S(2)}) async-start(bf16[16,144,128]{2,1,0:T(8,128)(2,1)} %get-tuple-element.53), calls=%async_computation.2 | async-start | bytes 1179648 | tf_op jit(solution)/shard_map/all_to_all | solution.py:604
Sparse Core Ops, SparseCore 0:
  53.4 26.8 all-gather.2

commit v5 on v4

--- a/solution.py
+++ b/solution.py
@@ -18,6 +18,7 @@
 TAIL = 144
 MSG = 160
 WROWS = 136
+TOGETHER = 16
 F32 = jnp.float32
 BF16 = jnp.bfloat16
 
@@ -137,19 +138,18 @@
         rank = counts[k] + above[:, k * LANES : (k + 1) * LANES] + float(k * PIECE - 1)
         slot = jnp.where(hits[k], rank, slot)
     slot = slot.astype(jnp.int32)
+    place_ref[...] = slot
     slot_high, slot_low = slot >> 7, slot & 127
     token_high, token_low = (token >> 7).astype(F32), (token & 127).astype(F32)
-    lane = lax.broadcasted_iota(jnp.int32, (1, LANES), 1).astype(F32)
-    total = jnp.zeros((256, LANES), F32)
+    total = jnp.zeros((LANES, LANES), F32)
     for base in range(0, 64, 4):
         lefts, rights = [], []
         for q in range(base, base + 4):
             hit = match_rows(slot_high[q : q + 1], 64)
-            values = (token_high[q : q + 1], token_low[q : q + 1], float(q), lane)
+            values = (token_high[q : q + 1], token_low[q : q + 1])
             lefts.append(jnp.concatenate([jnp.where(hit, value, 0.0) for value in values], axis=0).astype(BF16))
             rights.append(ones(match_rows(slot_low[q : q + 1], LANES)))
         total = total + nt(jnp.concatenate(lefts, axis=1), jnp.concatenate(rights, axis=1))
-    place_ref[...] = (total[128:192] * 128.0 + total[192:256]).astype(jnp.int32)
     for k in range(GROUPS):
         rows = slice(4 * k, 4 * k + 4)
         wanted = jnp.concatenate([total[rows], total[64 + 4 * k : 68 + 4 * k], jnp.zeros((8, LANES), F32)], axis=0)
@@ -236,52 +236,33 @@
             state[...] = decay * state[...] + got_ref[k, 0:CHUNK, :].astype(F32)
 
 
-def add_start(y_ref, c_ref, back_ref, e_slab, state, out_ref):
+def add_start(y_ref, c_ref, back_ref, e_slab, state, out_ref, base=0):
     start = state[...]
     for at in range(PER):
         rows = chunk_rows(at)
         held = (start * row_pair(e_slab, at)).astype(BF16)
         value = y_ref[rows, :] + back_ref[rows, :] * mm(c_ref[rows, :], held)
-        out_ref[rows, :] = value.astype(out_ref.dtype)
-
-
-def invert_lists(got_ref, slots):
-    high = lax.broadcasted_iota(jnp.int32, (64, LANES), 0).astype(F32)
-    low = lax.broadcasted_iota(jnp.int32, (LANES, LANES), 0).astype(F32)
-    lane = lax.broadcasted_iota(jnp.int32, (64, LANES), 1).astype(F32)
-    total = jnp.zeros((LANES, LANES), F32)
+        out_ref[pl.ds(pl.multiple_of(base + at * CHUNK, CHUNK), CHUNK), :] = value.astype(out_ref.dtype)
+
+
+def read_lists(got_ref, slots):
     for k in range(GROUPS):
         lists = got_ref[k, TAIL:MSG, :].astype(F32)
-        lefts, rights = [], []
-        for q in range(4):
-            hit = high == lists[q : q + 1]
-            lefts.append(
-                jnp.concatenate([jnp.where(hit, float(4 * k + q), 0.0), jnp.where(hit, lane, 0.0)], axis=0).astype(BF16)
-            )
-            rights.append(ones(low == lists[4 + q : 5 + q]))
-        total = total + nt(jnp.concatenate(lefts, axis=1), jnp.concatenate(rights, axis=1))
-    slots[...] = (total[0:64] * 128.0 + total[64:128]).astype(jnp.int32)
-
-
-def scatter(rows, table, line, ordered):
-    def put(i, _):
-        for q in range(LANES // 8):
-            value = rows[pl.ds(pl.multiple_of(i * LANES + q * 8, 8), 8), :]
-            for k in range(8):
-                ordered[pl.ds(table[line + i, q * 8 + k], 1), :] = value[k : k + 1, :]
-        return 0
-
-    lax.fori_loop(0, PER, put, 0)
+        slots[4 * k : 4 * k + 4, :] = (lists[0:4] * 128.0 + lists[4:8]).astype(jnp.int32)
+
+
+def take_rows(source, table, line, first, count):
+    return jnp.concatenate([source[pl.ds(table[line, first + k], 1), :] for k in range(count)], axis=0)
 
 
 def send_x_kernel(
-    y_ref, c_ref, back_ref, e_ref, got_ref, out_ref, state, rows, ordered, slots, table, sem
+    y_ref, c_ref, back_ref, e_ref, got_ref, out_ref, state, rows, slots, table, sem
 ):
     step = pl.program_id(0)
 
     @pl.when(step == 0)
     def _():
-        invert_lists(got_ref, slots)
+        read_lists(got_ref, slots)
         copy = pltpu.make_async_copy(slots, table, sem)
         copy.start()
         start_state(got_ref, state)
@@ -289,13 +270,18 @@
 
     @pl.when(step < STEPS)
     def _():
-        add_start(y_ref, c_ref, back_ref, e_ref[slab_at(step), :], state, rows)
-        scatter(rows, table, step * PER, ordered)
+        base = step * STEP
+        add_start(y_ref, c_ref, back_ref, e_ref[slab_at(step), :], state, rows, base)
 
     @pl.when(step >= STEPS)
     def _():
-        base = pl.multiple_of((step - STEPS) * STEP, STEP)
-        out_ref[...] = ordered[pl.ds(base, STEP), :].astype(BF16)
+        def take(i, _):
+            for q in range(LANES // 16):
+                here = pl.ds(pl.multiple_of(i * LANES + q * 16, 16), 16)
+                out_ref[here, :] = take_rows(rows, table, (step - STEPS) * PER + i, q * 16, 16).astype(BF16)
+            return 0
+
+        lax.fori_loop(0, PER, take, 0)
 
 
 def before_z_kernel(
@@ -329,7 +315,7 @@
         back_ref[rows, :] = silu * back[:, rows]
 
 
-def states_z_kernel(place, t_ref, f_ref, scale_ref, b_t_ref, got_ref, u2_ref, msg_ref, state, rows, ordered):
+def states_z_kernel(place, t_ref, f_ref, scale_ref, b_t_ref, got_ref, u2_ref, msg_ref, state, rows):
     step = pl.program_id(0)
 
     @pl.when(step == 0)
@@ -338,24 +324,25 @@
 
     @pl.when(step < STEPS)
     def _():
-        rows[...] = got_ref[...].astype(F32)
-        scatter(rows, place, step * PER, ordered)
+        rows[pl.ds(pl.multiple_of(step * STEP, STEP), STEP), :] = got_ref[...].astype(F32)
 
     @pl.when(step >= STEPS)
     def _():
-        base = (step - STEPS) * STEP
-        factor = f_ref[slab_at(step - STEPS), :]
-        u2s = []
-        for at in range(PER):
-            here = chunk_rows(at)
-            u = ordered[pl.ds(pl.multiple_of(base + at * CHUNK, CHUNK), CHUNK), :]
-            u2 = (u * scale_ref[here, :]).astype(BF16)
-            u2_ref[here, :] = u2
-            u2s.append(u2)
-        total = state[...]
-        for at in range(PER):
-            total = total + row_pair(factor, at) * mm(b_t_ref[:, chunk_rows(at)], u2s[at])
-        state[...] = total
+        block_at = step - STEPS
+
+        def one(i, total):
+            for at in range(TOGETHER):
+                chunk = i * TOGETHER + at
+                here = pl.ds(pl.multiple_of(chunk * CHUNK, CHUNK), CHUNK)
+                line = block_at * PER + chunk
+                u = take_rows(rows, place, line, 0, CHUNK)
+                u2 = (u * scale_ref[here, :]).astype(BF16)
+                u2_ref[here, :] = u2
+                factor = by_head(f_ref[pl.ds(2 * line, 1), :], f_ref[pl.ds(2 * line + 1, 1), :])
+                total = total + factor * mm(b_t_ref[:, here], u2)
+            return total
+
+        state[...] = lax.fori_loop(0, PER // TOGETHER, one, state[...])
 
     @pl.when(step == 2 * STEPS - 1)
     def _():
@@ -495,7 +482,7 @@
         [block(ROW, early), block(ROW, early), block(ROW, early), fixed(FLAT), fixed(GOT_X)],
         block(ROW, late), struct((TOK, LANES), BF16),
         [
-            STATE, pltpu.VMEM(ROW, F32), pltpu.VMEM((TOK, LANES), F32),
+            STATE, pltpu.VMEM((TOK, LANES), F32),
             pltpu.VMEM((64, LANES), jnp.int32), pltpu.SMEM((64, LANES), jnp.int32), pltpu.SemaphoreType.DMA,
         ], 12, loose=4,
     )(y, c, back, e, got)
@@ -527,7 +514,7 @@
         ],
         [block(ROW, late), fixed(GOT_Z)],
         [struct((TOK, LANES), BF16), struct(GOT_Z, BF16)],
-        [STATE, pltpu.VMEM(ROW, F32), pltpu.VMEM((TOK, LANES), F32)], 10, prefetch=1, loose=5,
+        [STATE, pltpu.VMEM((TOK, LANES), F32)], 10, prefetch=1, loose=5,
     )(place, t, f, scale, b_t, got)
 
 
@@ -551,7 +538,7 @@
 
 
 def final(x, w):
-    rows = 256
+    rows = 1024
     return call(
         final_kernel, "final", 1024 // rows,
         [block((8, rows, LANES), lambda i: (0, i, 0)), fixed((8, WROWS, 512))],

time: 163 us -> 159 us (0.975)
  Pallas kernels: 69.2 us -> 65.9 us
    pallas_call x8, Pallas kernels: 69.2 us -> 65.9 us  [run(): made(*[pltpu.with_memory_space_constraint(value, pltpu.HBM) if at != loos...]
where the time goes in v5:
time: 159 us
  Pallas kernels  65.9 us (41%)
  blocking collectives  31.6 us (20%)
  waiting for transfers between devices  27.7 us (17%)
  starting transfers between devices  19.2 us (12%)
  between operations  13.5 us (8%)
    pallas_call x8, Pallas kernels, run(): made(*[pltpu.with_memory_space_constraint(value, pltpu.HBM) if at != loos...  65.9 us
    all_to_all x1, blocking collectives, body(): whole = lax.all_to_all(gated.reshape(8, 1024, LANES), 'head', 0, 0)  31.6 us
    all_gather x1, waiting for transfers between devices, body(): lax.all_gather(jnp.concatenate([out_weight, gain], axis=0), 'head', axis=...  19.7 us
    all_to_all x1, starting transfers between devices, body(): got_x = lax.all_to_all(message, 'seq', 0, 0)  8.43 us
    all_to_all x1, starting transfers between devices, body(): got_z = lax.all_to_all(tails_z, 'seq', 0, 0)  6.67 us
    all_to_all x1, waiting for transfers between devices, body(): got_z = lax.all_to_all(tails_z, 'seq', 0, 0)  4.37 us
    all_to_all x1, starting transfers between devices, body(): lax.all_to_all(sent.reshape(GROUPS, PIECE, LANES), 'seq', 0, 0)  4.1 us
    all_to_all x1, waiting for transfers between devices, body(): got_x = lax.all_to_all(message, 'seq', 0, 0)  3.65 us
  transfers between devices with their start and end apart: 4, of which 3 were waited for; matrix products, arithmetic and copies ran while one was open for 0% of the time, Pallas kernels for 15%

profile of v5, /device:TPU:1, one launch (start us, length us, event | category | flops | bytes accessed | tf_op | source)
XLA Modules:
  0.0 158.7 jit_solution(18228066503727720603)
XLA Ops:
  6.5 5.8 %states_x.1 = (bf16[16,160,128]{2,1,0:T(8,128)(2,1)}, s32[64,128]{1,0:T(8,128)}) custom-call(s32[64,128]{1,0:T(8,128)} %bitcast.38, f32[128,128]{1,0:T(8,128)} %bitcast.34, f32[128,128]{1,0:T(8,128)} %bitcast.36, bf16[8192,128]{1,0:T(8,128)(2,1)} %b_ref.4, bf16[8192,128]{1,0:T(8,128)(2,1)} %u_ref.3), custom_call_target="tpu_custom_call" | custom-call | flops 1073741824 | bytes 4194304 | tf_op jit(solution)/shard_map/states_x/pallas_call | solution.py:448
  12.3 8.4 %all-to-all-start = ((bf16[16,160,128]{2,1,0:T(8,128)(2,1)}), bf16[16,160,128]{2,1,0:T(8,128)(2,1)S(1)}, u32[]{:S(2)}, u32[]{:S(2)}) async-start(bf16[16,160,128]{2,1,0:T(8,128)(2,1)} %get-tuple-element.37), calls=%async_computation | async-start | bytes 1310720 | tf_op jit(solution)/shard_map/all_to_all | solution.py:577
  20.8 8.1 %local_x.1 = (f32[8192,128]{1,0:T(8,128)}, f32[8192,128]{1,0:T(8,128)}, f32[128,128]{1,0:T(8,128)}) custom-call(f32[128,128]{1,0:T(8,128)} %bitcast.35, f32[128,128]{1,0:T(8,128)} %bitcast.37, bf16[8192,128]{1,0:T(8,128)(2,1)} %b_ref.4, bf16[8192,128]{1,0:T(8,128)(2,1)} %c_ref.6, bf16[8192,128]{1,0:T(8,128)(2,1)} %u_ref.3), custom_call_target="tpu_custom_call" | custom-call | flops 3221225472 | bytes 12582912 | tf_op jit(solution)/shard_map/local_x/pallas_call | solution.py:448
  28.9 3.7 %all-to-all-done.got_ref = bf16[16,160,128]{2,1,0:T(8,128)(2,1)S(1)} async-done(((bf16[16,160,128]{2,1,0:T(8,128)(2,1)}), bf16[16,160,128]{2,1,0:T(8,128)(2,1)S(1)}, u32[]{:S(2)}, u32[]{:S(2)}) %all-to-all-start) | async-done | bytes 655392 | tf_op jit(solution)/shard_map/all_to_all | solution.py:577
  32.5 0.0 copy-start.1
  32.5 13.2 %send_x.1 = bf16[8192,128]{1,0:T(8,128)(2,1)} custom-call(f32[8192,128]{1,0:T(8,128)} %get-tuple-element.34.y_ref, bf16[8192,128]{1,0:T(8,128)(2,1)} %c_ref.6, f32[8192,128]{1,0:T(8,128)} %get-tuple-element.35.back_ref, f32[128,128]{1,0:T(8,128)} %get-tuple-element.36.e_ref, bf16[16,160,128]{2,1,0:T(8,128)(2,1)S(1)} %all-to-all-done.got_ref), custom_call_target="tpu_custom_call" | custom-call | flops 3221225472 | bytes 12582912 | tf_op jit(solution)/shard_map/send_x/pallas_call | solution.py:448
  45.8 0.0 copy-done.1
  45.8 0.0 copy-start
  45.8 4.1 %all-to-all-start.1 = ((bf16[16,512,128]{2,1,0:T(8,128)(2,1)}), bf16[16,512,128]{2,1,0:T(8,128)(2,1)S(1)}, u32[]{:S(2)}, u32[]{:S(2)}) async-start(bf16[16,512,128]{2,1,0:T(8,128)(2,1)} %bitcast.32), calls=%async_computation.1 | async-start | bytes 4194304 | tf_op jit(solution)/shard_map/all_to_all | solution.py:585
  49.9 0.0 all-gather.3.cloned.1.call-start
  50.0 0.0 copy-done
  50.0 0.7 pad_maximum_fusion
  50.7 0.0 all-gather.3.cloned.1.call-update
  50.7 9.0 %before_z.1 = (bf16[8192,128]{1,0:T(8,128)(2,1)}, bf16[128,8192]{1,0:T(8,128)(2,1)}, f32[8192,128]{1,0:T(8,128)}, f32[8192,128]{1,0:T(8,128)}, f32[8,128]{1,0:T(...) custom-call(f32[128,128]{1,0:T(8,128)} %bitcast.40, f32[128,128]{1,0:T(8,128)} %bitcast.41, ...), custom_call_target="tpu_custom_call" | custom-call | flops 4831838208 | bytes 18874368 | tf_op jit(solution)/shard_map/before_z/pallas_call | solution.py:448
  59.7 19.7 %all-gather.3.cloned.1.call-done = bf16[1088,512]{1,0:T(8,128)(2,1)} async-done(((bf16[136,512]{1,0:T(8,128)(2,1)}), bf16[1088,512]{1,0:T(8,128)(2,1)}) %all-gather.3.cloned.1.call-update) | async-done | bytes 1114128 | tf_op jit(solution)/shard_map/all_gather | solution.py:584
  79.3 0.0 all-to-all-done.1
  79.3 12.3 %states_z.1 = (bf16[8192,128]{1,0:T(8,128)(2,1)}, bf16[16,144,128]{2,1,0:T(8,128)(2,1)}) custom-call(s32[64,128]{1,0:T(8,128)} %get-tuple-element.30.place, f32[8,128]{1,0:T(8,128)S(1)} %get-tuple-element.40.t_ref, f32[128,128]{1,0:T(8,128)} %get-tuple-element.41.f_ref, f32[8192,128]{1,0:T(8,128)} %get-tuple-element.42.scale_ref, ...), custom_call_target="tpu_custom_call" | custom-call | flops 2684354560 | bytes 10485760 | tf_op jit(solution)/shard_map/states_z/pallas_call | solution.py:448
  91.7 6.7 %all-to-all-start.2 = ((bf16[16,144,128]{2,1,0:T(8,128)(2,1)}), bf16[16,144,128]{2,1,0:T(8,128)(2,1)S(1)}, u32[]{:S(2)}, u32[]{:S(2)}) async-start(bf16[16,144,128]{2,1,0:T(8,128)(2,1)} %get-tuple-element.53), calls=%async_computation.2 | async-start | bytes 1179648 | tf_op jit(solution)/shard_map/all_to_all | solution.py:591
  98.3 7.2 %local_z.1.y_ref = f32[8192,128]{1,0:T(8,128)} custom-call(bf16[8192,128]{1,0:T(8,128)(2,1)} %get-tuple-element.48.u2_ref, bf16[8192,128]{1,0:T(8,128)(2,1)} %get-tuple-element.49.s_ref, bf16[128,8192]{1,0:T(8,128)(2,1)} %get-tuple-element.43.b_t_ref, bf16[8192,128]{1,0:T(8,128)(2,1)} %c_ref.9, f32[8192,128]{1,0:T(8,128)} %get-tuple-element.50.back_ref, ...), custom_call_target="tpu_custom_call" | custom-call | flops 3758096384 | bytes 14680064 | tf_op jit(solution)/shard_map/local_z/pallas_call | solution.py:448
  105.5 4.4 %all-to-all-done.2.got_ref = bf16[16,144,128]{2,1,0:T(8,128)(2,1)S(1)} async-done(((bf16[16,144,128]{2,1,0:T(8,128)(2,1)}), bf16[16,144,128]{2,1,0:T(8,128)(2,1)S(1)}, u32[]{:S(2)}, u32[]{:S(2)}) %all-to-all-start.2) | async-done | bytes 589856 | tf_op jit(solution)/shard_map/all_to_all | solution.py:591
  109.9 5.5 %gate_z.1 = bf16[8192,128]{1,0:T(8,128)(2,1)} custom-call(f32[8192,128]{1,0:T(8,128)} %local_z.1.y_ref, bf16[8192,128]{1,0:T(8,128)(2,1)} %c_ref.9, f32[8192,128]{1,0:T(8,128)} %get-tuple-element.50.back_ref, f32[128,128]{1,0:T(8,128)} %get-tuple-element.52.e_ref, bf16[16,144,128]{2,1,0:T(8,128)(2,1)S(1)} %all-to-all-done.2.got_ref), custom_call_target="tpu_custom_call" | custom-call | flops 3221225472 | bytes 12582912 | tf_op jit(solution)/shard_map/gate_z/pallas_call | solution.py:448
  115.4 31.6 %all_to_all.20.x_ref = bf16[8,1024,128]{2,1,0:T(8,128)(2,1)S(1)} all-to-all(bf16[8,1024,128]{2,1,0:T(8,128)(2,1)} %bitcast.33), channel_id=1, replica_groups=mesh['seq'=16,'head'=8] {'head'}, dimensions={0} | all-to-all | bytes 4194304 | tf_op jit(solution)/shard_map/all_to_all | solution.py:594
  147.0 4.8 %final.1 = bf16[1024,512]{1,0:T(8,128)(2,1)} custom-call(bf16[8,1024,128]{2,1,0:T(8,128)(2,1)S(1)} %all_to_all.20.x_ref, bf16[8,136,512]{2,1,0:T(8,128)(2,1)} %bitcast.39), custom_call_target="tpu_custom_call" | custom-call | flops 1342177280 | bytes 5242880 | tf_op jit(solution)/shard_map/final/pallas_call | solution.py:448
  (2 shorter events, 0.0 us)
Async XLA Ops:
  12.3 20.2 %all-to-all-start = ((bf16[16,160,128]{2,1,0:T(8,128)(2,1)}), bf16[16,160,128]{2,1,0:T(8,128)(2,1)S(1)}, u32[]{:S(2)}, u32[]{:S(2)}) async-start(bf16[16,160,128]{2,1,0:T(8,128)(2,1)} %get-tuple-element.37), calls=%async_computation | async-start | bytes 1310720 | tf_op jit(solution)/shard_map/all_to_all | solution.py:577
  32.5 13.3 %copy-start.1 = (f32[128]{0:T(128)S(1)}, f32[128]{0:T(128)}, u32[]{:S(2)}) copy-start(f32[128]{0:T(128)} %param.24) | copy-start | bytes 1540
  45.8 4.2 %copy-start = (bf16[128,512]{1,0:T(8,128)(2,1)S(1)}, bf16[128,512]{1,0:T(8,128)(2,1)}, u32[]{:S(2)}) copy-start(bf16[128,512]{1,0:T(8,128)(2,1)} %param.25) | copy-start | bytes 393220
  45.8 33.5 %all-to-all-start.1 = ((bf16[16,512,128]{2,1,0:T(8,128)(2,1)}), bf16[16,512,128]{2,1,0:T(8,128)(2,1)S(1)}, u32[]{:S(2)}, u32[]{:S(2)}) async-start(bf16[16,512,128]{2,1,0:T(8,128)(2,1)} %bitcast.32), calls=%async_computation.1 | async-start | bytes 4194304 | tf_op jit(solution)/shard_map/all_to_all | solution.py:585
  49.9 29.4 %all-gather.3.cloned.1.call-start = ((), (), s32[]{:S(2)}) async-start(), calls=%async_computation.4 | async-start | bytes 1253376 | tf_op jit(solution)/shard_map/all_gather | solution.py:584
  91.7 18.2 %all-to-all-start.2 = ((bf16[16,144,128]{2,1,0:T(8,128)(2,1)}), bf16[16,144,128]{2,1,0:T(8,128)(2,1)S(1)}, u32[]{:S(2)}, u32[]{:S(2)}) async-start(bf16[16,144,128]{2,1,0:T(8,128)(2,1)} %get-tuple-element.53), calls=%async_computation.2 | async-start | bytes 1179648 | tf_op jit(solution)/shard_map/all_to_all | solution.py:591
Sparse Core Ops, SparseCore 0:
  52.4 26.8 all-gather.2

commit v6 on v5

--- a/solution.py
+++ b/solution.py
@@ -18,7 +18,8 @@
 TAIL = 144
 MSG = 160
 WROWS = 136
-TOGETHER = 16
+TOGETHER = 32
+LINES = 2
 F32 = jnp.float32
 BF16 = jnp.bfloat16
 
@@ -218,7 +219,7 @@
     back = spread(r_all[here, :], mask[...])
 
     def finish(at, value):
-        y_ref[chunk_rows(at), :] = back[:, chunk_rows(at)] * value
+        y_ref[chunk_rows(at), :] = (back[:, chunk_rows(at)] * value).astype(BF16)
         back_ref[chunk_rows(at), :] = back[:, chunk_rows(at)]
 
     local_scan(u2s, scores, b_ts, cs, slabs, state, finish)
@@ -241,7 +242,7 @@
     for at in range(PER):
         rows = chunk_rows(at)
         held = (start * row_pair(e_slab, at)).astype(BF16)
-        value = y_ref[rows, :] + back_ref[rows, :] * mm(c_ref[rows, :], held)
+        value = y_ref[rows, :].astype(F32) + back_ref[rows, :] * mm(c_ref[rows, :], held)
         out_ref[pl.ds(pl.multiple_of(base + at * CHUNK, CHUNK), CHUNK), :] = value.astype(out_ref.dtype)
 
 
@@ -263,25 +264,29 @@
     @pl.when(step == 0)
     def _():
         read_lists(got_ref, slots)
-        copy = pltpu.make_async_copy(slots, table, sem)
-        copy.start()
+        pltpu.make_async_copy(slots, table, sem).start()
         start_state(got_ref, state)
-        copy.wait()
 
     @pl.when(step < STEPS)
     def _():
         base = step * STEP
         add_start(y_ref, c_ref, back_ref, e_ref[slab_at(step), :], state, rows, base)
 
+    @pl.when(step == 0)
+    def _():
+        pltpu.make_async_copy(slots, table, sem).wait()
+
     @pl.when(step >= STEPS)
     def _():
         def take(i, _):
-            for q in range(LANES // 16):
-                here = pl.ds(pl.multiple_of(i * LANES + q * 16, 16), 16)
-                out_ref[here, :] = take_rows(rows, table, (step - STEPS) * PER + i, q * 16, 16).astype(BF16)
+            for at in range(LINES):
+                line = i * LINES + at
+                for q in range(LANES // 16):
+                    here = pl.ds(pl.multiple_of(line * LANES + q * 16, 16), 16)
+                    out_ref[here, :] = take_rows(rows, table, (step - STEPS) * PER + line, q * 16, 16).astype(BF16)
             return 0
 
-        lax.fori_loop(0, PER, take, 0)
+        lax.fori_loop(0, PER // LINES, take, 0)
 
 
 def before_z_kernel(
@@ -315,16 +320,23 @@
         back_ref[rows, :] = silu * back[:, rows]
 
 
-def states_z_kernel(place, t_ref, f_ref, scale_ref, b_t_ref, got_ref, u2_ref, msg_ref, state, rows):
+def states_z_kernel(
+    place_ref, t_ref, f_ref, scale_ref, b_t_ref, got_ref, u2_ref, msg_ref, state, rows, place, sem
+):
     step = pl.program_id(0)
 
     @pl.when(step == 0)
     def _():
+        pltpu.make_async_copy(place_ref, place, sem).start()
         state[...] = jnp.zeros_like(state)
 
     @pl.when(step < STEPS)
     def _():
         rows[pl.ds(pl.multiple_of(step * STEP, STEP), STEP), :] = got_ref[...].astype(F32)
+
+    @pl.when(step == 0)
+    def _():
+        pltpu.make_async_copy(place_ref, place, sem).wait()
 
     @pl.when(step >= STEPS)
     def _():
@@ -364,7 +376,7 @@
     slabs = (ends_ref[0, here, :], ends_ref[1, here, :], ends_ref[2, here, :])
 
     def finish(at, value):
-        y_ref[chunk_rows(at), :] = back_ref[chunk_rows(at), :] * value
+        y_ref[chunk_rows(at), :] = (back_ref[chunk_rows(at), :] * value).astype(BF16)
 
     local_scan(u2s, scores, b_ts, cs, slabs, state, finish)
 
@@ -471,7 +483,7 @@
         local_x_kernel, "local_x", STEPS,
         [fixed(FLAT), fixed(FLAT), block(ROW, each), block(ROW, each), block(ROW, each)],
         [block(ROW, each), block(ROW, each), fixed(FLAT)],
-        [struct((TOK, LANES), F32), struct((TOK, LANES), F32), struct(FLAT, F32)],
+        [struct((TOK, LANES), BF16), struct((TOK, LANES), F32), struct(FLAT, F32)],
         [STATE, STATE, pltpu.VMEM(ENDS, F32), MASK, STATE], 12,
     )(g, d, b, c, u)
 
@@ -509,12 +521,14 @@
     return call(
         states_z_kernel, "states_z", 2 * STEPS,
         [
-            fixed((8, LANES)), fixed(FLAT), block(ROW, late),
-            block((CHUNK, STEP), lambda i, _: (0, jnp.maximum(i - STEPS, 0))), block(ROW, early),
+            fixed((64, LANES)), fixed((8, LANES)), fixed(FLAT), block(ROW, late),
+            block((CHUNK, STEP), lambda i: (0, jnp.maximum(i - STEPS, 0))), block(ROW, early),
         ],
         [block(ROW, late), fixed(GOT_Z)],
         [struct((TOK, LANES), BF16), struct(GOT_Z, BF16)],
-        [STATE, pltpu.VMEM((TOK, LANES), F32)], 10, prefetch=1, loose=5,
+        [
+            STATE, pltpu.VMEM((TOK, LANES), F32), pltpu.SMEM((64, LANES), jnp.int32), pltpu.SemaphoreType.DMA,
+        ], 10, loose=5,
     )(place, t, f, scale, b_t, got)
 
 
@@ -525,7 +539,7 @@
             block(ROW, each), block(ROW, each), block((CHUNK, STEP), lambda i: (0, i)), block(ROW, each),
             block(ROW, each), fixed(ENDS),
         ],
-        block(ROW, each), struct((TOK, LANES), F32), [STATE], 14,
+        block(ROW, each), struct((TOK, LANES), BF16), [STATE], 14,
     )(u2, s, b_t, c, back, ends)
 
 

time: 159 us -> 157 us (0.987)
  Pallas kernels: 65.9 us -> 62.9 us
    pallas_call x8, Pallas kernels: 65.9 us -> 62.9 us  [run(): made(*[pltpu.with_memory_space_constraint(value, pltpu.HBM) if at != loos...]
where the time goes in v6:
time: 157 us; the launch traced here: 156 us
  Pallas kernels  62.9 us (40%)
  blocking collectives  31.6 us (20%)
  waiting for transfers between devices  28.2 us (18%)
  starting transfers between devices  19.4 us (12%)
  between operations  13.5 us (9%)
    pallas_call x8, Pallas kernels, run(): made(*[pltpu.with_memory_space_constraint(value, pltpu.HBM) if at != loos...  62.9 us
    all_to_all x1, blocking collectives, body(): whole = lax.all_to_all(gated.reshape(8, 1024, LANES), 'head', 0, 0)  31.6 us
    all_gather x1, waiting for transfers between devices, body(): lax.all_gather(jnp.concatenate([out_weight, gain], axis=0), 'head', axis=...  19.5 us
    all_to_all x1, starting transfers between devices, body(): got_x = lax.all_to_all(message, 'seq', 0, 0)  8.43 us
    all_to_all x1, starting transfers between devices, body(): got_z = lax.all_to_all(tails_z, 'seq', 0, 0)  6.67 us
    all_to_all x1, waiting for transfers between devices, body(): got_z = lax.all_to_all(tails_z, 'seq', 0, 0)  4.7 us
    all_to_all x1, starting transfers between devices, body(): lax.all_to_all(sent.reshape(GROUPS, PIECE, LANES), 'seq', 0, 0)  4.1 us
    all_to_all x1, waiting for transfers between devices, body(): got_x = lax.all_to_all(message, 'seq', 0, 0)  3.97 us
  transfers between devices with their start and end apart: 4, of which 3 were waited for; matrix products, arithmetic and copies ran while one was open for 0% of the time, Pallas kernels for 15%

profile of v6, /device:TPU:1, one launch (start us, length us, event | category | flops | bytes accessed | tf_op | source)
XLA Modules:
  0.0 156.3 jit_solution(18372891436254886350)
XLA Ops:
  6.5 5.8 %states_x.1 = (bf16[16,160,128]{2,1,0:T(8,128)(2,1)}, s32[64,128]{1,0:T(8,128)}) custom-call(s32[64,128]{1,0:T(8,128)} %bitcast.38, f32[128,128]{1,0:T(8,128)} %bitcast.34, f32[128,128]{1,0:T(8,128)} %bitcast.36, bf16[8192,128]{1,0:T(8,128)(2,1)} %b_ref.4, bf16[8192,128]{1,0:T(8,128)(2,1)} %u_ref.3), custom_call_target="tpu_custom_call" | custom-call | flops 1073741824 | bytes 4194304 | tf_op jit(solution)/shard_map/states_x/pallas_call | solution.py:460
  12.3 8.4 %all-to-all-start = ((bf16[16,160,128]{2,1,0:T(8,128)(2,1)}), bf16[16,160,128]{2,1,0:T(8,128)(2,1)S(1)}, u32[]{:S(2)}, u32[]{:S(2)}) async-start(bf16[16,160,128]{2,1,0:T(8,128)(2,1)} %get-tuple-element.37), calls=%async_computation | async-start | bytes 1310720 | tf_op jit(solution)/shard_map/all_to_all | solution.py:591
  20.8 7.8 %local_x.1 = (bf16[8192,128]{1,0:T(8,128)(2,1)}, f32[8192,128]{1,0:T(8,128)}, f32[128,128]{1,0:T(8,128)}) custom-call(f32[128,128]{1,0:T(8,128)} %bitcast.35, f32[128,128]{1,0:T(8,128)} %bitcast.37, bf16[8192,128]{1,0:T(8,128)(2,1)} %b_ref.4, bf16[8192,128]{1,0:T(8,128)(2,1)} %c_ref.6, bf16[8192,128]{1,0:T(8,128)(2,1)} %u_ref.3), custom_call_target="tpu_custom_call" | custom-call | flops 3221225472 | bytes 12582912 | tf_op jit(solution)/shard_map/local_x/pallas_call | solution.py:460
  28.6 4.0 %all-to-all-done.got_ref = bf16[16,160,128]{2,1,0:T(8,128)(2,1)S(1)} async-done(((bf16[16,160,128]{2,1,0:T(8,128)(2,1)}), bf16[16,160,128]{2,1,0:T(8,128)(2,1)S(1)}, u32[]{:S(2)}, u32[]{:S(2)}) %all-to-all-start) | async-done | bytes 655392 | tf_op jit(solution)/shard_map/all_to_all | solution.py:591
  32.5 0.0 copy-start.1
  32.5 12.4 %send_x.1 = bf16[8192,128]{1,0:T(8,128)(2,1)} custom-call(bf16[8192,128]{1,0:T(8,128)(2,1)} %get-tuple-element.34.y_ref, bf16[8192,128]{1,0:T(8,128)(2,1)} %c_ref.6, f32[8192,128]{1,0:T(8,128)} %get-tuple-element.35.back_ref, f32[128,128]{1,0:T(8,128)} %get-tuple-element.36.e_ref, bf16[16,160,128]{2,1,0:T(8,128)(2,1)S(1)} %all-to-all-done.got_ref), custom_call_target="tpu_custom_call" | custom-call | flops 3221225472 | bytes 12582912 | tf_op jit(solution)/shard_map/send_x/pallas_call | solution.py:460
  44.9 0.0 copy-done.1
  44.9 0.0 copy-start
  44.9 4.1 %all-to-all-start.1 = ((bf16[16,512,128]{2,1,0:T(8,128)(2,1)}), bf16[16,512,128]{2,1,0:T(8,128)(2,1)S(1)}, u32[]{:S(2)}, u32[]{:S(2)}) async-start(bf16[16,512,128]{2,1,0:T(8,128)(2,1)} %bitcast.32), calls=%async_computation.1 | async-start | bytes 4194304 | tf_op jit(solution)/shard_map/all_to_all | solution.py:599
  49.0 0.2 all-gather.3.cloned.1.call-start
  49.3 0.0 copy-done
  49.3 0.7 pad_maximum_fusion
  50.0 0.0 all-gather.3.cloned.1.call-update
  50.0 8.9 %before_z.1 = (bf16[8192,128]{1,0:T(8,128)(2,1)}, bf16[128,8192]{1,0:T(8,128)(2,1)}, f32[8192,128]{1,0:T(8,128)}, f32[8192,128]{1,0:T(8,128)}, f32[8,128]{1,0:T(...) custom-call(f32[128,128]{1,0:T(8,128)} %bitcast.40, f32[128,128]{1,0:T(8,128)} %bitcast.41, ...), custom_call_target="tpu_custom_call" | custom-call | flops 4831838208 | bytes 18874368 | tf_op jit(solution)/shard_map/before_z/pallas_call | solution.py:460
  58.9 19.5 %all-gather.3.cloned.1.call-done = bf16[1088,512]{1,0:T(8,128)(2,1)} async-done(((bf16[136,512]{1,0:T(8,128)(2,1)}), bf16[1088,512]{1,0:T(8,128)(2,1)}) %all-gather.3.cloned.1.call-update) | async-done | bytes 1114128 | tf_op jit(solution)/shard_map/all_gather | solution.py:598
  78.4 0.0 all-to-all-done.1
  78.4 11.4 %states_z.1 = (bf16[8192,128]{1,0:T(8,128)(2,1)}, bf16[16,144,128]{2,1,0:T(8,128)(2,1)}) custom-call(s32[64,128]{1,0:T(8,128)} %get-tuple-element.30.place_ref, f32[8,128]{1,0:T(8,128)S(1)} %get-tuple-element.40.t_ref, f32[128,128]{1,0:T(8,128)} %get-tuple-element.41.f_ref, f32[8192,128]{1,0:T(8,128)} %get-tuple-element.42.scale_ref, ...), custom_call_target="tpu_custom_call" | custom-call | flops 2684354560 | bytes 10485760 | tf_op jit(solution)/shard_map/states_z/pallas_call | solution.py:460
  89.8 6.7 %all-to-all-start.2 = ((bf16[16,144,128]{2,1,0:T(8,128)(2,1)}), bf16[16,144,128]{2,1,0:T(8,128)(2,1)S(1)}, u32[]{:S(2)}, u32[]{:S(2)}) async-start(bf16[16,144,128]{2,1,0:T(8,128)(2,1)} %get-tuple-element.53), calls=%async_computation.2 | async-start | bytes 1179648 | tf_op jit(solution)/shard_map/all_to_all | solution.py:605
  96.5 6.8 %local_z.1.y_ref = bf16[8192,128]{1,0:T(8,128)(2,1)} custom-call(bf16[8192,128]{1,0:T(8,128)(2,1)} %get-tuple-element.48.u2_ref, bf16[8192,128]{1,0:T(8,128)(2,1)} %get-tuple-element.49.s_ref, bf16[128,8192]{1,0:T(8,128)(2,1)} %get-tuple-element.43.b_t_ref, bf16[8192,128]{1,0:T(8,128)(2,1)} %c_ref.9, f32[8192,128]{1,0:T(8,128)} %get-tuple-element.50.back_ref, ...), custom_call_target="tpu_custom_call" | custom-call | flops 3758096384 | bytes 14680064 | tf_op jit(solution)/shard_map/local_z/pallas_call | solution.py:460
  103.3 4.7 %all-to-all-done.2.got_ref = bf16[16,144,128]{2,1,0:T(8,128)(2,1)S(1)} async-done(((bf16[16,144,128]{2,1,0:T(8,128)(2,1)}), bf16[16,144,128]{2,1,0:T(8,128)(2,1)S(1)}, u32[]{:S(2)}, u32[]{:S(2)}) %all-to-all-start.2) | async-done | bytes 589856 | tf_op jit(solution)/shard_map/all_to_all | solution.py:605
  108.0 5.0 %gate_z.1 = bf16[8192,128]{1,0:T(8,128)(2,1)} custom-call(bf16[8192,128]{1,0:T(8,128)(2,1)} %local_z.1.y_ref, bf16[8192,128]{1,0:T(8,128)(2,1)} %c_ref.9, f32[8192,128]{1,0:T(8,128)} %get-tuple-element.50.back_ref, f32[128,128]{1,0:T(8,128)} %get-tuple-element.52.e_ref, bf16[16,144,128]{2,1,0:T(8,128)(2,1)S(1)} %all-to-all-done.2.got_ref), custom_call_target="tpu_custom_call" | custom-call | flops 3221225472 | bytes 12582912 | tf_op jit(solution)/shard_map/gate_z/pallas_call | solution.py:460
  113.0 31.6 %all_to_all.20.x_ref = bf16[8,1024,128]{2,1,0:T(8,128)(2,1)S(1)} all-to-all(bf16[8,1024,128]{2,1,0:T(8,128)(2,1)} %bitcast.33), channel_id=1, replica_groups=mesh['seq'=16,'head'=8] {'head'}, dimensions={0} | all-to-all | bytes 4194304 | tf_op jit(solution)/shard_map/all_to_all | solution.py:608
  144.7 4.8 %final.1 = bf16[1024,512]{1,0:T(8,128)(2,1)} custom-call(bf16[8,1024,128]{2,1,0:T(8,128)(2,1)S(1)} %all_to_all.20.x_ref, bf16[8,136,512]{2,1,0:T(8,128)(2,1)} %bitcast.39), custom_call_target="tpu_custom_call" | custom-call | flops 1342177280 | bytes 5242880 | tf_op jit(solution)/shard_map/final/pallas_call | solution.py:460
  (2 shorter events, 0.0 us)
Async XLA Ops:
  12.3 20.2 %all-to-all-start = ((bf16[16,160,128]{2,1,0:T(8,128)(2,1)}), bf16[16,160,128]{2,1,0:T(8,128)(2,1)S(1)}, u32[]{:S(2)}, u32[]{:S(2)}) async-start(bf16[16,160,128]{2,1,0:T(8,128)(2,1)} %get-tuple-element.37), calls=%async_computation | async-start | bytes 1310720 | tf_op jit(solution)/shard_map/all_to_all | solution.py:591
  32.5 12.4 %copy-start.1 = (f32[128]{0:T(128)S(1)}, f32[128]{0:T(128)}, u32[]{:S(2)}) copy-start(f32[128]{0:T(128)} %param.24) | copy-start | bytes 1540
  44.9 4.4 %copy-start = (bf16[128,512]{1,0:T(8,128)(2,1)S(1)}, bf16[128,512]{1,0:T(8,128)(2,1)}, u32[]{:S(2)}) copy-start(bf16[128,512]{1,0:T(8,128)(2,1)} %param.25) | copy-start | bytes 393220
  44.9 33.5 %all-to-all-start.1 = ((bf16[16,512,128]{2,1,0:T(8,128)(2,1)}), bf16[16,512,128]{2,1,0:T(8,128)(2,1)S(1)}, u32[]{:S(2)}, u32[]{:S(2)}) async-start(bf16[16,512,128]{2,1,0:T(8,128)(2,1)} %bitcast.32), calls=%async_computation.1 | async-start | bytes 4194304 | tf_op jit(solution)/shard_map/all_to_all | solution.py:599
  49.0 29.4 %all-gather.3.cloned.1.call-start = ((), (), s32[]{:S(2)}) async-start(), calls=%async_computation.4 | async-start | bytes 1253376 | tf_op jit(solution)/shard_map/all_gather | solution.py:598
  89.8 18.2 %all-to-all-start.2 = ((bf16[16,144,128]{2,1,0:T(8,128)(2,1)}), bf16[16,144,128]{2,1,0:T(8,128)(2,1)S(1)}, u32[]{:S(2)}, u32[]{:S(2)}) async-start(bf16[16,144,128]{2,1,0:T(8,128)(2,1)} %get-tuple-element.53), calls=%async_computation.2 | async-start | bytes 1179648 | tf_op jit(solution)/shard_map/all_to_all | solution.py:605
Sparse Core Ops, SparseCore 0:
  51.6 26.8 all-gather.2

commit v7 on v6

--- a/solution.py
+++ b/solution.py
@@ -396,13 +396,13 @@
     squares = sum(part * part for part in parts)
     mean = jnp.sum(squares, axis=1, keepdims=True) * (1.0 / 1024.0)
     scale = lax.rsqrt(mean + 1e-05)
-    total = None
+    normed = []
     for k in range(8):
-        parts3 = w_ref[k, LANES:WROWS, 0:LANES].astype(F32)
-        gain = parts3[0:1] + parts3[1:2] + parts3[2:3]
-        term = mm((parts[k] * scale * gain).astype(BF16), w_ref[k, 0:LANES, :])
-        total = term if total is None else total + term
-    out_ref[...] = total.astype(BF16)
+        pieces_of = w_ref[k, LANES:WROWS, 0:LANES].astype(F32)
+        gain = pieces_of[0:1] + pieces_of[1:2] + pieces_of[2:3]
+        normed.append((parts[k] * scale * gain).astype(BF16))
+    weight = jnp.concatenate([w_ref[k, 0:LANES, :] for k in range(8)], axis=0)
+    out_ref[...] = mm(jnp.concatenate(normed, axis=1), weight).astype(BF16)
 
 
 ROW = (STEP, LANES)

time: 157 us -> 156 us (level)
  no operation moved by 1% of the time
where the time goes in v7:
time: 156 us; the launch traced here: 155 us
  Pallas kernels  61.8 us (40%)
  blocking collectives  31.6 us (20%)
  waiting for transfers between devices  28.2 us (18%)
  starting transfers between devices  19.5 us (12%)
  between operations  13.5 us (9%)
    pallas_call x8, Pallas kernels, run(): made(*[pltpu.with_memory_space_constraint(value, pltpu.HBM) if at != loos...  61.8 us
    all_to_all x1, blocking collectives, body(): whole = lax.all_to_all(gated.reshape(8, 1024, LANES), 'head', 0, 0)  31.6 us
    all_gather x1, waiting for transfers between devices, body(): lax.all_gather(jnp.concatenate([out_weight, gain], axis=0), 'head', axis=...  19.5 us
    all_to_all x1, starting transfers between devices, body(): got_x = lax.all_to_all(message, 'seq', 0, 0)  8.43 us
    all_to_all x1, starting transfers between devices, body(): got_z = lax.all_to_all(tails_z, 'seq', 0, 0)  6.7 us
    all_to_all x1, waiting for transfers between devices, body(): got_z = lax.all_to_all(tails_z, 'seq', 0, 0)  4.7 us
    all_to_all x1, starting transfers between devices, body(): lax.all_to_all(sent.reshape(GROUPS, PIECE, LANES), 'seq', 0, 0)  4.1 us
    all_to_all x1, waiting for transfers between devices, body(): got_x = lax.all_to_all(message, 'seq', 0, 0)  3.97 us
  transfers between devices with their start and end apart: 4, of which 3 were waited for; matrix products, arithmetic and copies ran while one was open for 0% of the time, Pallas kernels for 15%

profile of v7, /device:TPU:1, one launch (start us, length us, event | category | flops | bytes accessed | tf_op | source)
XLA Modules:
  0.0 155.2 jit_solution(3867887819019245395)
XLA Ops:
  6.5 5.8 %states_x.1 = (bf16[16,160,128]{2,1,0:T(8,128)(2,1)}, s32[64,128]{1,0:T(8,128)}) custom-call(s32[64,128]{1,0:T(8,128)} %bitcast.38, f32[128,128]{1,0:T(8,128)} %bitcast.34, f32[128,128]{1,0:T(8,128)} %bitcast.36, bf16[8192,128]{1,0:T(8,128)(2,1)} %b_ref.4, bf16[8192,128]{1,0:T(8,128)(2,1)} %u_ref.3), custom_call_target="tpu_custom_call" | custom-call | flops 1073741824 | bytes 4194304 | tf_op jit(solution)/shard_map/states_x/pallas_call | solution.py:460
  12.3 8.4 %all-to-all-start = ((bf16[16,160,128]{2,1,0:T(8,128)(2,1)}), bf16[16,160,128]{2,1,0:T(8,128)(2,1)S(1)}, u32[]{:S(2)}, u32[]{:S(2)}) async-start(bf16[16,160,128]{2,1,0:T(8,128)(2,1)} %get-tuple-element.37), calls=%async_computation | async-start | bytes 1310720 | tf_op jit(solution)/shard_map/all_to_all | solution.py:591
  20.8 7.8 %local_x.1 = (bf16[8192,128]{1,0:T(8,128)(2,1)}, f32[8192,128]{1,0:T(8,128)}, f32[128,128]{1,0:T(8,128)}) custom-call(f32[128,128]{1,0:T(8,128)} %bitcast.35, f32[128,128]{1,0:T(8,128)} %bitcast.37, bf16[8192,128]{1,0:T(8,128)(2,1)} %b_ref.4, bf16[8192,128]{1,0:T(8,128)(2,1)} %c_ref.6, bf16[8192,128]{1,0:T(8,128)(2,1)} %u_ref.3), custom_call_target="tpu_custom_call" | custom-call | flops 3221225472 | bytes 12582912 | tf_op jit(solution)/shard_map/local_x/pallas_call | solution.py:460
  28.6 4.0 %all-to-all-done.got_ref = bf16[16,160,128]{2,1,0:T(8,128)(2,1)S(1)} async-done(((bf16[16,160,128]{2,1,0:T(8,128)(2,1)}), bf16[16,160,128]{2,1,0:T(8,128)(2,1)S(1)}, u32[]{:S(2)}, u32[]{:S(2)}) %all-to-all-start) | async-done | bytes 655392 | tf_op jit(solution)/shard_map/all_to_all | solution.py:591
  32.5 0.0 copy-start.1
  32.5 12.4 %send_x.1 = bf16[8192,128]{1,0:T(8,128)(2,1)} custom-call(bf16[8192,128]{1,0:T(8,128)(2,1)} %get-tuple-element.34.y_ref, bf16[8192,128]{1,0:T(8,128)(2,1)} %c_ref.6, f32[8192,128]{1,0:T(8,128)} %get-tuple-element.35.back_ref, f32[128,128]{1,0:T(8,128)} %get-tuple-element.36.e_ref, bf16[16,160,128]{2,1,0:T(8,128)(2,1)S(1)} %all-to-all-done.got_ref), custom_call_target="tpu_custom_call" | custom-call | flops 3221225472 | bytes 12582912 | tf_op jit(solution)/shard_map/send_x/pallas_call | solution.py:460
  44.9 0.0 copy-done.1
  44.9 0.0 copy-start
  44.9 4.1 %all-to-all-start.1 = ((bf16[16,512,128]{2,1,0:T(8,128)(2,1)}), bf16[16,512,128]{2,1,0:T(8,128)(2,1)S(1)}, u32[]{:S(2)}, u32[]{:S(2)}) async-start(bf16[16,512,128]{2,1,0:T(8,128)(2,1)} %bitcast.32), calls=%async_computation.1 | async-start | bytes 4194304 | tf_op jit(solution)/shard_map/all_to_all | solution.py:599
  49.0 0.2 all-gather.3.cloned.1.call-start
  49.3 0.0 copy-done
  49.3 0.7 pad_maximum_fusion
  50.0 0.0 all-gather.3.cloned.1.call-update
  50.0 8.9 %before_z.1 = (bf16[8192,128]{1,0:T(8,128)(2,1)}, bf16[128,8192]{1,0:T(8,128)(2,1)}, f32[8192,128]{1,0:T(8,128)}, f32[8192,128]{1,0:T(8,128)}, f32[8,128]{1,0:T(...) custom-call(f32[128,128]{1,0:T(8,128)} %bitcast.40, f32[128,128]{1,0:T(8,128)} %bitcast.41, ...), custom_call_target="tpu_custom_call" | custom-call | flops 4831838208 | bytes 18874368 | tf_op jit(solution)/shard_map/before_z/pallas_call | solution.py:460
  58.9 19.5 %all-gather.3.cloned.1.call-done = bf16[1088,512]{1,0:T(8,128)(2,1)} async-done(((bf16[136,512]{1,0:T(8,128)(2,1)}), bf16[1088,512]{1,0:T(8,128)(2,1)}) %all-gather.3.cloned.1.call-update) | async-done | bytes 1114128 | tf_op jit(solution)/shard_map/all_gather | solution.py:598
  78.4 0.0 all-to-all-done.1
  78.4 11.3 %states_z.1 = (bf16[8192,128]{1,0:T(8,128)(2,1)}, bf16[16,144,128]{2,1,0:T(8,128)(2,1)}) custom-call(s32[64,128]{1,0:T(8,128)} %get-tuple-element.30.place_ref, f32[8,128]{1,0:T(8,128)S(1)} %get-tuple-element.40.t_ref, f32[128,128]{1,0:T(8,128)} %get-tuple-element.41.f_ref, f32[8192,128]{1,0:T(8,128)} %get-tuple-element.42.scale_ref, ...), custom_call_target="tpu_custom_call" | custom-call | flops 2684354560 | bytes 10485760 | tf_op jit(solution)/shard_map/states_z/pallas_call | solution.py:460
  89.8 6.7 %all-to-all-start.2 = ((bf16[16,144,128]{2,1,0:T(8,128)(2,1)}), bf16[16,144,128]{2,1,0:T(8,128)(2,1)S(1)}, u32[]{:S(2)}, u32[]{:S(2)}) async-start(bf16[16,144,128]{2,1,0:T(8,128)(2,1)} %get-tuple-element.53), calls=%async_computation.2 | async-start | bytes 1179648 | tf_op jit(solution)/shard_map/all_to_all | solution.py:605
  96.5 6.8 %local_z.1.y_ref = bf16[8192,128]{1,0:T(8,128)(2,1)} custom-call(bf16[8192,128]{1,0:T(8,128)(2,1)} %get-tuple-element.48.u2_ref, bf16[8192,128]{1,0:T(8,128)(2,1)} %get-tuple-element.49.s_ref, bf16[128,8192]{1,0:T(8,128)(2,1)} %get-tuple-element.43.b_t_ref, bf16[8192,128]{1,0:T(8,128)(2,1)} %c_ref.9, f32[8192,128]{1,0:T(8,128)} %get-tuple-element.50.back_ref, ...), custom_call_target="tpu_custom_call" | custom-call | flops 3758096384 | bytes 14680064 | tf_op jit(solution)/shard_map/local_z/pallas_call | solution.py:460
  103.3 4.7 %all-to-all-done.2.got_ref = bf16[16,144,128]{2,1,0:T(8,128)(2,1)S(1)} async-done(((bf16[16,144,128]{2,1,0:T(8,128)(2,1)}), bf16[16,144,128]{2,1,0:T(8,128)(2,1)S(1)}, u32[]{:S(2)}, u32[]{:S(2)}) %all-to-all-start.2) | async-done | bytes 589856 | tf_op jit(solution)/shard_map/all_to_all | solution.py:605
  108.0 5.0 %gate_z.1 = bf16[8192,128]{1,0:T(8,128)(2,1)} custom-call(bf16[8192,128]{1,0:T(8,128)(2,1)} %local_z.1.y_ref, bf16[8192,128]{1,0:T(8,128)(2,1)} %c_ref.9, f32[8192,128]{1,0:T(8,128)} %get-tuple-element.50.back_ref, f32[128,128]{1,0:T(8,128)} %get-tuple-element.52.e_ref, bf16[16,144,128]{2,1,0:T(8,128)(2,1)S(1)} %all-to-all-done.2.got_ref), custom_call_target="tpu_custom_call" | custom-call | flops 3221225472 | bytes 12582912 | tf_op jit(solution)/shard_map/gate_z/pallas_call | solution.py:460
  113.0 31.6 %all_to_all.20.x_ref = bf16[8,1024,128]{2,1,0:T(8,128)(2,1)S(1)} all-to-all(bf16[8,1024,128]{2,1,0:T(8,128)(2,1)} %bitcast.33), channel_id=1, replica_groups=mesh['seq'=16,'head'=8] {'head'}, dimensions={0} | all-to-all | bytes 4194304 | tf_op jit(solution)/shard_map/all_to_all | solution.py:608
  144.7 3.7 %final.1 = bf16[1024,512]{1,0:T(8,128)(2,1)} custom-call(bf16[8,1024,128]{2,1,0:T(8,128)(2,1)S(1)} %all_to_all.20.x_ref, bf16[8,136,512]{2,1,0:T(8,128)(2,1)} %bitcast.39), custom_call_target="tpu_custom_call" | custom-call | flops 1342177280 | bytes 5242880 | tf_op jit(solution)/shard_map/final/pallas_call | solution.py:460
  (2 shorter events, 0.0 us)
Async XLA Ops:
  12.3 20.2 %all-to-all-start = ((bf16[16,160,128]{2,1,0:T(8,128)(2,1)}), bf16[16,160,128]{2,1,0:T(8,128)(2,1)S(1)}, u32[]{:S(2)}, u32[]{:S(2)}) async-start(bf16[16,160,128]{2,1,0:T(8,128)(2,1)} %get-tuple-element.37), calls=%async_computation | async-start | bytes 1310720 | tf_op jit(solution)/shard_map/all_to_all | solution.py:591
  32.5 12.4 %copy-start.1 = (f32[128]{0:T(128)S(1)}, f32[128]{0:T(128)}, u32[]{:S(2)}) copy-start(f32[128]{0:T(128)} %param.24) | copy-start | bytes 1540
  44.9 4.4 %copy-start = (bf16[128,512]{1,0:T(8,128)(2,1)S(1)}, bf16[128,512]{1,0:T(8,128)(2,1)}, u32[]{:S(2)}) copy-start(bf16[128,512]{1,0:T(8,128)(2,1)} %param.25) | copy-start | bytes 393220
  44.9 33.5 %all-to-all-start.1 = ((bf16[16,512,128]{2,1,0:T(8,128)(2,1)}), bf16[16,512,128]{2,1,0:T(8,128)(2,1)S(1)}, u32[]{:S(2)}, u32[]{:S(2)}) async-start(bf16[16,512,128]{2,1,0:T(8,128)(2,1)} %bitcast.32), calls=%async_computation.1 | async-start | bytes 4194304 | tf_op jit(solution)/shard_map/all_to_all | solution.py:599
  49.0 29.4 %all-gather.3.cloned.1.call-start = ((), (), s32[]{:S(2)}) async-start(), calls=%async_computation.4 | async-start | bytes 1253376 | tf_op jit(solution)/shard_map/all_gather | solution.py:598
  89.8 18.3 %all-to-all-start.2 = ((bf16[16,144,128]{2,1,0:T(8,128)(2,1)}), bf16[16,144,128]{2,1,0:T(8,128)(2,1)S(1)}, u32[]{:S(2)}, u32[]{:S(2)}) async-start(bf16[16,144,128]{2,1,0:T(8,128)(2,1)} %get-tuple-element.53), calls=%async_computation.2 | async-start | bytes 1179648 | tf_op jit(solution)/shard_map/all_to_all | solution.py:605
Sparse Core Ops, SparseCore 0:
  51.6 26.8 all-gather.2
